TPU v7x, 32 devices: a whole 2x2x4 slice. The times are simulated.
32 devices in a mesh: dp: 8 (over y, x, core), sp: 4 (over z).
Axes of the slice: x: 2, y: 2, z: 4, core: 2. Of those that a mesh axis runs over, the one named last changes fastest.
Arguments:
- hidden_in: bfloat16 [32, 1024, 768], P('dp', 'sp'), may hold values from -6 to 6
- time_embed: bfloat16 [32, 128], P('dp'), may hold values from -6 to 6
- ada_weight: bfloat16 [128, 4608], replicated, may hold values from -0.25 to 0.25
- ada_bias: bfloat16 [4608], replicated, may hold values from -1.5 to 1.5
- attn_gain: bfloat16 [768], replicated, may hold values from 0.25 to 1.75
- query_key_value_matrix: bfloat16 [768, 2304], replicated, may hold values from -0.21875 to 0.21875
- attention_output_matrix: bfloat16 [768, 768], replicated, may hold values from -1.75 to 1.75
- mlp_gain: bfloat16 [768], replicated, may hold values from 0.25 to 1.75
- up_projection_matrix: bfloat16 [768, 3072], replicated, may hold values from -0.21875 to 0.21875
- up_bias: bfloat16 [3072], replicated, may hold values from -3 to 3
- down_projection_matrix: bfloat16 [3072, 768], replicated, may hold values from -0.109375 to 0.109375
- down_bias: bfloat16 [768], replicated, may hold values from -3 to 3
- out_cotangent: bfloat16 [32, 1024, 768], P('dp', 'sp'), may hold values from -6 to 6
Outputs:
- output: bfloat16 [32, 1024, 768], P('dp', 'sp')
- hidden_grad: float32 [32, 1024, 768], P('dp', 'sp')
- time_grad: float32 [32, 128], P('dp')
- ada_weight_grad: float32 [128, 4608], P('sp')
- ada_bias_grad: float32 [4608], P('sp')
- attn_gain_grad: float32 [768], P('sp')
- qkv_weight_grad: float32 [768, 2304], P('sp')
- proj_weight_grad: float32 [768, 768], P('sp')
- mlp_gain_grad: float32 [768], P('sp')
- up_weight_grad: float32 [768, 3072], P('sp')
- up_bias_grad: float32 [3072], P('sp')
- down_weight_grad: float32 [3072, 768], P('sp')
- down_bias_grad: float32 [768], P('sp')
All inputs are finite; a program needn't handle non-finite values.
Results may differ from a plain program's by a relative error of at most 0.012.
The roundings to bfloat16 on the way count: a program that leaves them out, or rounds other values in their place, can miss the bound.
Values may be sent and summed in bfloat16 or wider, within the bound.
No kernel may reach another device: no remote copies, remote signals or barrier semaphores. Data moves between devices by JAX's collectives and lax.ppermute only.
A program may use at most 192 MiB of HBM per device.

v0:
```python
import functools

import jax
import jax.numpy as jnp
from jax import lax
from jax.experimental import pallas as pl
from jax.experimental.pallas import tpu as pltpu
from jax.sharding import PartitionSpec as P

HEAD_DIM = 64
HALF = HEAD_DIM // 2
LANES = 128
EPSILON = 1e-05
LOG2E = 1.4426950408889634
SCALE = HEAD_DIM ** (-0.5)
f32 = jnp.float32
COVER = pl.CostEstimate(flops=40_000_000_000, bytes_accessed=100_000_000, transcendentals=0)
bf16 = jnp.bfloat16


def dot_nn(a, b):
    return lax.dot_general(a, b, (((1,), (0,)), ((), ())), preferred_element_type=f32)


def dot_nt(a, b):
    return lax.dot_general(a, b, (((1,), (1,)), ((), ())), preferred_element_type=f32)


def dot_tn(a, b):
    return lax.dot_general(a, b, (((0,), (0,)), ((), ())), preferred_element_type=f32)


def column_sum(values):
    return jnp.sum(values, axis=0, keepdims=True)


def norm_forward(values):
    center = values - jnp.mean(values, axis=-1, keepdims=True)
    inverse = lax.rsqrt(jnp.mean(center * center, axis=-1, keepdims=True) + EPSILON)
    return center * inverse, inverse


def norm_backward(grad, normed, inverse):
    first = jnp.mean(grad, axis=-1, keepdims=True)
    second = jnp.mean(grad * normed, axis=-1, keepdims=True)
    return inverse * (grad - first - normed * second)


def swap_halves(values):
    lane = lax.broadcasted_iota(jnp.int32, (1, LANES), 1)
    lower = (lane & (HEAD_DIM - 1)) < HALF
    up = pltpu.roll(values, LANES - HALF, 1)
    down = pltpu.roll(values, HALF, 1)
    return lower, up, down


def rotary(values, cos, sin):
    lower, up, down = swap_halves(values)
    return values * cos + jnp.where(lower, -up, down) * sin


def unrotary(values, cos, sin):
    lower, up, down = swap_halves(values * sin)
    return values * cos + jnp.where(lower, up, -down)


def qkv_kernel(x_ref, mod_ref, w_ref, cos_ref, sin_ref, xm_ref, q_ref, k_ref, v_ref):
    width = x_ref.shape[1]
    normed, _ = norm_forward(x_ref[...].astype(f32))
    xm = (normed * mod_ref[0:1, :] + mod_ref[1:2, :]).astype(bf16)
    xm_ref[...] = xm
    cos, sin = cos_ref[...], sin_ref[...]
    for part, ref in enumerate((q_ref, k_ref, v_ref)):
        whole = dot_nn(xm, w_ref[:, part * width : (part + 1) * width]).astype(bf16)
        if part == 2:
            ref[...] = whole
            continue
        for lane in range(0, width, LANES):
            piece = whole[:, lane : lane + LANES].astype(f32)
            ref[:, lane : lane + LANES] = rotary(piece, cos, sin).astype(bf16)


def project_qkv(x, mods, weight, cos, sin, rows=256):
    length, width = x.shape
    block = pl.BlockSpec((rows, width), lambda i: (i, 0))
    table = pl.BlockSpec((rows, LANES), lambda i: (i, 0))
    shape = jax.ShapeDtypeStruct((length, width), bf16)
    return pl.pallas_call(
        qkv_kernel,
        grid=(length // rows,),
        in_specs=[
            block,
            pl.BlockSpec(mods.shape, lambda i: (0, 0)),
            pl.BlockSpec(weight.shape, lambda i: (0, 0)),
            table,
            table,
        ],
        out_specs=[block] * 4,
        out_shape=[shape] * 4,
        cost_estimate=COVER,
        name="project_qkv",
    )(x, mods, weight, cos, sin)


def attention_forward_kernel(q_ref, k_ref, v_ref, o_ref, lse_ref):
    q, k, v = q_ref[...], k_ref[...], v_ref[...]
    first = lax.broadcasted_iota(jnp.int32, (1, LANES), 1) < HEAD_DIM
    c = LOG2E * SCALE
    outs = []
    for h in range(2):
        mine = first if h == 0 else ~first
        kh = jnp.where(mine, k, jnp.zeros_like(k))
        st = dot_nt(kh, q)
        top = jnp.max(st, axis=0, keepdims=True) * c
        p = jnp.exp2(st * c - top).astype(bf16)
        ot = dot_tn(jnp.where(mine, v, jnp.ones_like(v)), p)
        own, ones = (ot[:HEAD_DIM], ot[HEAD_DIM:]) if h == 0 else (ot[HEAD_DIM:], ot[:HEAD_DIM])
        total = ones[0:1]
        outs.append(own * (1.0 / total))
        lse_ref[0, h : h + 1, :] = top + jnp.log2(total)
    o_ref[...] = jnp.concatenate(outs, axis=0).T.astype(bf16)


def attention_forward(q, k, v):
    length, width = q.shape
    pairs = width // LANES
    block = pl.BlockSpec((length, LANES), lambda i: (0, i))
    return pl.pallas_call(
        attention_forward_kernel,
        grid=(pairs,),
        in_specs=[block] * 3,
        out_specs=[block, pl.BlockSpec((1, 2, length), lambda i: (i, 0, 0))],
        out_shape=[
            jax.ShapeDtypeStruct((length, width), bf16),
            jax.ShapeDtypeStruct((pairs, 2, length), f32),
        ],
        cost_estimate=COVER,
        name="attention_forward",
    )(q, k, v)


def attention_backward_kernel(
    q_ref, k_ref, v_ref, do_ref, o_ref, lse_ref, cos_ref, sin_ref, *rest
):
    g_ref = rest[-1]
    first = lax.broadcasted_iota(jnp.int32, (1, LANES), 1) < HEAD_DIM
    upper = lax.broadcasted_iota(jnp.int32, (LANES, 1), 0) < HEAD_DIM
    c = LOG2E * SCALE
    q, k, v, do = q_ref[...], k_ref[...], v_ref[...], do_ref[...]
    prod = (do.astype(f32) * o_ref[...].astype(f32)).T
    kt = k.T
    zero = jnp.zeros_like(k)
    dq = dk = dv = None
    for h in range(2):
        mine = first if h == 0 else ~first
        row = column_sum(prod[h * HEAD_DIM : (h + 1) * HEAD_DIM])
        st = dot_nt(jnp.where(mine, k, zero), q)
        p = jnp.exp2(st * c - lse_ref[0, h : h + 1, :])
        dp = dot_nt(jnp.where(mine, v, zero), do)
        ds = (p * (dp - row)).astype(bf16)
        dvh = dot_nn(p.astype(bf16), jnp.where(mine, do, zero))
        dkh = dot_nn(ds, jnp.where(mine, q, zero))
        dqh = dot_nn(jnp.where(upper if h == 0 else ~upper, kt, jnp.zeros_like(kt)), ds)
        dq, dk, dv = (dqh, dkh, dvh) if h == 0 else (dq + dqh, dk + dkh, dv + dvh)
    cos, sin = cos_ref[...], sin_ref[...]
    g_ref[0] = unrotary(dq.T * SCALE, cos, sin).astype(bf16)
    g_ref[1] = unrotary(dk * SCALE, cos, sin).astype(bf16)
    g_ref[2] = dv.astype(bf16)


def attention_backward(q, k, v, do, o, lse, cos, sin, start, count, into=None):
    length, width = q.shape
    block = pl.BlockSpec((length, LANES), lambda i: (0, start + i))
    table = pl.BlockSpec((length, LANES), lambda i: (0, 0))
    extra = [] if into is None else [into]
    return pl.pallas_call(
        attention_backward_kernel,
        grid=(count,),
        in_specs=[block] * 5
        + [pl.BlockSpec((1, 2, length), lambda i: (start + i, 0, 0)), table, table]
        + [pl.BlockSpec(memory_space=pl.ANY)] * len(extra),
        out_specs=pl.BlockSpec((3, length, LANES), lambda i: (0, 0, start + i)),
        out_shape=jax.ShapeDtypeStruct((3, length, width), bf16),
        input_output_aliases={8: 0} if extra else {},
        cost_estimate=COVER,
        name="attention_backward",
    )(q, k, v, do, o, lse, cos, sin, *extra)


def mlp_kernel(
    x_ref, mixed_ref, cot_ref, mod_ref, bias_ref, wo_ref, wu_ref, wd_ref,
    xm_ref, act_ref, gd_ref, gp_ref, gm_ref, gmix_ref, sum_ref, up_sum_ref, out_ref,
):
    chunk, ff = wu_ref.shape
    gate_attn, scaled, shift = mod_ref[0:1, :], mod_ref[1:2, :], mod_ref[2:3, :]
    gate_mlp, down_bias = mod_ref[3:4, :], mod_ref[4:5, :]
    cot = cot_ref[...].astype(f32)
    projected = dot_nn(mixed_ref[...], wo_ref[...])
    middle = x_ref[...].astype(f32) + gate_attn * projected
    normed, inverse = norm_forward(middle)
    xm = (normed * scaled + shift).astype(bf16)
    xm_ref[0] = xm
    xm_ref[1] = mixed_ref[...]
    gd = (gate_mlp * cot).astype(bf16)
    gd_ref[...] = gd
    down = grad_mod = None
    c0 = 0.7978845608028654
    c1 = c0 * 0.044715
    up_sums = []
    for at in range(0, ff, chunk):
        cols = slice(at, at + chunk)
        pre = dot_nn(xm, wu_ref[:, cols]) + bias_ref[:, cols]
        square = pre * pre
        t = jnp.tanh(pre * (c0 + c1 * square))
        half = 0.5 + 0.5 * t
        act = (pre * half).astype(bf16)
        act_ref[:, cols] = act
        slope = half + (0.5 * pre) * (1.0 - t * t) * (c0 + (3.0 * c1) * square)
        gp = (slope * dot_nt(gd, wd_ref[cols, :])).astype(bf16)
        gp_ref[at // chunk] = gp
        up_sums.append(column_sum(gp.astype(f32)))
        d = dot_nn(act, wd_ref[cols, :])
        g = dot_nt(gp, wu_ref[:, cols])
        down, grad_mod = (d, g) if down is None else (down + d, grad_mod + g)
    down = down + down_bias
    out_ref[...] = (middle + gate_mlp * down).astype(bf16)
    gm = cot + norm_backward(grad_mod * scaled, normed, inverse)
    gm_ref[...] = gm
    gpj = (gate_attn * gm).astype(bf16)
    gp_ref[ff // chunk] = gpj
    gmix_ref[...] = dot_nt(gpj, wo_ref[...]).astype(bf16)
    sums = jnp.concatenate(
        [
            column_sum(cot * down),
            column_sum(gd.astype(f32)),
            column_sum(grad_mod),
            column_sum(grad_mod * normed),
            column_sum(gm * projected),
            jnp.zeros((3, cot.shape[1]), f32),
        ],
        axis=0,
    )
    up_sum = jnp.concatenate(up_sums, axis=1)

    @pl.when(pl.program_id(0) == 0)
    def _():
        sum_ref[...] = sums
        up_sum_ref[...] = up_sum

    @pl.when(pl.program_id(0) > 0)
    def _():
        sum_ref[...] += sums
        up_sum_ref[...] += up_sum


def feed_forward(x, mixed, cot, mods, up_bias, wo, wu, wd, rows):
    length, width = x.shape
    ff = wu.shape[1]
    block = pl.BlockSpec((rows, width), lambda i: (i, 0))
    wide = pl.BlockSpec((rows, ff), lambda i: (i, 0))

    def whole(a):
        return pl.BlockSpec(a.shape, lambda i: (0, 0), pipeline_mode=pl.Buffered(1))

    narrow = jax.ShapeDtypeStruct((length, width), bf16)
    broad = jax.ShapeDtypeStruct((length, ff), bf16)
    return pl.pallas_call(
        mlp_kernel,
        grid=(length // rows,),
        in_specs=[block, block, block] + [whole(a) for a in (mods, up_bias, wo, wu, wd)],
        out_specs=[
            pl.BlockSpec((2, rows, width), lambda i: (0, i, 0)),
            wide,
            block,
            pl.BlockSpec((ff // width + 1, rows, width), lambda i: (0, i, 0)),
            block,
            block,
            pl.BlockSpec((8, width), lambda i: (0, 0)),
            pl.BlockSpec((1, ff), lambda i: (0, 0)),
        ]
        + [block],
        out_shape=[
            jax.ShapeDtypeStruct((2, length, width), bf16), broad, narrow,
            jax.ShapeDtypeStruct((ff // width + 1, length, width), bf16),
            jax.ShapeDtypeStruct((length, width), f32), narrow,
            jax.ShapeDtypeStruct((8, width), f32), jax.ShapeDtypeStruct((1, ff), f32),
        ]
        + [narrow],
        cost_estimate=COVER,
        name="feed_forward",
    )(x, mixed, cot, mods, up_bias, wo, wu, wd)


def late_grads_kernel(
    core_ref, x_ref, tile_ref, gm_ref, mod_ref, w_ref, xm_ref, block_ref,
    sum_ref, hg_ref, send_ref, keep_ref, turned_ref, *, tiles,
):
    step = pl.program_id(0)
    width = x_ref.shape[1]

    @pl.when(step < tiles)
    def _():
        normed, inverse = norm_forward(x_ref[...].astype(f32))
        grad = None
        for part in range(3):
            g = dot_nt(tile_ref[part], w_ref[:, part * width : (part + 1) * width])
            grad = g if grad is None else grad + g
        hg = gm_ref[...] + norm_backward(grad * mod_ref[0:1, :], normed, inverse)
        hg_ref[...] = hg.astype(bf16)
        sums = jnp.concatenate(
            [column_sum(grad), column_sum(grad * normed), jnp.zeros((6, width), f32)], axis=0
        )

        @pl.when(step == 0)
        def _():
            sum_ref[...] = sums

        @pl.when(step > 0)
        def _():
            sum_ref[...] += sums

    @pl.when(step == tiles)
    def _():
        turned_ref[...] = xm_ref[...].T

    @pl.when(step >= tiles)
    def _():
        product = dot_nn(turned_ref[...], block_ref[0])
        half = send_ref.shape[1]
        for i, (send, keep) in enumerate(split_halves(product, half, core_ref[0] == 0)):
            send_ref[i] = send
            keep_ref[i] = keep


def late_grads(core, x, grads, gm, mods, weight, xm, sp, rows):
    length, width = x.shape
    tiles = length // rows
    n = grads.shape[0]
    half = width // sp // 2

    def tile(i, c):
        return (jnp.minimum(i, tiles - 1), 0)

    def part(i):
        return jnp.maximum(i - tiles, 0)

    block = pl.BlockSpec((rows, width), tile)

    def whole(a):
        return pl.BlockSpec(a.shape, lambda i, c: (0, 0), pipeline_mode=pl.Buffered(1))

    out = pl.BlockSpec((sp, half, width), lambda i, c: (0, part(i), 0))
    shape = jax.ShapeDtypeStruct((sp, n * half, width), bf16)
    return pl.pallas_call(
        functools.partial(late_grads_kernel, tiles=tiles),
        grid_spec=pltpu.PrefetchScalarGridSpec(
            num_scalar_prefetch=1,
            grid=(tiles + n,),
            in_specs=[
                block,
                pl.BlockSpec((n, rows, width), lambda i, c: (0, jnp.minimum(i, tiles - 1), 0)),
                block,
                whole(mods),
                whole(weight),
                whole(xm),
                pl.BlockSpec((1, length, width), lambda i, c: (part(i), 0, 0)),
            ],
            out_specs=[pl.BlockSpec((8, width), lambda i, c: (0, 0)), block, out, out],
            scratch_shapes=[pltpu.VMEM((width, length), bf16)],
        ),
        out_shape=[
            jax.ShapeDtypeStruct((8, width), f32),
            jax.ShapeDtypeStruct((length, width), bf16),
            shape,
            shape,
        ],
        cost_estimate=COVER,
        name="late_grads",
    )(core, x, grads, gm, mods, weight, xm, grads)


def split_halves(product, half, this_core):
    pieces = []
    for at in range(0, product.shape[0], 2 * half):
        low = product[at : at + half].astype(bf16)
        high = product[at + half : at + 2 * half].astype(bf16)
        pieces.append((jnp.where(this_core, high, low), jnp.where(this_core, low, high)))
    return pieces


def row_grad_kernel(core_ref, a_ref, b_ref, send_ref, keep_ref, *, half):
    product = dot_tn(a_ref[...], b_ref[...])
    for i, (send, keep) in enumerate(split_halves(product, half, core_ref[0] == 0)):
        send_ref[0, i * half : (i + 1) * half] = send
        keep_ref[0, i * half : (i + 1) * half] = keep


def row_grad(core, a, b, sp):
    length, width = b.shape
    out = jax.ShapeDtypeStruct((sp, width // 2, width), bf16)
    block = pl.BlockSpec((1, width // 2, width), lambda j, c: (j, 0, 0))
    return pl.pallas_call(
        functools.partial(row_grad_kernel, half=width // sp // 2),
        grid_spec=pltpu.PrefetchScalarGridSpec(
            num_scalar_prefetch=1,
            grid=(sp,),
            in_specs=[
                pl.BlockSpec((length, width), lambda j, c: (0, j)),
                pl.BlockSpec((length, width), lambda j, c: (0, 0)),
            ],
            out_specs=[block, block],
        ),
        out_shape=[out, out],
        cost_estimate=COVER,
        name="row_grad",
    )(core, a, b)


def column_grad_kernel(core_ref, a_ref, b_ref, send_ref, keep_ref, turned_ref):
    @pl.when((pl.program_id(0) == 0) | (pl.program_id(0) == core_ref[1]))
    def _():
        turned_ref[...] = a_ref[0].T

    product = dot_nn(turned_ref[...], b_ref[0])
    for i, (send, keep) in enumerate(split_halves(product, send_ref.shape[1], core_ref[0] == 0)):
        send_ref[i] = send
        keep_ref[i] = keep


def column_grad(core, a, b, sp, blocks, second):
    _, length, width = a.shape
    n = b.shape[0]
    half = width // sp // 2
    out = jax.ShapeDtypeStruct((sp, blocks * half, width), bf16)
    block = pl.BlockSpec((sp, half, width), lambda j, c: (0, j, 0))
    return pl.pallas_call(
        column_grad_kernel,
        grid_spec=pltpu.PrefetchScalarGridSpec(
            num_scalar_prefetch=1,
            grid=(n,),
            in_specs=[
                pl.BlockSpec((1, length, width), lambda j, c: (j // second, 0, 0)),
                pl.BlockSpec((1, length, width), lambda j, c: (j, 0, 0)),
            ],
            out_specs=[block, block],
            scratch_shapes=[pltpu.VMEM((width, length), bf16)],
        ),
        out_shape=[out, out],
        cost_estimate=COVER,
        name="column_grad",
    )(jnp.concatenate([core, jnp.full((1,), second, jnp.int32)]), a, b)


def vector_grad_kernel(core_ref, timing_ref, parts_ref, sums_ref, _, __, send_ref, keep_ref):
    sp, half, width = send_ref.shape
    parts = parts_ref.shape[0] // 2
    count = timing_ref.shape[0] // sp
    filled = parts * count
    rest = half - filled - sums_ref.shape[2]
    for ref, side in ((send_ref, 1 - core_ref[0]), (keep_ref, core_ref[0])):
        for s in range(sp):
            for p in range(parts):
                part = jnp.where(side == 0, parts_ref[p : p + 1, :], parts_ref[parts + p : parts + p + 1, :])
                column = timing_ref[s * count : (s + 1) * count, :]
                ref[s, p * count : (p + 1) * count] = (column * part).astype(bf16)
            ref[s, filled : filled + sums_ref.shape[2]] = jnp.where(
                side == 0, sums_ref[0, s], sums_ref[1, s]
            ).astype(bf16)
            if rest:
                ref[s, half - rest : half] = jnp.zeros((rest, width), bf16)


def vector_grad(core, timing, parts, sums, send, keep, rows):
    sp, total, width = send.shape
    block = pl.BlockSpec((sp, rows, width), lambda i, c: (0, total // rows - 1, 0))
    return pl.pallas_call(
        vector_grad_kernel,
        grid_spec=pltpu.PrefetchScalarGridSpec(
            num_scalar_prefetch=1,
            grid=(1,),
            in_specs=[
                pl.BlockSpec(timing.shape, lambda i, c: (0, 0)),
                pl.BlockSpec(parts.shape, lambda i, c: (0, 0)),
                pl.BlockSpec(sums.shape, lambda i, c: (0, 0, 0, 0)),
                pl.BlockSpec(memory_space=pl.ANY),
                pl.BlockSpec(memory_space=pl.ANY),
            ],
            out_specs=[block, block],
        ),
        out_shape=[jax.ShapeDtypeStruct(send.shape, bf16)] * 2,
        input_output_aliases={4: 0, 5: 1},
        cost_estimate=COVER,
        name="vector_grad",
    )(core, timing, parts, sums, send, keep)


def shift_permute(value, axis, by):
    n = lax.axis_size(axis)
    return lax.ppermute(value, axis, [(i, (i + by) % n) for i in range(n)])


def pair_permute(value, bit, axis="dp"):
    n = lax.axis_size(axis)
    return lax.ppermute(value, axis, [(i, i ^ bit) for i in range(n)])


def pick(values, index, axis=0):
    return lax.dynamic_index_in_dim(values, index, axis, keepdims=False)


def after(values, *others):
    return lax.optimization_barrier((values, others))[0]


VMEM = pl.BlockSpec(memory_space=pltpu.VMEM)
SMEM = pl.BlockSpec(memory_space=pltpu.SMEM)


def bit_of(index, bit):
    return (index // bit) % 2


def add(a, b):
    return (a.astype(f32) + b.astype(f32)).astype(bf16)


CORE, FIRST, SECOND = 1, 2, 4


def first_halves_kernel(at_ref, row_keep, row_got, col_keep, col_got, *outs):
    columns = outs[0].shape[2]
    start = 0
    for keep, got in ((row_keep, row_got), (col_keep, col_got)):
        total = add(keep[0], got[0])
        n = total.shape[0] // 2
        low, high = total[:n], total[n:]
        for side in range(2):
            cols = slice(side * columns, (side + 1) * columns)
            mine = at_ref[side] == 0
            outs[2 * side][0, start : start + n] = jnp.where(mine, high, low)[:, cols]
            outs[2 * side + 1][0, start : start + n] = jnp.where(mine, low, high)[:, cols]
        start += n


def first_halves(at, row_keep, row_got, col_keep, col_got):
    sp, rows, width = row_keep.shape
    cols = col_keep.shape[1]

    def spec(a):
        return pl.BlockSpec((1,) + a.shape[1:], lambda s, t: (s, 0, 0))

    out = jax.ShapeDtypeStruct((sp, (rows + cols) // 2, width // 2), bf16)
    return pl.pallas_call(
        first_halves_kernel,
        grid_spec=pltpu.PrefetchScalarGridSpec(
            num_scalar_prefetch=1,
            grid=(sp,),
            in_specs=[spec(a) for a in (row_keep, row_got, col_keep, col_got)],
            out_specs=[spec(out)] * 4,
        ),
        out_shape=[out] * 4,
        cost_estimate=COVER,
        name="first_halves",
    )(at, row_keep, row_got, col_keep, col_got)


def second_halves_kernel(at_ref, *refs):
    for side in range(2):
        mine = at_ref[1 - side]
        keep, got = refs[2 * side : 2 * side + 2]
        for s in range(keep.shape[0]):
            refs[4 + 2 * side][s] = add(keep[s, 1 - mine], got[s, 1 - mine])
            refs[5 + 2 * side][s] = add(keep[s, mine], got[s, mine])


def second_halves(at, *arrays):
    sp, rows, columns = arrays[0].shape
    out = jax.ShapeDtypeStruct((sp, rows // 2, columns), bf16)
    return pl.pallas_call(
        second_halves_kernel,
        in_specs=[SMEM] + [VMEM] * 4,
        out_specs=[VMEM] * 4,
        out_shape=[out] * 4,
        cost_estimate=COVER,
        name="second_halves",
    )(at, *[a.reshape(sp, 2, rows // 2, columns) for a in arrays])


def near_halves_kernel(at_ref, *refs, terms, sides):
    ins, outs = refs[:-2], refs[-2:]
    mine = lax.rem(at_ref[2], 2)
    for out, bit in zip(outs, (1 - mine, mine)):
        for s in range(out.shape[0]):
            at = 0
            for side in range(sides):
                total = None
                for ref in ins[side * terms : (side + 1) * terms]:
                    value = ref[2 * s + bit].astype(f32)
                    total = value if total is None else total + value
                out[s, :, at : at + total.shape[1]] = total.astype(bf16)
                at += total.shape[1]


def near_halves(at, sides):
    terms = len(sides[0])
    flat = [a for side in sides for a in side]
    sp, rows, _ = flat[0].shape
    width = sum(side[0].shape[2] for side in sides)
    out = jax.ShapeDtypeStruct((sp // 2, rows, width), bf16)
    return pl.pallas_call(
        functools.partial(near_halves_kernel, terms=terms, sides=len(sides)),
        in_specs=[SMEM] + [VMEM] * len(flat),
        out_specs=[VMEM] * 2,
        out_shape=[out] * 2,
        cost_estimate=COVER,
        name="near_halves",
    )(at, *flat)


def far_halves_kernel(at_ref, keep, got, send_ref, keep_ref):
    mine = lax.div(at_ref[2], 2)
    send_ref[...] = add(keep[1 - mine], got[1 - mine])
    keep_ref[...] = add(keep[mine], got[mine])


def far_halves(at, keep, got):
    out = jax.ShapeDtypeStruct(keep.shape[1:], bf16)
    return pl.pallas_call(
        far_halves_kernel,
        in_specs=[SMEM] + [VMEM] * 2,
        out_specs=[VMEM] * 2,
        out_shape=[out] * 2,
        cost_estimate=COVER,
        name="far_halves",
    )(at, keep, got)


def hand_over_kernel(in_ref, out_ref):
    out_ref[...] = in_ref[...].astype(out_ref.dtype)


def widen(value):
    return hand_over(value, f32)


def hand_over(value, dtype=bf16):
    block = pl.BlockSpec((1,) + value.shape[1:], lambda i: (i, 0, 0))
    return pl.pallas_call(
        hand_over_kernel,
        grid=(value.shape[0],),
        in_specs=[block],
        out_specs=block,
        out_shape=jax.ShapeDtypeStruct(value.shape, dtype),
        cost_estimate=COVER,
        name="hand_over",
    )(value)


def own_kernel(keep_ref, got_ref, out_ref):
    out_ref[...] = add(keep_ref[...], got_ref[...])


def own_sum(keep, got):
    return pl.pallas_call(
        own_kernel,
        in_specs=[VMEM] * 2,
        out_specs=VMEM,
        out_shape=jax.ShapeDtypeStruct(keep.shape, bf16),
        cost_estimate=COVER,
        name="own_sum",
    )(keep, got)


def quarters_kernel(at_ref, keep_ref, got_ref, *outs):
    for i, out in enumerate(outs):
        index = 2 * (at_ref[0] ^ (i // 2)) + (at_ref[1] ^ (i % 2))
        for s in range(keep_ref.shape[0]):
            out[s] = add(keep_ref[s, index], got_ref[s, index])


def quarters(at, keep, got):
    sp, rows, width = keep.shape
    out = jax.ShapeDtypeStruct((sp, rows // 4, width), bf16)
    return pl.pallas_call(
        quarters_kernel,
        in_specs=[SMEM] + [VMEM] * 2,
        out_specs=[VMEM] * 4,
        out_shape=[out] * 4,
        cost_estimate=COVER,
        name="quarters",
    )(at, keep.reshape(sp, 4, rows // 4, width), got.reshape(sp, 4, rows // 4, width))


def four_chips_kernel(at_ref, *refs, crossed):
    pieces, out_ref = refs[:4], refs[4]
    columns = out_ref.shape[2] // 2
    for i, piece in enumerate(pieces):
        x, y = at_ref[0] ^ (i // 2), at_ref[1] ^ (i % 2)
        out_ref[2 * x + y, :, :columns] = piece[:, :columns]
        out_ref[2 * y + x if crossed else 2 * x + y, :, columns:] = piece[:, columns:]


def four_chips(at, pieces, crossed):
    rows, width = pieces[0].shape
    return pl.pallas_call(
        functools.partial(four_chips_kernel, crossed=crossed),
        in_specs=[SMEM] + [VMEM] * 4,
        out_specs=VMEM,
        out_shape=jax.ShapeDtypeStruct((4, rows, width), bf16),
        cost_estimate=COVER,
        name="four_chips",
    )(at, *pieces).reshape(4 * rows, width)


def spread(own):
    return [own] + [pair_permute(own, bit) for bit in (SECOND, FIRST, FIRST + SECOND)]


def finish_kernel(core_ref, mine_ref, other_ref, *outs, half, layout):
    first = core_ref[0] == 0
    width = mine_ref.shape[1]
    for out, (_, across, starts) in zip(outs, layout):
        for n, at in enumerate(starts):
            cols = slice(n % across * width, (n % across + 1) * width)
            mine = mine_ref[at : at + half].astype(f32)
            other = other_ref[at : at + half].astype(f32)
            to = n // across * 2 * half
            out[to : to + half, cols] = jnp.where(first, mine, other)
            out[to + half : to + 2 * half, cols] = jnp.where(first, other, mine)


def finish(core, mine, other, half, layout):
    width = mine.shape[1]
    shapes = [(2 * half * down, width * across) for down, across, _ in layout]
    return pl.pallas_call(
        functools.partial(finish_kernel, half=half, layout=layout),
        grid=(1,),
        in_specs=[SMEM] + [VMEM] * 2,
        out_specs=[pl.BlockSpec(s, lambda i: (0, 0)) for s in shapes],
        out_shape=[jax.ShapeDtypeStruct(s, f32) for s in shapes],
        cost_estimate=COVER,
        name="finish",
    )(core, mine, other)


def late_row_kernel(sums_ref, parts_ref, mod_ref, ada_ref, timing_ref, row_ref):
    width = sums_ref.shape[1]
    cond = timing_ref.shape[1]
    shift, scaled = sums_ref[0:1, :], sums_ref[1:2, :]
    scale = scaled * mod_ref[0:1, :]
    row = jnp.concatenate([shift, scale] + [parts_ref[i : i + 1, :] for i in range(4)], axis=1)
    high = row.astype(bf16)
    low = (row - high.astype(f32)).astype(bf16)
    time = dot_nt(high, ada_ref[...]) + dot_nt(low, ada_ref[...])
    row_ref[:, :width] = shift.astype(bf16)
    row_ref[:, width : 2 * width] = scale.astype(bf16)
    row_ref[:, 2 * width : 3 * width] = (scaled * mod_ref[1:2, :]).astype(bf16)
    row_ref[:, 3 * width : 3 * width + cond] = time.astype(bf16)
    row_ref[:, 3 * width + cond :] = timing_ref[...]


def late_row(sums, parts, mods, ada, timing):
    columns = 3 * sums.shape[1] + 2 * timing.shape[1]
    return pl.pallas_call(
        late_row_kernel,
        in_specs=[VMEM] * 5,
        out_specs=VMEM,
        out_shape=jax.ShapeDtypeStruct((1, columns), bf16),
        cost_estimate=COVER,
        name="late_row",
    )(sums, parts, mods, ada, timing)


def vector_outputs_kernel(
    at_ref, rows_ref, vector_ref, ada_ref, bias_ref, attn_gain_ref, mlp_gain_ref, up_ref, down_ref,
    grad_ref, *, half, sp,
):
    count, width = ada_ref.shape[0], vector_ref.shape[1]
    quarter = width // sp
    me = at_ref[2]
    grad_ref[...] = dot_tn(
        rows_ref[:, 3 * width + grad_ref.shape[0] :], rows_ref[:, : 2 * width]
    ).reshape(grad_ref.shape)
    ada_ref[:, : 2 * width] = grad_ref[pl.ds(pl.multiple_of(me * count, count), count), :]
    for p in range(4):
        start = p // 2 * half + p % 2 * count
        ada_ref[:, (2 + p) * width : (3 + p) * width] = vector_ref[start : start + count, :]
    totals = column_sum(rows_ref[:, : 3 * width].astype(f32))
    row = 2 * count
    own = bias_ref.shape[1]
    late_bias = jnp.concatenate([totals[:, : 2 * width], jnp.zeros((1, 4 * width), f32)], axis=1)
    bias, gain = late_bias[:, :own], totals[:, 2 * width : 2 * width + quarter]
    for s in range(1, sp):
        bias = jnp.where(me == s, late_bias[:, s * own : (s + 1) * own], bias)
        at = 2 * width + s * quarter
        gain = jnp.where(me == s, totals[:, at : at + quarter], gain)
    bias_ref[:, :width] = bias[:, :width] + vector_ref[row + 1 : row + 2, :]
    bias_ref[:, width:] = bias[:, width:] + vector_ref[half + row + 1 : half + row + 2, : own - width]
    attn_gain_ref[...] = gain
    up_ref[...] = vector_ref[row : row + 1, :]
    mlp_gain_ref[...] = vector_ref[half + row : half + row + 1, :quarter]
    down_ref[...] = vector_ref[half + row : half + row + 1, quarter : 2 * quarter]


def vector_outputs(at, rows, vectors, half, cond, sp):
    width = vectors.shape[1]
    quarter = width // sp
    shapes = [(cond // sp, 6 * width), (1, 6 * width // sp), (1, quarter), (1, quarter), (1, width), (1, quarter)]
    return pl.pallas_call(
        functools.partial(vector_outputs_kernel, half=half, sp=sp),
        in_specs=[SMEM] + [VMEM] * 2,
        out_specs=[VMEM] * 6,
        out_shape=[jax.ShapeDtypeStruct(s, f32) for s in shapes],
        scratch_shapes=[pltpu.VMEM((cond, 2 * width), f32)],
        cost_estimate=COVER,
        name="vector_outputs",
    )(at, rows, vectors)


def sum_over_rest(total):
    bit = 2 * SECOND
    while bit < lax.axis_size("dp"):
        total = add(total, pair_permute(total, bit))
        bit *= 2
    return total


def double(rows, bit, axis):
    return jnp.concatenate([rows, pair_permute(rows, bit, axis)], axis=0)


def bits(axis):
    n, bit = lax.axis_size(axis), 1
    while bit < n:
        yield bit
        bit *= 2


def body(
    hidden_in,
    time_embed,
    ada_weight,
    ada_bias,
    attn_gain,
    query_key_value_matrix,
    attention_output_matrix,
    mlp_gain,
    up_projection_matrix,
    up_bias,
    down_projection_matrix,
    down_bias,
    out_cotangent,
):
    sequences, local_len, width = hidden_in.shape
    sp, me = lax.axis_size("sp"), lax.axis_index("sp")
    assert sequences == sp
    def exchange(values):
        values = values.reshape(sp, local_len, width)
        return lax.all_to_all(values, "sp", split_axis=0, concat_axis=0, tiled=True)

    x = exchange(hidden_in).reshape(-1, width)
    cot = exchange(after(out_cotangent, x)).reshape(-1, width)
    here = lax.axis_index("dp")
    core = bit_of(here, CORE).reshape(1)
    at = jnp.stack([bit_of(here, FIRST), bit_of(here, SECOND), me])

    timing = lax.dynamic_slice_in_dim(time_embed, me, 1, 0)
    modulation = dot_nn(timing, ada_weight) + ada_bias.astype(f32)[None]
    shift_attn, scale_attn, gate_attn, shift_mlp, scale_mlp, gate_mlp = jnp.split(
        modulation, 6, axis=-1
    )
    gain_attn = attn_gain.astype(f32)[None]
    gain_mlp = mlp_gain.astype(f32)[None]
    zero = jnp.zeros_like(shift_attn)
    attn_mods = jnp.concatenate(
        [gain_attn * (1.0 + scale_attn), shift_attn] + [zero] * 6, axis=0
    )
    mlp_mods = jnp.concatenate(
        [gate_attn, gain_mlp * (1.0 + scale_mlp), shift_mlp, gate_mlp, down_bias.astype(f32)[None]]
        + [zero] * 3,
        axis=0,
    )
    lane = lax.broadcasted_iota(jnp.int32, (1, LANES), 1)
    frequency = 10000.0 ** (-((lane % HALF).astype(f32) * 2.0 / HEAD_DIM))
    row = lax.broadcasted_iota(jnp.int32, (sp * local_len, 1), 0)
    angles = row.astype(f32) * frequency
    cos, sin = jnp.cos(angles), jnp.sin(angles)

    xm_attn, q, k, v = project_qkv(x, attn_mods, query_key_value_matrix, cos, sin)
    mixed, lse = attention_forward(q, k, v)
    both_in, act, gd, both_grad, gm, gmix, sums, up_sum, out = feed_forward(
        x,
        mixed,
        cot,
        mlp_mods,
        up_bias.astype(f32)[None],
        attention_output_matrix,
        up_projection_matrix,
        down_projection_matrix,
        local_len,
    )
    ff = up_bias.shape[0]
    assert ff == sp * width
    n_up = ff // width
    half = width // sp // 2
    quarter = width // sp
    cond = timing.shape[1]
    column = timing.astype(f32).reshape(cond, 1)

    def shards(row):
        return row.reshape(sp, -1)

    def sum_rows(rows):
        filled = [
            jnp.stack([jnp.pad(r, ((0, 0), (0, width - r.shape[1]))) for r in side], axis=1)
            for side in rows
        ]
        return jnp.stack([jnp.pad(f, ((0, 0), (0, 16 - f.shape[1]), (0, 0))) for f in filled])

    output = exchange(out)
    col_send, col_keep = column_grad(core, both_in, both_grad, sp, n_up + 2, n_up)
    early_parts = jnp.concatenate([sums[4:5], sums[2:3], sums[3:4] * gain_mlp, sums[0:1]], axis=0)
    six = 6 * width
    early_bias = jnp.concatenate([jnp.zeros((2 * width,), f32), early_parts.reshape(-1)])
    early_bias = shards(early_bias)
    early_sums = sum_rows(
        [
            [shards(up_sum), early_bias[:, :width]],
            [
                jnp.concatenate(
                    [shards(sums[3:4] * (1.0 + scale_mlp)), shards(sums[1:2])], axis=1
                ),
                early_bias[:, width:],
            ],
        ]
    )
    col_send, col_keep = vector_grad(core, column, early_parts, early_sums, col_send, col_keep, half)
    col_got = pair_permute(col_send, CORE)
    row_send, row_keep = row_grad(core, *after((act, gd), col_keep), sp)
    row_got = pair_permute(row_send, CORE)

    pairs = width // LANES

    def backward(start, stop, into=None):
        return attention_backward(
            q, k, v, gmix, mixed, lse, cos, sin, start, stop - start, into
        )

    left_send, left, right_send, right = first_halves(at, row_keep, row_got, col_keep, col_got)
    left_got, right_got = pair_permute(left_send, FIRST), pair_permute(right_send, SECOND)
    gmix = after(gmix, left, right)
    grads = backward(0, pairs)
    left_got, right_got, output = after((left_got, right_got, output), grads)
    left_send, left, right_send, right = second_halves(at, left, left_got, right, right_got)
    left_got, right_got = pair_permute(left_send, SECOND), pair_permute(right_send, FIRST)
    grads = after(grads, left, right, output)

    attn_sums, hg, late_send, late_keep = late_grads(
        core, x, grads, gm, attn_mods, query_key_value_matrix, xm_attn, sp, local_len
    )
    hidden_grad = exchange(hg)
    row_mods = jnp.concatenate([gain_attn, 1.0 + scale_attn] + [zero] * 6, axis=0)
    late_got = pair_permute(late_send, CORE)
    left_got, right_got = after((left_got, right_got), late_keep)
    if lax.axis_size("dp") > 2 * SECOND:
        left, right = sum_over_rest(add(left, left_got)), sum_over_rest(add(right, right_got))
        sides = [(left,), (right,)]
    else:
        sides = [(left, left_got), (right, right_got)]
    near_send, near = near_halves(at, sides)
    near_got = pair_permute(near_send, 1, "sp")
    rows = late_row(after(attn_sums, near), early_parts, row_mods, ada_weight, timing)
    late_got = after(late_got, rows)
    own_quarter, *other_quarters = quarters(at, late_keep, late_got)
    quarter_parts = [own_quarter] + [
        pair_permute(p, bit)
        for p, bit in zip(other_quarters, (SECOND, FIRST, FIRST + SECOND))
    ]
    rows = after(rows, own_quarter)
    for bit in bits("dp"):
        rows = double(rows, bit, "dp")
    near_got, hidden_grad = after((near_got, hidden_grad), rows)
    far_send, far = far_halves(at, near, after(near_got, hidden_grad))
    far_got = pair_permute(far_send, 2, "sp")
    quarter_parts = after(quarter_parts, far)
    if lax.axis_size("dp") > 2 * SECOND:
        total = sum(p.astype(f32) for p in quarter_parts).astype(bf16)
        quarter_parts = [sum_over_rest(total)]
    late_near_send, late_near = near_halves(at, [quarter_parts])
    late_near_got = pair_permute(late_near_send, 1, "sp")
    rows = double(after(rows, late_near), 1, "sp")
    output = hand_over(after(output, late_near))
    late_near_got = after(late_near_got, rows, output)
    late_far_send, late_far = far_halves(at, late_near, late_near_got)
    late_far_got = pair_permute(late_far_send, 2, "sp")
    early_own = own_sum(far, after(far_got, late_far))
    early_four = spread(early_own)
    rows = double(after(rows, early_own), 2, "sp")
    late_own = own_sum(late_far, after(late_far_got, rows))
    hidden_grad = widen(after(hidden_grad, late_own))
    early_half = four_chips(at, after(early_four, hidden_grad), True)
    early_other = pair_permute(early_half, CORE)
    late_four = spread(after(late_own, early_half))
    time_rows = rows[:: lax.axis_size("dp"), 3 * width : 3 * width + cond]
    time_grad = jnp.concatenate([pick(time_rows, me ^ s)[None] for s in range(sp)], axis=0)
    n_row, n_col = row_keep.shape[1] // 2, col_keep.shape[1] // 2
    row_starts = [x * (n_row + n_col) + i for x in range(2) for i in range(0, n_row, half)]
    col_starts = [x * (n_row + n_col) + n_row + i for x in range(2) for i in range(0, n_col, half)]
    down_grad, up_grad, proj_grad, vectors = finish(
        core,
        early_half,
        after(early_other, late_four[0]),
        half,
        (
            (sp, 1, row_starts),
            (1, n_up, col_starts[:n_up]),
            (1, 1, col_starts[n_up : n_up + 1]),
            (1, 1, col_starts[n_up + 1 :]),
        ),
    )
    late_half = four_chips(at, after(late_four, down_grad), False)
    late_other = pair_permute(late_half, CORE)
    ada_weight_grad, *small = vector_outputs(at, after(rows, late_half), vectors, half, cond, sp)
    (qkv_grad,) = finish(
        core, late_half, after(late_other, ada_weight_grad), half, ((1, 3, [0, half, 2 * half]),)
    )
    ada_bias_grad, attn_gain_grad, mlp_gain_grad, up_bias_grad, down_bias_grad = (
        v.reshape(-1) for v in small
    )
    time_grad = time_grad.astype(f32)
    return (
        output,
        hidden_grad,
        time_grad,
        ada_weight_grad,
        ada_bias_grad,
        attn_gain_grad,
        qkv_grad,
        proj_grad,
        mlp_gain_grad,
        up_grad,
        up_bias_grad,
        down_grad,
        down_bias_grad,
    )


def solution(mesh):
    return jax.shard_map(
        body,
        mesh=mesh,
        in_specs=(P("dp", "sp", None), P("dp", None)) + (P(),) * 10 + (P("dp", "sp", None),),
        out_specs=(
            P("dp", "sp", None),
            P("dp", "sp", None),
            P("dp", None),
            P("sp", None),
            P("sp"),
            P("sp"),
            P("sp", None),
            P("sp", None),
            P("sp"),
            P("sp", None),
            P("sp"),
            P("sp", None),
            P("sp"),
        ),
        check_vma=False,
    )
```

profile of v0, /device:TPU:0, one launch (start us, length us, event | category | flops | bytes accessed | tf_op | source)
XLA Modules:
  0.0 350.6 jit_solution(3276820482250109097)
XLA Ops:
  0.7 6.5 %all-to-all-start = ((bf16[4,256,768]{2,1,0:T(8,128)(2,1)}), bf16[4,256,768]{2,1,0:T(8,128)(2,1)S(1)}, u32[]{:S(2)}, u32[]{:S(2)}) async-start(bf16[4,256,768]{2,1,0:T(8,128)(2,1)} %param.13), calls=%async_computation | async-start | bytes 3145728 | tf_op jit(solution)/shard_map/all_to_all | solution.py:859
  11.1 3.0 multiply_sine_fusion
  14.1 30.0 %all-to-all-done = bf16[4,256,768]{2,1,0:T(8,128)(2,1)S(1)} async-done(((bf16[4,256,768]{2,1,0:T(8,128)(2,1)}), bf16[4,256,768]{2,1,0:T(8,128)(2,1)S(1)}, u32[]{:S(2)}, u32[]{:S(2)}) %all-to-all-start) | async-done | bytes 1572896 | tf_op jit(solution)/shard_map/all_to_all | solution.py:859
  45.3 3.6 %all-to-all-start.1 = ((bf16[4,256,768]{2,1,0:T(8,128)(2,1)}), bf16[4,256,768]{2,1,0:T(8,128)(2,1)S(1)}, u32[]{:S(2)}, u32[]{:S(2)}) async-start(bf16[4,256,768]{2,1,0:T(8,128)(2,1)} %param.25), calls=%async_computation.1 | async-start | bytes 3145728 | tf_op jit(solution)/shard_map/all_to_all | solution.py:859
  48.9 8.7 %project_qkv.1 = (bf16[1024,768]{1,0:T(8,128)(2,1)}, bf16[1024,768]{1,0:T(8,128)(2,1)}, bf16[1024,768]{1,0:T(8,128)(2,1)}, bf16[1024,768]{1,0:T(8,128)(2,1)}) custom-call(bf16[1024,768]{1,0:T(8,128)(2,1)} %bitcast.34, f32[8,768]{1,0:T(8,128)} %get-tuple-element.223.mod_ref, bf16[768,2304]{1,0:T(8,128)(2,1)} %w_ref.3, ...), custom_call_target="tpu_custom_call" | custom-call | flops 40000000000 | bytes 100000000 | tf_op jit(solution)/shard_map/project_qkv/pallas_call | solution.py:88
  57.6 22.7 %attention_forward.1 = (bf16[1024,768]{1,0:T(8,128)(2,1)}, f32[6,2,1024]{2,1,0:T(2,128)}) custom-call(bf16[1024,768]{1,0:T(8,128)(2,1)} %get-tuple-element.107.q_ref, bf16[1024,768]{1,0:T(8,128)(2,1)} %get-tuple-element.108.k_ref, bf16[1024,768]{1,0:T(8,128)(2,1)} %get-tuple-element.109.v_ref), custom_call_target="tpu_custom_call" | custom-call | flops 40000000000 | bytes 100000000 | tf_op jit(solution)/shard_map/attention_forward/pallas_call | solution.py:128
  80.3 5.0 %all-to-all-done.1 = bf16[4,256,768]{2,1,0:T(8,128)(2,1)S(1)} async-done(((bf16[4,256,768]{2,1,0:T(8,128)(2,1)}), bf16[4,256,768]{2,1,0:T(8,128)(2,1)S(1)}, u32[]{:S(2)}, u32[]{:S(2)}) %all-to-all-start.1) | async-done | bytes 1572896 | tf_op jit(solution)/shard_map/all_to_all | solution.py:859
  86.4 35.9 %feed_forward.1 = (bf16[2,1024,768]{2,1,0:T(8,128)(2,1)}, bf16[1024,3072]{1,0:T(8,128)(2,1)}, bf16[1024,768]{1,0:T(8,128)(2,1)}, bf16[5,1024,768]{2,1,0:T(8,128)...) custom-call(bf16[1024,768]{1,0:T(8,128)(2,1)} %bitcast.35, ...), custom_call_target="tpu_custom_call" | custom-call | flops 40000000000 | bytes 100000000 | tf_op jit(solution)/shard_map/feed_forward/pallas_call | solution.py:267
  126.5 13.1 %column_grad.1 = (bf16[4,576,768]{2,1,0:T(8,128)(2,1)}, bf16[4,576,768]{2,1,0:T(8,128)(2,1)}) custom-call(s32[2]{0:T(128)} %pad_add_fusion.1.core_ref, bf16[2,1024,768]{2,1,0:T(8,128)(2,1)} %get-tuple-element.116.a_ref, bf16[5,1024,768]{2,1,0:T(8,128)(2,1)} %get-tuple-element.117.b_ref), custom_call_target="tpu_custom_call" | custom-call | flops 40000000000 | bytes 100000000 | tf_op jit(solution)/shard_map/column_grad/pallas_call | solution.py:436
  141.9 9.2 %row_grad.1 = (bf16[4,384,768]{2,1,0:T(8,128)(2,1)}, bf16[4,384,768]{2,1,0:T(8,128)(2,1)}) custom-call(s32[1]{0:T(128)} %bitcast.3.core_ref, bf16[1024,3072]{1,0:T(8,128)(2,1)} %get-tuple-element.121.a_ref, bf16[1024,768]{1,0:T(8,128)(2,1)} %get-tuple-element.122.b_ref), custom_call_target="tpu_custom_call" | custom-call | flops 40000000000 | bytes 100000000 | tf_op jit(solution)/shard_map/row_grad/pallas_call | solution.py:402
  152.2 3.6 %all-to-all-start.2 = ((bf16[4,256,768]{2,1,0:T(8,128)(2,1)}), bf16[4,256,768]{2,1,0:T(8,128)(2,1)S(1)}, u32[]{:S(2)}, u32[]{:S(2)}) async-start(bf16[4,256,768]{2,1,0:T(8,128)(2,1)} %bitcast.13), calls=%async_computation.2 | async-start | bytes 3145728 | tf_op jit(solution)/shard_map/all_to_all | solution.py:859
  156.1 7.9 %first_halves.1 = (bf16[4,480,384]{2,1,0:T(8,128)(2,1)}, bf16[4,480,384]{2,1,0:T(8,128)(2,1)}, bf16[4,480,384]{2,1,0:T(8,128)(2,1)}, bf16[4,480,384]{2,1,0:T(8,128)(2,1)}) custom-call(s32[3]{0:T(128)} %pad_add_fusion.at_ref, bf16[4,384,768]{2,1,0:T(8,128)(2,1)} %get-tuple-element.123.row_keep, bf16[4,384,768]{2,1,0:T(8,128)(2,1)} %collective-permute-done.row_got, ...), custom_call_target="tpu_custom_call" | custom-call | flops 40000000000 | bytes 100000000 | tf_op jit(solution)/shard_map/first_halves/pallas_call | solution.py:553
  167.0 34.3 %attention_backward.1.tile_ref.block_ref = bf16[3,1024,768]{2,1,0:T(8,128)(2,1)} custom-call(bf16[1024,768]{1,0:T(8,128)(2,1)} %get-tuple-element.107.q_ref, bf16[1024,768]{1,0:T(8,128)(2,1)} %get-tuple-element.108.k_ref, bf16[1024,768]{1,0:T(8,128)(2,1)} %get-tuple-element.109.v_ref, bf16[1024,768]{1,0:T(8,128)(2,1)} %get-tuple-element.132.do_ref, ...), custom_call_target="tpu_custom_call" | custom-call | flops 40000000000 | bytes 100000000 | tf_op jit(solution)/shard_map/attention_backward/pallas_call | solution.py:176
  202.4 4.5 %second_halves.1 = (bf16[4,240,384]{2,1,0:T(8,128)(2,1)}, bf16[4,240,384]{2,1,0:T(8,128)(2,1)}, bf16[4,240,384]{2,1,0:T(8,128)(2,1)}, bf16[4,240,384]{2,1,0:T(8,128)(2,1)}) custom-call(s32[3]{0:T(128)} %pad_add_fusion.at_ref, bf16[4,2,240,384]{3,2,1,0:T(8,128)(2,1)} %bitcast.47, bf16[4,2,240,384]{3,2,1,0:T(8,128)(2,1)} %bitcast.43, ...), custom_call_target="tpu_custom_call" | custom-call | flops 40000000000 | bytes 100000000 | tf_op jit(solution)/shard_map/second_halves/pallas_call | solution.py:579
  208.0 16.1 %late_grads.1 = (f32[8,768]{1,0:T(8,128)}, bf16[1024,768]{1,0:T(8,128)(2,1)}, bf16[4,288,768]{2,1,0:T(8,128)(2,1)}, bf16[4,288,768]{2,1,0:T(8,128)(2,1)}) custom-call(s32[1]{0:T(128)} %bitcast.3.core_ref, bf16[1024,768]{1,0:T(8,128)(2,1)} %bitcast.36, bf16[3,1024,768]{2,1,0:T(8,128)(2,1)} %attention_backward.1.tile_ref.block_ref, ...), custom_call_target="tpu_custom_call" | custom-call | flops 40000000000 | bytes 100000000 | tf_op jit(solution)/shard_map/late_grads/pallas_call | solution.py:354
  224.1 4.7 %all-to-all-start.3 = ((bf16[4,256,768]{2,1,0:T(8,128)(2,1)}), bf16[4,256,768]{2,1,0:T(8,128)(2,1)S(1)}, u32[]{:S(2)}, u32[]{:S(2)}) async-start(bf16[4,256,768]{2,1,0:T(8,128)(2,1)} %bitcast.37), calls=%async_computation.3 | async-start | bytes 3145728 | tf_op jit(solution)/shard_map/all_to_all | solution.py:859
  228.8 3.1 near_halves.2
  231.9 2.6 late_row.1
  235.8 3.6 %quarters.1 = (bf16[4,72,768]{2,1,0:T(8,128)(2,1)}, bf16[4,72,768]{2,1,0:T(8,128)(2,1)}, bf16[4,72,768]{2,1,0:T(8,128)(2,1)}, bf16[4,72,768]{2,1,0:T(8,128)(2,1)}) custom-call(s32[3]{0:T(128)} %pad_add_fusion.at_ref, bf16[4,4,72,768]{3,2,1,0:T(8,128)(2,1)} %bitcast.46, bf16[4,4,72,768]{3,2,1,0:T(8,128)(2,1)} %bitcast.40), custom_call_target="tpu_custom_call" | custom-call | flops 40000000000 | bytes 100000000 | tf_op jit(solution)/shard_map/quarters/pallas_call | solution.py:684
  250.4 22.5 %collective-permute-done.10.got = bf16[2,240,768]{2,1,0:T(8,128)(2,1)S(1)} collective-permute-done((bf16[2,240,768]{2,1,0:T(8,128)(2,1)}, bf16[2,240,768]{2,1,0:T(8,128)(2,1)S(1)}, u32[]{:S(2)}, u32[]{:S(2)}) %collective-permute-start.10) | collective-permute-done | bytes 737312 | tf_op jit(solution)/shard_map/ppermute | solution.py:504
  273.8 2.9 far_halves.2
  277.6 2.3 near_halves.3
  280.3 3.6 %hand_over.2 = bf16[4,256,768]{2,1,0:T(8,128)(2,1)} custom-call(bf16[4,256,768]{2,1,0:T(8,128)(2,1)} %copy-done.1), custom_call_target="tpu_custom_call" | custom-call | flops 40000000000 | bytes 100000000 | tf_op jit(solution)/shard_map/hand_over/pallas_call | solution.py:648
  285.6 2.5 collective-permute-start.17
  288.0 7.5 %collective-permute-done.14.got = bf16[2,72,768]{2,1,0:T(8,128)(2,1)S(1)} collective-permute-done((bf16[2,72,768]{2,1,0:T(8,128)(2,1)S(1)}, bf16[2,72,768]{2,1,0:T(8,128)(2,1)S(1)}, u32[]{:S(2)}, u32[]{:S(2)}) %collective-permute-start.14) | collective-permute-done | bytes 221216 | tf_op jit(solution)/shard_map/ppermute | solution.py:504
  298.0 9.3 %collective-permute-done.17.got_ref = bf16[240,768]{1,0:T(8,128)(2,1)S(1)} collective-permute-done((bf16[240,768]{1,0:T(8,128)(2,1)S(1)}, bf16[240,768]{1,0:T(8,128)(2,1)S(1)}, u32[]{:S(2)}, u32[]{:S(2)}) %collective-permute-start.17) | collective-permute-done | bytes 368672 | tf_op jit(solution)/shard_map/ppermute | solution.py:504
  313.5 2.5 collective-permute-done.18
  318.4 3.9 %hand_over.3 = f32[4,256,768]{2,1,0:T(8,128)} custom-call(bf16[4,256,768]{2,1,0:T(8,128)(2,1)} %copy-done.2), custom_call_target="tpu_custom_call" | custom-call | flops 40000000000 | bytes 100000000 | tf_op jit(solution)/shard_map/hand_over/pallas_call | solution.py:648
  322.7 3.9 %collective-permute-done.21.refs_3_ = bf16[240,768]{1,0:T(8,128)(2,1)S(1)} collective-permute-done((bf16[240,768]{1,0:T(8,128)(2,1)}, bf16[240,768]{1,0:T(8,128)(2,1)S(1)}, u32[]{:S(2)}, u32[]{:S(2)}) %collective-permute-start.21) | collective-permute-done | bytes 368672 | tf_op jit(solution)/shard_map/ppermute | solution.py:504
  327.4 2.6 four_chips.2
  335.2 4.6 %finish.2 = (f32[768,768]{1,0:T(8,128)}, f32[192,3072]{1,0:T(8,128)}, f32[192,768]{1,0:T(8,128)}, f32[192,768]{1,0:T(8,128)}) custom-call(s32[1]{0:T(128)} %bitcast.3.core_ref, bf16[960,768]{1,0:T(8,128)(2,1)} %bitcast.42, bf16[960,768]{1,0:T(8,128)(2,1)} %copy-done.16), custom_call_target="tpu_custom_call" | custom-call | flops 40000000000 | bytes 100000000 | tf_op jit(solution)/shard_map/finish/pallas_call | solution.py:735
  348.1 2.5 finish.3
  (175 shorter events, 60.9 us)
Async XLA Ops:
  0.7 43.4 %all-to-all-start = ((bf16[4,256,768]{2,1,0:T(8,128)(2,1)}), bf16[4,256,768]{2,1,0:T(8,128)(2,1)S(1)}, u32[]{:S(2)}, u32[]{:S(2)}) async-start(bf16[4,256,768]{2,1,0:T(8,128)(2,1)} %param.13), calls=%async_computation | async-start | bytes 3145728 | tf_op jit(solution)/shard_map/all_to_all | solution.py:859
  45.3 40.0 %all-to-all-start.1 = ((bf16[4,256,768]{2,1,0:T(8,128)(2,1)}), bf16[4,256,768]{2,1,0:T(8,128)(2,1)S(1)}, u32[]{:S(2)}, u32[]{:S(2)}) async-start(bf16[4,256,768]{2,1,0:T(8,128)(2,1)} %param.25), calls=%async_computation.1 | async-start | bytes 3145728 | tf_op jit(solution)/shard_map/all_to_all | solution.py:859
  123.3 16.3 %copy-start.6 = (f32[4,768]{1,0:T(4,128)}, f32[4,768]{1,0:T(4,128)S(1)}, u32[]{:S(2)}) copy-start(f32[4,768]{1,0:T(4,128)S(1)} %pad_maximum_fusion.3.parts_ref) | copy-start | bytes 36868
  141.9 14.2 %collective-permute-start.1 = (bf16[4,576,768]{2,1,0:T(8,128)(2,1)}, bf16[4,576,768]{2,1,0:T(8,128)(2,1)}, u32[]{:S(2)}, u32[]{:S(2)}) collective-permute-start(bf16[4,576,768]{2,1,0:T(8,128)(2,1)} %get-tuple-element.125), channel_id=1, source_target_pairs={{0,4},{4,0},{8,12},{12,8},{16,20},{20,16},{24,28},{28,24},{1,5},{5... | collective-permute-start | bytes 10616840 | tf_op jit(solution)/shard_map/ppermute | solution.py:504
  151.1 5.0 %collective-permute-start = (bf16[4,384,768]{2,1,0:T(8,128)(2,1)}, bf16[4,384,768]{2,1,0:T(8,128)(2,1)}, u32[]{:S(2)}, u32[]{:S(2)}) collective-permute-start(bf16[4,384,768]{2,1,0:T(8,128)(2,1)} %get-tuple-element.124), channel_id=1, source_target_pairs={{0,4},{4,0},{8,12},{12,8},{16,20},{20,16},{24,28},{28,24},{1,5},{5... | collective-permute-start | bytes 7077896 | tf_op jit(solution)/shard_map/ppermute | solution.py:504
  152.2 49.1 %all-to-all-start.2 = ((bf16[4,256,768]{2,1,0:T(8,128)(2,1)}), bf16[4,256,768]{2,1,0:T(8,128)(2,1)S(1)}, u32[]{:S(2)}, u32[]{:S(2)}) async-start(bf16[4,256,768]{2,1,0:T(8,128)(2,1)} %bitcast.13), calls=%async_computation.2 | async-start | bytes 3145728 | tf_op jit(solution)/shard_map/all_to_all | solution.py:859
  163.9 37.3 %collective-permute-start.2 = (bf16[4,480,384]{2,1,0:T(8,128)(2,1)}, bf16[4,480,384]{2,1,0:T(8,128)(2,1)S(1)}, u32[]{:S(2)}, u32[]{:S(2)}) collective-permute-start(bf16[4,480,384]{2,1,0:T(8,128)(2,1)} %get-tuple-element.126), channel_id=1, source_target_pairs={{0,8},{4,12},{8,0},{12,4},{16,24},{20,28},{24,16},{28,20},{1,9},{5... | collective-permute-start | bytes 4423688 | tf_op jit(solution)/shard_map/ppermute | solution.py:504
  165.4 35.9 %collective-permute-start.3 = (bf16[4,480,384]{2,1,0:T(8,128)(2,1)}, bf16[4,480,384]{2,1,0:T(8,128)(2,1)}, u32[]{:S(2)}, u32[]{:S(2)}) collective-permute-start(bf16[4,480,384]{2,1,0:T(8,128)(2,1)} %get-tuple-element.127), channel_id=1, source_target_pairs={{0,16},{4,20},{8,24},{12,28},{16,0},{20,4},{24,8},{28,12},{1,17},{... | collective-permute-start | bytes 4423688 | tf_op jit(solution)/shard_map/ppermute | solution.py:504
  206.9 21.9 %collective-permute-start.5 = (bf16[4,240,384]{2,1,0:T(8,128)(2,1)}, bf16[4,240,384]{2,1,0:T(8,128)(2,1)}, u32[]{:S(2)}, u32[]{:S(2)}) collective-permute-start(bf16[4,240,384]{2,1,0:T(8,128)(2,1)} %get-tuple-element.145), channel_id=1, source_target_pairs={{0,16},{4,20},{8,24},{12,28},{16,0},{20,4},{24,8},{28,12},{1,17},{... | collective-permute-start | bytes 2211848 | tf_op jit(solution)/shard_map/ppermute | solution.py:504
  207.5 21.4 %collective-permute-start.6 = (bf16[4,240,384]{2,1,0:T(8,128)(2,1)}, bf16[4,240,384]{2,1,0:T(8,128)(2,1)}, u32[]{:S(2)}, u32[]{:S(2)}) collective-permute-start(bf16[4,240,384]{2,1,0:T(8,128)(2,1)} %get-tuple-element.146), channel_id=1, source_target_pairs={{0,8},{4,12},{8,0},{12,4},{16,24},{20,28},{24,16},{28,20},{1,9},{5... | collective-permute-start | bytes 2211848 | tf_op jit(solution)/shard_map/ppermute | solution.py:504
  224.1 10.5 %collective-permute-start.4 = (bf16[4,288,768]{2,1,0:T(8,128)(2,1)}, bf16[4,288,768]{2,1,0:T(8,128)(2,1)S(1)}, u32[]{:S(2)}, u32[]{:S(2)}) collective-permute-start(bf16[4,288,768]{2,1,0:T(8,128)(2,1)} %get-tuple-element.143), channel_id=1, source_target_pairs={{0,4},{4,0},{8,12},{12,8},{16,20},{20,16},{24,28},{28,24},{1,5},{5... | collective-permute-start | bytes 5308424 | tf_op jit(solution)/shard_map/ppermute | solution.py:504
  224.1 48.8 %all-to-all-start.3 = ((bf16[4,256,768]{2,1,0:T(8,128)(2,1)}), bf16[4,256,768]{2,1,0:T(8,128)(2,1)S(1)}, u32[]{:S(2)}, u32[]{:S(2)}) async-start(bf16[4,256,768]{2,1,0:T(8,128)(2,1)} %bitcast.37), calls=%async_computation.3 | async-start | bytes 3145728 | tf_op jit(solution)/shard_map/all_to_all | solution.py:859
  239.3 2.1 collective-permute-start.11
  239.5 33.4 %collective-permute-start.10 = (bf16[2,240,768]{2,1,0:T(8,128)(2,1)}, bf16[2,240,768]{2,1,0:T(8,128)(2,1)S(1)}, u32[]{:S(2)}, u32[]{:S(2)}) collective-permute-start(bf16[2,240,768]{2,1,0:T(8,128)(2,1)} %get-tuple-element.156), channel_id=1, source_target_pairs={{0,1},{1,0},{2,3},{3,2},{4,5},{5,4},{6,7},{7,6},{8,9},{9,8},{10,11... | collective-permute-start | bytes 2211848 | tf_op jit(solution)/shard_map/ppermute | solution.py:504
  241.4 3.7 %collective-permute-start.12 = (bf16[2,2560]{1,0:T(2,128)(2,1)S(1)}, bf16[2,2560]{1,0:T(2,128)(2,1)S(1)}, u32[]{:S(2)}, u32[]{:S(2)}) collective-permute-start(bf16[2,2560]{1,0:T(2,128)(2,1)S(1)} %pad_maximum_fusion.4), channel_id=1, source_target_pairs={{0,8},{4,12},{8,0},{12,4},{16,24},{20,28},{24,16},{28,20},{1,9},{5... | collective-permute-start | bytes 30728 | tf_op jit(solution)/shard_map/ppermute | solution.py:504
  245.2 5.1 %collective-permute-start.13 = (bf16[4,2560]{1,0:T(4,128)(2,1)S(1)}, bf16[4,2560]{1,0:T(4,128)(2,1)S(1)}, u32[]{:S(2)}, u32[]{:S(2)}) collective-permute-start(bf16[4,2560]{1,0:T(4,128)(2,1)S(1)} %pad_maximum_fusion.2), channel_id=1, source_target_pairs={{0,16},{4,20},{8,24},{12,28},{16,0},{20,4},{24,8},{28,12},{1,17},{... | collective-permute-start | bytes 61448 | tf_op jit(solution)/shard_map/ppermute | solution.py:504
  246.8 29.8 %collective-permute-start.7 = (bf16[4,72,768]{2,1,0:T(8,128)(2,1)}, bf16[4,72,768]{2,1,0:T(8,128)(2,1)S(1)}, u32[]{:S(2)}, u32[]{:S(2)}) collective-permute-start(bf16[4,72,768]{2,1,0:T(8,128)(2,1)} %get-tuple-element.153), channel_id=1, source_target_pairs={{0,16},{4,20},{8,24},{12,28},{16,0},{20,4},{24,8},{28,12},{1,17},{... | collective-permute-start | bytes 1327112 | tf_op jit(solution)/shard_map/ppermute | solution.py:504
  247.3 29.3 %collective-permute-start.8 = (bf16[4,72,768]{2,1,0:T(8,128)(2,1)}, bf16[4,72,768]{2,1,0:T(8,128)(2,1)S(1)}, u32[]{:S(2)}, u32[]{:S(2)}) collective-permute-start(bf16[4,72,768]{2,1,0:T(8,128)(2,1)} %get-tuple-element.154), channel_id=1, source_target_pairs={{0,8},{4,12},{8,0},{12,4},{16,24},{20,28},{24,16},{28,20},{1,9},{5... | collective-permute-start | bytes 1327112 | tf_op jit(solution)/shard_map/ppermute | solution.py:504
  248.8 27.9 %collective-permute-start.9 = (bf16[4,72,768]{2,1,0:T(8,128)(2,1)}, bf16[4,72,768]{2,1,0:T(8,128)(2,1)}, u32[]{:S(2)}, u32[]{:S(2)}) collective-permute-start(bf16[4,72,768]{2,1,0:T(8,128)(2,1)} %get-tuple-element.155), channel_id=1, source_target_pairs={{0,24},{4,28},{8,16},{12,20},{16,8},{20,12},{24,0},{28,4},{1,25},{... | collective-permute-start | bytes 1327112 | tf_op jit(solution)/shard_map/ppermute | solution.py:504
  279.9 8.1 %collective-permute-start.15 = (bf16[8,2560]{1,0:T(8,128)(2,1)S(1)}, bf16[8,2560]{1,0:T(8,128)(2,1)S(1)}, u32[]{:S(2)}, u32[]{:S(2)}) collective-permute-start(bf16[8,2560]{1,0:T(8,128)(2,1)S(1)} %pad_maximum_fusion.1), channel_id=1, source_target_pairs={{0,1},{1,0},{2,3},{3,2},{4,5},{5,4},{6,7},{7,6},{8,9},{9,8},{10,11... | collective-permute-start | bytes 122888 | tf_op jit(solution)/shard_map/ppermute | solution.py:504
  283.8 11.7 %collective-permute-start.14 = (bf16[2,72,768]{2,1,0:T(8,128)(2,1)S(1)}, bf16[2,72,768]{2,1,0:T(8,128)(2,1)S(1)}, u32[]{:S(2)}, u32[]{:S(2)}) collective-permute-start(bf16[2,72,768]{2,1,0:T(8,128)(2,1)S(1)} %copy-done.27), channel_id=1, source_target_pairs={{0,1},{1,0},{2,3},{3,2},{4,5},{5,4},{6,7},{7,6},{8,9},{9,8},{10,11... | collective-permute-start | bytes 663560 | tf_op jit(solution)/shard_map/ppermute | solution.py:504
  285.6 21.7 %collective-permute-start.17 = (bf16[240,768]{1,0:T(8,128)(2,1)S(1)}, bf16[240,768]{1,0:T(8,128)(2,1)S(1)}, u32[]{:S(2)}, u32[]{:S(2)}) collective-permute-start(bf16[240,768]{1,0:T(8,128)(2,1)S(1)} %copy-done.22), channel_id=1, source_target_pairs={{0,2},{1,3},{2,0},{3,1},{4,6},{5,7},{6,4},{7,5},{8,10},{9,11},{10,... | collective-permute-start | bytes 1105928 | tf_op jit(solution)/shard_map/ppermute | solution.py:504
  298.0 18.0 %collective-permute-start.16 = (bf16[72,768]{1,0:T(8,128)(2,1)}, bf16[72,768]{1,0:T(8,128)(2,1)S(1)}, u32[]{:S(2)}, u32[]{:S(2)}) collective-permute-start(bf16[72,768]{1,0:T(8,128)(2,1)} %get-tuple-element.173), channel_id=1, source_target_pairs={{0,2},{1,3},{2,0},{3,1},{4,6},{5,7},{6,4},{7,5},{8,10},{9,11},{10,... | collective-permute-start | bytes 331784 | tf_op jit(solution)/shard_map/ppermute | solution.py:504
  310.0 6.0 %collective-permute-start.18 = (bf16[16,2560]{1,0:T(8,128)(2,1)S(1)}, bf16[16,2560]{1,0:T(8,128)(2,1)S(1)}, u32[]{:S(2)}, u32[]{:S(2)}) collective-permute-start(bf16[16,2560]{1,0:T(8,128)(2,1)S(1)} %constant_dynamic-update-slice_fusion), channel_id=1, source_target_pairs={{0,2},{1,3},{2,0},{3,1},{4,6},{5,7},{6,4},{7,5},{8,10},{9,11},{10,... | collective-permute-start | bytes 245768 | tf_op jit(solution)/shard_map/ppermute | solution.py:504
  310.0 12.3 %collective-permute-start.19 = (bf16[240,768]{1,0:T(8,128)(2,1)}, bf16[240,768]{1,0:T(8,128)(2,1)S(1)}, u32[]{:S(2)}, u32[]{:S(2)}) collective-permute-start(bf16[240,768]{1,0:T(8,128)(2,1)} %own_sum.2.refs_0_), channel_id=1, source_target_pairs={{0,16},{4,20},{8,24},{12,28},{16,0},{20,4},{24,8},{28,12},{1,17},{... | collective-permute-start | bytes 1105928 | tf_op jit(solution)/shard_map/ppermute | solution.py:504
  311.6 11.1 %collective-permute-start.20 = (bf16[240,768]{1,0:T(8,128)(2,1)}, bf16[240,768]{1,0:T(8,128)(2,1)S(1)}, u32[]{:S(2)}, u32[]{:S(2)}) collective-permute-start(bf16[240,768]{1,0:T(8,128)(2,1)} %own_sum.2.refs_0_), channel_id=1, source_target_pairs={{0,8},{4,12},{8,0},{12,4},{16,24},{20,28},{24,16},{28,20},{1,9},{5... | collective-permute-start | bytes 1105928 | tf_op jit(solution)/shard_map/ppermute | solution.py:504
  313.1 13.6 %collective-permute-start.21 = (bf16[240,768]{1,0:T(8,128)(2,1)}, bf16[240,768]{1,0:T(8,128)(2,1)S(1)}, u32[]{:S(2)}, u32[]{:S(2)}) collective-permute-start(bf16[240,768]{1,0:T(8,128)(2,1)} %own_sum.2.refs_0_), channel_id=1, source_target_pairs={{0,24},{4,28},{8,16},{12,20},{16,8},{20,12},{24,0},{28,4},{1,25},{... | collective-permute-start | bytes 1105928 | tf_op jit(solution)/shard_map/ppermute | solution.py:504
  329.9 4.1 %collective-permute-start.25 = (bf16[960,768]{1,0:T(8,128)(2,1)}, bf16[960,768]{1,0:T(8,128)(2,1)S(1)}, u32[]{:S(2)}, u32[]{:S(2)}) collective-permute-start(bf16[960,768]{1,0:T(8,128)(2,1)} %bitcast.41), channel_id=1, source_target_pairs={{0,4},{4,0},{8,12},{12,8},{16,20},{20,16},{24,28},{28,24},{1,5},{5... | collective-permute-start | bytes 4423688 | tf_op jit(solution)/shard_map/ppermute | solution.py:504
  330.6 9.3 %collective-permute-start.22 = (bf16[72,768]{1,0:T(8,128)(2,1)S(1)}, bf16[72,768]{1,0:T(8,128)(2,1)S(1)}, u32[]{:S(2)}, u32[]{:S(2)}) collective-permute-start(bf16[72,768]{1,0:T(8,128)(2,1)S(1)} %copy-done.29), channel_id=1, source_target_pairs={{0,16},{4,20},{8,24},{12,28},{16,0},{20,4},{24,8},{28,12},{1,17},{... | collective-permute-start | bytes 331784 | tf_op jit(solution)/shard_map/ppermute | solution.py:504
  332.1 7.8 %collective-permute-start.23 = (bf16[72,768]{1,0:T(8,128)(2,1)S(1)}, bf16[72,768]{1,0:T(8,128)(2,1)S(1)}, u32[]{:S(2)}, u32[]{:S(2)}) collective-permute-start(bf16[72,768]{1,0:T(8,128)(2,1)S(1)} %copy-done.29), channel_id=1, source_target_pairs={{0,8},{4,12},{8,0},{12,4},{16,24},{20,28},{24,16},{28,20},{1,9},{5... | collective-permute-start | bytes 331784 | tf_op jit(solution)/shard_map/ppermute | solution.py:504
  333.6 6.3 %collective-permute-start.24 = (bf16[72,768]{1,0:T(8,128)(2,1)S(1)}, bf16[72,768]{1,0:T(8,128)(2,1)S(1)}, u32[]{:S(2)}, u32[]{:S(2)}) collective-permute-start(bf16[72,768]{1,0:T(8,128)(2,1)S(1)} %copy-done.29), channel_id=1, source_target_pairs={{0,24},{4,28},{8,16},{12,20},{16,8},{20,12},{24,0},{28,4},{1,25},{... | collective-permute-start | bytes 331784 | tf_op jit(solution)/shard_map/ppermute | solution.py:504
  342.4 4.9 %collective-permute-start.26 = (bf16[288,768]{1,0:T(8,128)(2,1)}, bf16[288,768]{1,0:T(8,128)(2,1)S(1)}, u32[]{:S(2)}, u32[]{:S(2)}) collective-permute-start(bf16[288,768]{1,0:T(8,128)(2,1)} %bitcast.44), channel_id=1, source_target_pairs={{0,4},{4,0},{8,12},{12,8},{16,20},{20,16},{24,28},{28,24},{1,5},{5... | collective-permute-start | bytes 1327112 | tf_op jit(solution)/shard_map/ppermute | solution.py:504
  (33 other events, 114.5 us)
where the time goes:
time: 353 us; the launch traced here: 351 us
  Pallas kernels  196 us (56%)
  waiting for transfers between devices  83.8 us (24%)
  starting transfers between devices  43.2 us (12%)
  local copies, waits for them, and re-layouts  14.3 us (4%)
  other arithmetic  12.1 us (3%)
    ppermute x27, waiting for transfers between devices, pair_permute(): return lax.ppermute(value, axis, [(i, i ^ bit) for i in range(n)])  48.8 us
    pallas_call x1, Pallas kernels, feed_forward(): pl.pallas_call(mlp_kernel, grid=(length // rows,), in_specs=[block, block...  35.9 us
    all_to_all x4, waiting for transfers between devices, exchange(): return lax.all_to_all(values, 'sp', split_axis=0, concat_axis=0, tiled=True)  35 us
    pallas_call x1, Pallas kernels, attention_backward(): pl.pallas_call(attention_backward_kernel, grid=(count,), in_specs=[block]...  34.3 us
    ppermute x27, starting transfers between devices, pair_permute(): return lax.ppermute(value, axis, [(i, i ^ bit) for i in range(n)])  24.9 us
    pallas_call x1, Pallas kernels, attention_forward(): pl.pallas_call(attention_forward_kernel, grid=(pairs,), in_specs=[block]...  22.7 us
    all_to_all x4, starting transfers between devices, exchange(): return lax.all_to_all(values, 'sp', split_axis=0, concat_axis=0, tiled=True)  18.3 us
    pallas_call x1, Pallas kernels, late_grads(): pl.pallas_call(functools.partial(late_grads_kernel, tiles=tiles), grid_sp...  16.1 us
  transfers between devices with their start and end apart: 31, of which 10 were waited for; matrix products, arithmetic and copies ran while one was open for 3% of the time, Pallas kernels for 37%

commit v1 on v0

--- a/solution.py
+++ b/solution.py
@@ -8,6 +8,8 @@
 from jax.sharding import PartitionSpec as P
 
 HEAD_DIM = 64
+VMEM = pl.BlockSpec(memory_space=pltpu.VMEM)
+SMEM = pl.BlockSpec(memory_space=pltpu.SMEM)
 HALF = HEAD_DIM // 2
 LANES = 128
 EPSILON = 1e-05
@@ -90,8 +92,8 @@
         grid=(length // rows,),
         in_specs=[
             block,
-            pl.BlockSpec(mods.shape, lambda i: (0, 0)),
-            pl.BlockSpec(weight.shape, lambda i: (0, 0)),
+            VMEM,
+            VMEM,
             table,
             table,
         ],
@@ -102,23 +104,34 @@
     )(x, mods, weight, cos, sin)
 
 
-def attention_forward_kernel(q_ref, k_ref, v_ref, o_ref, lse_ref):
-    q, k, v = q_ref[...], k_ref[...], v_ref[...]
+def attention_forward_kernel(q_ref, k_ref, v_ref, o_ref, lse_ref, *, chunk, ahead):
+    k, v = k_ref[...], v_ref[...]
     first = lax.broadcasted_iota(jnp.int32, (1, LANES), 1) < HEAD_DIM
     c = LOG2E * SCALE
-    outs = []
-    for h in range(2):
-        mine = first if h == 0 else ~first
-        kh = jnp.where(mine, k, jnp.zeros_like(k))
-        st = dot_nt(kh, q)
+    masks = (first, ~first)
+    keys = [jnp.where(m, k, jnp.zeros_like(k)) for m in masks]
+    values = [jnp.where(m, v, jnp.ones_like(v)) for m in masks]
+    items = [(h, start) for start in range(0, q_ref.shape[0], chunk) for h in range(2)]
+
+    def scores(h, start):
+        return dot_nt(keys[h], q_ref[start : start + chunk, :])
+
+    waiting = [scores(*item) for item in items[:ahead]]
+    outs = {}
+    for i, (h, start) in enumerate(items):
+        st = waiting.pop(0)
+        if i + ahead < len(items):
+            waiting.append(scores(*items[i + ahead]))
+        rows = slice(start, start + chunk)
         top = jnp.max(st, axis=0, keepdims=True) * c
         p = jnp.exp2(st * c - top).astype(bf16)
-        ot = dot_tn(jnp.where(mine, v, jnp.ones_like(v)), p)
+        ot = dot_tn(values[h], p)
         own, ones = (ot[:HEAD_DIM], ot[HEAD_DIM:]) if h == 0 else (ot[HEAD_DIM:], ot[:HEAD_DIM])
         total = ones[0:1]
-        outs.append(own * (1.0 / total))
-        lse_ref[0, h : h + 1, :] = top + jnp.log2(total)
-    o_ref[...] = jnp.concatenate(outs, axis=0).T.astype(bf16)
+        outs[h] = own * (1.0 / total)
+        lse_ref[0, h : h + 1, rows] = top + jnp.log2(total)
+        if h == 1:
+            o_ref[rows, :] = jnp.concatenate([outs[0], outs[1]], axis=0).T.astype(bf16)
 
 
 def attention_forward(q, k, v):
@@ -126,7 +139,7 @@
     pairs = width // LANES
     block = pl.BlockSpec((length, LANES), lambda i: (0, i))
     return pl.pallas_call(
-        attention_forward_kernel,
+        functools.partial(attention_forward_kernel, chunk=length // 2, ahead=2),
         grid=(pairs,),
         in_specs=[block] * 3,
         out_specs=[block, pl.BlockSpec((1, 2, length), lambda i: (i, 0, 0))],
@@ -213,12 +226,14 @@
         square = pre * pre
         t = jnp.tanh(pre * (c0 + c1 * square))
         half = 0.5 + 0.5 * t
-        act = (pre * half).astype(bf16)
+        wide_act = pre * half
+        act = wide_act.astype(bf16)
         act_ref[:, cols] = act
-        slope = half + (0.5 * pre) * (1.0 - t * t) * (c0 + (3.0 * c1) * square)
-        gp = (slope * dot_nt(gd, wd_ref[cols, :])).astype(bf16)
+        slope = half + wide_act * (1.0 - half) * (2.0 * c0 + (6.0 * c1) * square)
+        wide_gp = slope * dot_nt(gd, wd_ref[cols, :])
+        gp = wide_gp.astype(bf16)
         gp_ref[at // chunk] = gp
-        up_sums.append(column_sum(gp.astype(f32)))
+        up_sums.append(column_sum(wide_gp))
         d = dot_nn(act, wd_ref[cols, :])
         g = dot_nt(gp, wu_ref[:, cols])
         down, grad_mod = (d, g) if down is None else (down + d, grad_mod + g)
@@ -259,15 +274,12 @@
     block = pl.BlockSpec((rows, width), lambda i: (i, 0))
     wide = pl.BlockSpec((rows, ff), lambda i: (i, 0))
 
-    def whole(a):
-        return pl.BlockSpec(a.shape, lambda i: (0, 0), pipeline_mode=pl.Buffered(1))
-
     narrow = jax.ShapeDtypeStruct((length, width), bf16)
     broad = jax.ShapeDtypeStruct((length, ff), bf16)
     return pl.pallas_call(
         mlp_kernel,
         grid=(length // rows,),
-        in_specs=[block, block, block] + [whole(a) for a in (mods, up_bias, wo, wu, wd)],
+        in_specs=[block, block, block] + [VMEM] * 5,
         out_specs=[
             pl.BlockSpec((2, rows, width), lambda i: (0, i, 0)),
             wide,
@@ -292,8 +304,8 @@
 
 
 def late_grads_kernel(
-    core_ref, x_ref, tile_ref, gm_ref, mod_ref, w_ref, xm_ref, block_ref,
-    sum_ref, hg_ref, send_ref, keep_ref, turned_ref, *, tiles,
+    core_ref, x_ref, tile_ref, gm_ref, mod_ref, w_ref, xm_ref, ada_ref, timing_ref, early_ref, block_ref,
+    time_ref, hg_ref, send_ref, keep_ref, turned_ref, sum_ref, *, tiles, parts,
 ):
     step = pl.program_id(0)
     width = x_ref.shape[1]
@@ -323,7 +335,7 @@
     def _():
         turned_ref[...] = xm_ref[...].T
 
-    @pl.when(step >= tiles)
+    @pl.when((step >= tiles) & (step < tiles + parts))
     def _():
         product = dot_nn(turned_ref[...], block_ref[0])
         half = send_ref.shape[1]
@@ -331,8 +343,38 @@
             send_ref[i] = send
             keep_ref[i] = keep
 
-
-def late_grads(core, x, grads, gm, mods, weight, xm, sp, rows):
+    @pl.when(step == tiles + parts)
+    def _():
+        sp, half, _ = send_ref.shape
+        shift, scaled = sum_ref[0:1, :], sum_ref[1:2, :]
+        scale = scaled * mod_ref[2:3, :]
+        gain = scaled * mod_ref[3:4, :]
+        row = jnp.concatenate([shift, scale] + [early_ref[i : i + 1, :] for i in range(4)], axis=1)
+        high = row.astype(bf16)
+        low = (row - high.astype(f32)).astype(bf16)
+        time_ref[...] = (dot_nt(high, ada_ref[...]) + dot_nt(low, ada_ref[...])).astype(bf16)
+        bias = jnp.concatenate([shift, scale, jnp.zeros((1, 4 * width), f32)], axis=1)
+        count, own, quarter = timing_ref.shape[0] // sp, 6 * width // sp, width // sp
+        for ref, first in ((send_ref, core_ref[0] == 1), (keep_ref, core_ref[0] == 0)):
+            part = jnp.where(first, shift, scale)
+            for i in range(sp):
+                ref[i, :count] = (timing_ref[i * count : (i + 1) * count, :] * part).astype(bf16)
+                mine = bias[:, i * own : (i + 1) * own]
+                rest = jnp.concatenate(
+                    [
+                        mine[:, width:],
+                        gain[:, i * quarter : (i + 1) * quarter],
+                        jnp.zeros((1, 2 * width - own - quarter), f32),
+                    ],
+                    axis=1,
+                )
+                sums = jnp.concatenate(
+                    [jnp.where(first, mine[:, :width], rest), jnp.zeros((half - count - 1, width), f32)], axis=0
+                )
+                ref[i, count:] = sums.astype(bf16)
+
+
+def late_grads(core, x, grads, gm, mods, weight, xm, ada, timing, early, sp, rows):
     length, width = x.shape
     tiles = length // rows
     n = grads.shape[0]
@@ -344,39 +386,43 @@
     def part(i):
         return jnp.maximum(i - tiles, 0)
 
+    def piece(i, c):
+        return (jnp.minimum(part(i), n - 1), 0, 0)
+
     block = pl.BlockSpec((rows, width), tile)
 
-    def whole(a):
-        return pl.BlockSpec(a.shape, lambda i, c: (0, 0), pipeline_mode=pl.Buffered(1))
-
     out = pl.BlockSpec((sp, half, width), lambda i, c: (0, part(i), 0))
-    shape = jax.ShapeDtypeStruct((sp, n * half, width), bf16)
-    return pl.pallas_call(
-        functools.partial(late_grads_kernel, tiles=tiles),
+    shape = jax.ShapeDtypeStruct((sp, (n + 1) * half, width), bf16)
+    cond = timing.shape[0]
+    return pl.pallas_call(
+        functools.partial(late_grads_kernel, tiles=tiles, parts=n),
         grid_spec=pltpu.PrefetchScalarGridSpec(
             num_scalar_prefetch=1,
-            grid=(tiles + n,),
+            grid=(tiles + n + 1,),
             in_specs=[
                 block,
                 pl.BlockSpec((n, rows, width), lambda i, c: (0, jnp.minimum(i, tiles - 1), 0)),
                 block,
-                whole(mods),
-                whole(weight),
-                whole(xm),
-                pl.BlockSpec((1, length, width), lambda i, c: (part(i), 0, 0)),
+                VMEM,
+                VMEM,
+                VMEM,
+                VMEM,
+                VMEM,
+                VMEM,
+                pl.BlockSpec((1, length, width), piece),
             ],
-            out_specs=[pl.BlockSpec((8, width), lambda i, c: (0, 0)), block, out, out],
-            scratch_shapes=[pltpu.VMEM((width, length), bf16)],
+            out_specs=[pl.BlockSpec((1, cond), lambda i, c: (0, 0)), block, out, out],
+            scratch_shapes=[pltpu.VMEM((width, length), bf16), pltpu.VMEM((8, width), f32)],
         ),
         out_shape=[
-            jax.ShapeDtypeStruct((8, width), f32),
+            jax.ShapeDtypeStruct((1, cond), bf16),
             jax.ShapeDtypeStruct((length, width), bf16),
             shape,
             shape,
         ],
         cost_estimate=COVER,
         name="late_grads",
-    )(core, x, grads, gm, mods, weight, xm, grads)
+    )(core, x, grads, gm, mods, weight, xm, ada, timing, early, grads)
 
 
 def split_halves(product, half, this_core):
@@ -416,82 +462,73 @@
     )(core, a, b)
 
 
-def column_grad_kernel(core_ref, a_ref, b_ref, send_ref, keep_ref, turned_ref):
-    @pl.when((pl.program_id(0) == 0) | (pl.program_id(0) == core_ref[1]))
+def column_grad_kernel(
+    core_ref, sum_ref, up_sum_ref, mod_ref, timing_ref, a_ref, b_ref, send_ref, keep_ref, parts_ref, *, blocks
+):
+    step = pl.program_id(0)
+    sp, half, width = send_ref.shape
+
+    @pl.when(step < blocks)
     def _():
-        turned_ref[...] = a_ref[0].T
-
-    product = dot_nn(turned_ref[...], b_ref[0])
-    for i, (send, keep) in enumerate(split_halves(product, send_ref.shape[1], core_ref[0] == 0)):
-        send_ref[i] = send
-        keep_ref[i] = keep
-
-
-def column_grad(core, a, b, sp, blocks, second):
+        product = dot_tn(a_ref[0], b_ref[0])
+        for i, (send, keep) in enumerate(split_halves(product, half, core_ref[0] == 0)):
+            send_ref[i] = send
+            keep_ref[i] = keep
+
+    @pl.when(step == blocks)
+    def _():
+        scaled = sum_ref[3:4, :]
+        parts = [sum_ref[4:5, :], sum_ref[2:3, :], scaled * mod_ref[0:1, :], sum_ref[0:1, :]]
+        for i, part in enumerate(parts):
+            parts_ref[i : i + 1, :] = part
+        gain = scaled * mod_ref[1:2, :]
+        bias = jnp.concatenate([jnp.zeros((1, 2 * width), f32)] + parts, axis=1)
+        count, own, quarter = timing_ref.shape[0] // sp, 6 * width // sp, width // sp
+        for ref, first in ((send_ref, core_ref[0] == 1), (keep_ref, core_ref[0] == 0)):
+            for i in range(sp):
+                column = timing_ref[i * count : (i + 1) * count, :]
+                for p in range(2):
+                    part = jnp.where(first, parts[p], parts[p + 2])
+                    ref[i, p * count : (p + 1) * count] = (column * part).astype(bf16)
+                shard = slice(i * quarter, (i + 1) * quarter)
+                mine = bias[:, i * own : (i + 1) * own]
+                gains = jnp.concatenate(
+                    [gain[:, shard], sum_ref[1:2, shard], jnp.zeros((1, width - 2 * quarter), f32)], axis=1
+                )
+                rest = jnp.concatenate([mine[:, width:], jnp.zeros((1, 2 * width - own), f32)], axis=1)
+                sums = jnp.concatenate(
+                    [
+                        jnp.where(first, up_sum_ref[:, i * width : (i + 1) * width], gains),
+                        jnp.where(first, mine[:, :width], rest),
+                        jnp.zeros((half - 2 * count - 2, width), f32),
+                    ],
+                    axis=0,
+                )
+                ref[i, 2 * count :] = sums.astype(bf16)
+
+
+def column_grad(core, sums, up_sum, mods, timing, a, b, sp, second):
     _, length, width = a.shape
     n = b.shape[0]
     half = width // sp // 2
-    out = jax.ShapeDtypeStruct((sp, blocks * half, width), bf16)
+    out = jax.ShapeDtypeStruct((sp, (n + 1) * half, width), bf16)
     block = pl.BlockSpec((sp, half, width), lambda j, c: (0, j, 0))
     return pl.pallas_call(
-        column_grad_kernel,
+        functools.partial(column_grad_kernel, blocks=n),
         grid_spec=pltpu.PrefetchScalarGridSpec(
             num_scalar_prefetch=1,
-            grid=(n,),
-            in_specs=[
-                pl.BlockSpec((1, length, width), lambda j, c: (j // second, 0, 0)),
-                pl.BlockSpec((1, length, width), lambda j, c: (j, 0, 0)),
+            grid=(n + 1,),
+            in_specs=[VMEM] * 4
+            + [
+                pl.BlockSpec((1, length, width), lambda j, c: (jnp.minimum(j, n - 1) // second, 0, 0)),
+                pl.BlockSpec((1, length, width), lambda j, c: (jnp.minimum(j, n - 1), 0, 0)),
             ],
-            out_specs=[block, block],
-            scratch_shapes=[pltpu.VMEM((width, length), bf16)],
+            out_specs=[block, block, pl.BlockSpec((4, width), lambda j, c: (0, 0))],
         ),
-        out_shape=[out, out],
+        out_shape=[out, out, jax.ShapeDtypeStruct((4, width), f32)],
         cost_estimate=COVER,
         name="column_grad",
-    )(jnp.concatenate([core, jnp.full((1,), second, jnp.int32)]), a, b)
-
-
-def vector_grad_kernel(core_ref, timing_ref, parts_ref, sums_ref, _, __, send_ref, keep_ref):
-    sp, half, width = send_ref.shape
-    parts = parts_ref.shape[0] // 2
-    count = timing_ref.shape[0] // sp
-    filled = parts * count
-    rest = half - filled - sums_ref.shape[2]
-    for ref, side in ((send_ref, 1 - core_ref[0]), (keep_ref, core_ref[0])):
-        for s in range(sp):
-            for p in range(parts):
-                part = jnp.where(side == 0, parts_ref[p : p + 1, :], parts_ref[parts + p : parts + p + 1, :])
-                column = timing_ref[s * count : (s + 1) * count, :]
-                ref[s, p * count : (p + 1) * count] = (column * part).astype(bf16)
-            ref[s, filled : filled + sums_ref.shape[2]] = jnp.where(
-                side == 0, sums_ref[0, s], sums_ref[1, s]
-            ).astype(bf16)
-            if rest:
-                ref[s, half - rest : half] = jnp.zeros((rest, width), bf16)
-
-
-def vector_grad(core, timing, parts, sums, send, keep, rows):
-    sp, total, width = send.shape
-    block = pl.BlockSpec((sp, rows, width), lambda i, c: (0, total // rows - 1, 0))
-    return pl.pallas_call(
-        vector_grad_kernel,
-        grid_spec=pltpu.PrefetchScalarGridSpec(
-            num_scalar_prefetch=1,
-            grid=(1,),
-            in_specs=[
-                pl.BlockSpec(timing.shape, lambda i, c: (0, 0)),
-                pl.BlockSpec(parts.shape, lambda i, c: (0, 0)),
-                pl.BlockSpec(sums.shape, lambda i, c: (0, 0, 0, 0)),
-                pl.BlockSpec(memory_space=pl.ANY),
-                pl.BlockSpec(memory_space=pl.ANY),
-            ],
-            out_specs=[block, block],
-        ),
-        out_shape=[jax.ShapeDtypeStruct(send.shape, bf16)] * 2,
-        input_output_aliases={4: 0, 5: 1},
-        cost_estimate=COVER,
-        name="vector_grad",
-    )(core, timing, parts, sums, send, keep)
+    )(core, sums, up_sum, mods, timing, a, b)
 
 
 def shift_permute(value, axis, by):
@@ -510,10 +547,6 @@
 
 def after(values, *others):
     return lax.optimization_barrier((values, others))[0]
-
-
-VMEM = pl.BlockSpec(memory_space=pltpu.VMEM)
-SMEM = pl.BlockSpec(memory_space=pltpu.SMEM)
 
 
 def bit_of(index, bit):
@@ -743,78 +776,43 @@
     )(core, mine, other)
 
 
-def late_row_kernel(sums_ref, parts_ref, mod_ref, ada_ref, timing_ref, row_ref):
-    width = sums_ref.shape[1]
-    cond = timing_ref.shape[1]
-    shift, scaled = sums_ref[0:1, :], sums_ref[1:2, :]
-    scale = scaled * mod_ref[0:1, :]
-    row = jnp.concatenate([shift, scale] + [parts_ref[i : i + 1, :] for i in range(4)], axis=1)
-    high = row.astype(bf16)
-    low = (row - high.astype(f32)).astype(bf16)
-    time = dot_nt(high, ada_ref[...]) + dot_nt(low, ada_ref[...])
-    row_ref[:, :width] = shift.astype(bf16)
-    row_ref[:, width : 2 * width] = scale.astype(bf16)
-    row_ref[:, 2 * width : 3 * width] = (scaled * mod_ref[1:2, :]).astype(bf16)
-    row_ref[:, 3 * width : 3 * width + cond] = time.astype(bf16)
-    row_ref[:, 3 * width + cond :] = timing_ref[...]
-
-
-def late_row(sums, parts, mods, ada, timing):
-    columns = 3 * sums.shape[1] + 2 * timing.shape[1]
-    return pl.pallas_call(
-        late_row_kernel,
-        in_specs=[VMEM] * 5,
-        out_specs=VMEM,
-        out_shape=jax.ShapeDtypeStruct((1, columns), bf16),
-        cost_estimate=COVER,
-        name="late_row",
-    )(sums, parts, mods, ada, timing)
-
-
 def vector_outputs_kernel(
-    at_ref, rows_ref, vector_ref, ada_ref, bias_ref, attn_gain_ref, mlp_gain_ref, up_ref, down_ref,
-    grad_ref, *, half, sp,
+    early_ref, late_ref, ada_ref, bias_ref, attn_gain_ref, mlp_gain_ref, up_ref, down_ref, *, half
 ):
-    count, width = ada_ref.shape[0], vector_ref.shape[1]
-    quarter = width // sp
-    me = at_ref[2]
-    grad_ref[...] = dot_tn(
-        rows_ref[:, 3 * width + grad_ref.shape[0] :], rows_ref[:, : 2 * width]
-    ).reshape(grad_ref.shape)
-    ada_ref[:, : 2 * width] = grad_ref[pl.ds(pl.multiple_of(me * count, count), count), :]
+    count, width = ada_ref.shape[0], early_ref.shape[1]
+    quarter, own = attn_gain_ref.shape[1], bias_ref.size
+    for p in range(2):
+        ada_ref[:, p * width : (p + 1) * width] = late_ref[p * half : p * half + count, :]
     for p in range(4):
         start = p // 2 * half + p % 2 * count
-        ada_ref[:, (2 + p) * width : (3 + p) * width] = vector_ref[start : start + count, :]
-    totals = column_sum(rows_ref[:, : 3 * width].astype(f32))
-    row = 2 * count
-    own = bias_ref.shape[1]
-    late_bias = jnp.concatenate([totals[:, : 2 * width], jnp.zeros((1, 4 * width), f32)], axis=1)
-    bias, gain = late_bias[:, :own], totals[:, 2 * width : 2 * width + quarter]
-    for s in range(1, sp):
-        bias = jnp.where(me == s, late_bias[:, s * own : (s + 1) * own], bias)
-        at = 2 * width + s * quarter
-        gain = jnp.where(me == s, totals[:, at : at + quarter], gain)
-    bias_ref[:, :width] = bias[:, :width] + vector_ref[row + 1 : row + 2, :]
-    bias_ref[:, width:] = bias[:, width:] + vector_ref[half + row + 1 : half + row + 2, : own - width]
-    attn_gain_ref[...] = gain
-    up_ref[...] = vector_ref[row : row + 1, :]
-    mlp_gain_ref[...] = vector_ref[half + row : half + row + 1, :quarter]
-    down_ref[...] = vector_ref[half + row : half + row + 1, quarter : 2 * quarter]
-
-
-def vector_outputs(at, rows, vectors, half, cond, sp):
-    width = vectors.shape[1]
+        ada_ref[:, (2 + p) * width : (3 + p) * width] = early_ref[start : start + count, :]
+    row, low = 2 * count, half + count
+    rest = own - width
+    attn_gain_ref[...] = late_ref[low : low + 1, rest : rest + quarter]
+    for lane in range(0, own, LANES):
+        i, cols = lane // LANES, slice(lane % width, lane % width + LANES)
+        a, b = (row + 1, count) if lane < width else (half + row + 1, low)
+        bias_ref[i : i + 1, :] = early_ref[a : a + 1, cols] + late_ref[b : b + 1, cols]
+    for lane in range(0, width, LANES):
+        i = lane // LANES
+        up_ref[i : i + 1, :] = early_ref[row : row + 1, lane : lane + LANES]
+    mlp_gain_ref[...] = early_ref[half + row : half + row + 1, :quarter]
+    down_ref[...] = early_ref[half + row : half + row + 1, quarter : 2 * quarter]
+
+
+def vector_outputs(early, late, half, cond, sp):
+    width = early.shape[1]
     quarter = width // sp
-    shapes = [(cond // sp, 6 * width), (1, 6 * width // sp), (1, quarter), (1, quarter), (1, width), (1, quarter)]
-    return pl.pallas_call(
-        functools.partial(vector_outputs_kernel, half=half, sp=sp),
-        in_specs=[SMEM] + [VMEM] * 2,
+    one = (1, quarter)
+    shapes = [(cond // sp, 6 * width), (6 * width // sp // LANES, LANES), one, one, (width // LANES, LANES), one]
+    return pl.pallas_call(
+        functools.partial(vector_outputs_kernel, half=half),
+        in_specs=[VMEM] * 2,
         out_specs=[VMEM] * 6,
         out_shape=[jax.ShapeDtypeStruct(s, f32) for s in shapes],
-        scratch_shapes=[pltpu.VMEM((cond, 2 * width), f32)],
         cost_estimate=COVER,
         name="vector_outputs",
-    )(at, rows, vectors)
+    )(early, late)
 
 
 def sum_over_rest(total):
@@ -880,6 +878,12 @@
         + [zero] * 3,
         axis=0,
     )
+    late_mods = jnp.concatenate([attn_mods[:2], gain_attn, 1.0 + scale_attn] + [zero] * 4, axis=0)
+    mlp_grad_mods = jnp.concatenate([gain_mlp, 1.0 + scale_mlp] + [zero] * 6, axis=0)
+    column = timing.astype(f32).reshape(timing.shape[1], 1)
+    attn_mods, mlp_mods, late_mods, mlp_grad_mods, column, at, core = lax.optimization_barrier(
+        (attn_mods, mlp_mods, late_mods, mlp_grad_mods, column, at, core)
+    )
     lane = lax.broadcasted_iota(jnp.int32, (1, LANES), 1)
     frequency = 10000.0 ** (-((lane % HALF).astype(f32) * 2.0 / HEAD_DIM))
     row = lax.broadcasted_iota(jnp.int32, (sp * local_len, 1), 0)
@@ -905,36 +909,10 @@
     half = width // sp // 2
     quarter = width // sp
     cond = timing.shape[1]
-    column = timing.astype(f32).reshape(cond, 1)
-
-    def shards(row):
-        return row.reshape(sp, -1)
-
-    def sum_rows(rows):
-        filled = [
-            jnp.stack([jnp.pad(r, ((0, 0), (0, width - r.shape[1]))) for r in side], axis=1)
-            for side in rows
-        ]
-        return jnp.stack([jnp.pad(f, ((0, 0), (0, 16 - f.shape[1]), (0, 0))) for f in filled])
-
     output = exchange(out)
-    col_send, col_keep = column_grad(core, both_in, both_grad, sp, n_up + 2, n_up)
-    early_parts = jnp.concatenate([sums[4:5], sums[2:3], sums[3:4] * gain_mlp, sums[0:1]], axis=0)
-    six = 6 * width
-    early_bias = jnp.concatenate([jnp.zeros((2 * width,), f32), early_parts.reshape(-1)])
-    early_bias = shards(early_bias)
-    early_sums = sum_rows(
-        [
-            [shards(up_sum), early_bias[:, :width]],
-            [
-                jnp.concatenate(
-                    [shards(sums[3:4] * (1.0 + scale_mlp)), shards(sums[1:2])], axis=1
-                ),
-                early_bias[:, width:],
-            ],
-        ]
-    )
-    col_send, col_keep = vector_grad(core, column, early_parts, early_sums, col_send, col_keep, half)
+    col_send, col_keep, early_parts = column_grad(
+        core, sums, up_sum, mlp_grad_mods, column, both_in, both_grad, sp, n_up
+    )
     col_got = pair_permute(col_send, CORE)
     row_send, row_keep = row_grad(core, *after((act, gd), col_keep), sp)
     row_got = pair_permute(row_send, CORE)
@@ -955,11 +933,11 @@
     left_got, right_got = pair_permute(left_send, SECOND), pair_permute(right_send, FIRST)
     grads = after(grads, left, right, output)
 
-    attn_sums, hg, late_send, late_keep = late_grads(
-        core, x, grads, gm, attn_mods, query_key_value_matrix, xm_attn, sp, local_len
+    time_row, hg, late_send, late_keep = late_grads(
+        core, x, grads, gm, late_mods, query_key_value_matrix, xm_attn, ada_weight, column, early_parts,
+        sp, local_len,
     )
     hidden_grad = exchange(hg)
-    row_mods = jnp.concatenate([gain_attn, 1.0 + scale_attn] + [zero] * 6, axis=0)
     late_got = pair_permute(late_send, CORE)
     left_got, right_got = after((left_got, right_got), late_keep)
     if lax.axis_size("dp") > 2 * SECOND:
@@ -969,17 +947,15 @@
         sides = [(left, left_got), (right, right_got)]
     near_send, near = near_halves(at, sides)
     near_got = pair_permute(near_send, 1, "sp")
-    rows = late_row(after(attn_sums, near), early_parts, row_mods, ada_weight, timing)
-    late_got = after(late_got, rows)
+    late_got = after(late_got, near)
     own_quarter, *other_quarters = quarters(at, late_keep, late_got)
     quarter_parts = [own_quarter] + [
         pair_permute(p, bit)
         for p, bit in zip(other_quarters, (SECOND, FIRST, FIRST + SECOND))
     ]
-    rows = after(rows, own_quarter)
-    for bit in bits("dp"):
-        rows = double(rows, bit, "dp")
-    near_got, hidden_grad = after((near_got, hidden_grad), rows)
+    output = hand_over(after(output, own_quarter))
+    near_got, hidden_grad, quarter_parts = after((near_got, hidden_grad, quarter_parts), output)
+    near_got = after(near_got, quarter_parts)
     far_send, far = far_halves(at, near, after(near_got, hidden_grad))
     far_got = pair_permute(far_send, 2, "sp")
     quarter_parts = after(quarter_parts, far)
@@ -988,25 +964,24 @@
         quarter_parts = [sum_over_rest(total)]
     late_near_send, late_near = near_halves(at, [quarter_parts])
     late_near_got = pair_permute(late_near_send, 1, "sp")
-    rows = double(after(rows, late_near), 1, "sp")
-    output = hand_over(after(output, late_near))
-    late_near_got = after(late_near_got, rows, output)
     late_far_send, late_far = far_halves(at, late_near, late_near_got)
     late_far_got = pair_permute(late_far_send, 2, "sp")
     early_own = own_sum(far, after(far_got, late_far))
     early_four = spread(early_own)
-    rows = double(after(rows, early_own), 2, "sp")
-    late_own = own_sum(late_far, after(late_far_got, rows))
-    hidden_grad = widen(after(hidden_grad, late_own))
-    early_half = four_chips(at, after(early_four, hidden_grad), True)
+    late_own = own_sum(late_far, after(late_far_got, early_own))
+    hidden_grad = after(hidden_grad, late_own).astype(f32)
+    time_rows = after(time_row, late_own)
+    for bit in bits("sp"):
+        time_rows = double(time_rows, bit, "sp")
+    time_grad = jnp.concatenate([pick(time_rows, me ^ s)[None] for s in range(sp)], axis=0)
+    time_grad = time_grad.astype(f32)
+    early_half = four_chips(at, after(early_four, late_own, time_rows, hidden_grad), True)
     early_other = pair_permute(early_half, CORE)
     late_four = spread(after(late_own, early_half))
-    time_rows = rows[:: lax.axis_size("dp"), 3 * width : 3 * width + cond]
-    time_grad = jnp.concatenate([pick(time_rows, me ^ s)[None] for s in range(sp)], axis=0)
     n_row, n_col = row_keep.shape[1] // 2, col_keep.shape[1] // 2
     row_starts = [x * (n_row + n_col) + i for x in range(2) for i in range(0, n_row, half)]
     col_starts = [x * (n_row + n_col) + n_row + i for x in range(2) for i in range(0, n_col, half)]
-    down_grad, up_grad, proj_grad, vectors = finish(
+    down_grad, up_grad, proj_grad, early_vectors = finish(
         core,
         early_half,
         after(early_other, late_four[0]),
@@ -1020,14 +995,13 @@
     )
     late_half = four_chips(at, after(late_four, down_grad), False)
     late_other = pair_permute(late_half, CORE)
-    ada_weight_grad, *small = vector_outputs(at, after(rows, late_half), vectors, half, cond, sp)
-    (qkv_grad,) = finish(
-        core, late_half, after(late_other, ada_weight_grad), half, ((1, 3, [0, half, 2 * half]),)
-    )
+    qkv_grad, late_vectors = finish(
+        core, late_half, late_other, half, ((1, 3, [0, half, 2 * half]), (1, 1, [3 * half]))
+    )
+    ada_weight_grad, *small = vector_outputs(early_vectors, late_vectors, half, cond, sp)
     ada_bias_grad, attn_gain_grad, mlp_gain_grad, up_bias_grad, down_bias_grad = (
         v.reshape(-1) for v in small
     )
-    time_grad = time_grad.astype(f32)
     return (
         output,
         hidden_grad,

time: 353 us -> 339 us (0.960)
  Pallas kernels: 196 us -> 185 us
  other arithmetic: 12.1 us -> 7.5 us
    pallas_call x7 -> x5, Pallas kernels: 67.8 us -> 59.7 us  [the longest x1 19.5 us: attention_forward(): pl.pallas_call(functools.partial(attention_forward_kernel, chunk=length /...]
    pallas_call x3 -> x0, other arithmetic: 3.97 us -> none  [the longest x2 2.59 us: vector_outputs(): pl.pallas_call(functools.partial(vector_outputs_kernel, half=half, sp=sp)...]
    pallas_call x2 -> x1, Pallas kernels: 7.44 us -> 3.56 us  [hand_over(): pl.pallas_call(hand_over_kernel, grid=(value.shape[0],), in_specs=[block]...]
    ppermute x27 -> x24, starting transfers between devices: 24.9 us -> 27.7 us  [pair_permute(): return lax.ppermute(value, axis, [(i, i ^ bit) for i in range(n)])]
    ppermute x27 -> x24, waiting for transfers between devices: 48.8 us -> 46.4 us  [pair_permute(): return lax.ppermute(value, axis, [(i, i ^ bit) for i in range(n)])]
    unnamed x70 -> x64, local copies, waits for them, and re-layouts: 12 us -> 11.7 us
  transfers between devices with their start and end apart: 31 -> 28, of which waited for: 10 -> 10; matrix products, arithmetic and copies ran while one was open for 3% -> 3% of each run, Pallas kernels for 37% -> 35%
where the time goes in v1:
time: 339 us; the launch traced here: 338 us
  Pallas kernels  185 us (55%)
  waiting for transfers between devices  84.2 us (25%)
  starting transfers between devices  45.4 us (13%)
  local copies, waits for them, and re-layouts  13.8 us (4%)
  other arithmetic  7.5 us (2%)
    ppermute x24, waiting for transfers between devices, pair_permute(): return lax.ppermute(value, axis, [(i, i ^ bit) for i in range(n)])  46.4 us
    all_to_all x4, waiting for transfers between devices, exchange(): return lax.all_to_all(values, 'sp', split_axis=0, concat_axis=0, tiled=True)  37.7 us
    pallas_call x1, Pallas kernels, feed_forward(): pl.pallas_call(mlp_kernel, grid=(length // rows,), in_specs=[block, block...  36 us
    pallas_call x1, Pallas kernels, attention_backward(): pl.pallas_call(attention_backward_kernel, grid=(count,), in_specs=[block]...  34.3 us
    ppermute x24, starting transfers between devices, pair_permute(): return lax.ppermute(value, axis, [(i, i ^ bit) for i in range(n)])  27.7 us
    pallas_call x1, Pallas kernels, attention_forward(): pl.pallas_call(functools.partial(attention_forward_kernel, chunk=length /...  19.5 us
    all_to_all x4, starting transfers between devices, exchange(): return lax.all_to_all(values, 'sp', split_axis=0, concat_axis=0, tiled=True)  17.7 us
    pallas_call x1, Pallas kernels, late_grads(): pl.pallas_call(functools.partial(late_grads_kernel, tiles=tiles, parts=n)...  17.4 us
  transfers between devices with their start and end apart: 28, of which 10 were waited for; matrix products, arithmetic and copies ran while one was open for 3% of the time, Pallas kernels for 35%

profile of v1, /device:TPU:0, one launch (start us, length us, event | category | flops | bytes accessed | tf_op | source)
XLA Modules:
  0.0 337.7 jit_solution(10806198213475287707)
XLA Ops:
  0.7 6.5 %all-to-all-start = ((bf16[4,256,768]{2,1,0:T(8,128)(2,1)}), bf16[4,256,768]{2,1,0:T(8,128)(2,1)S(1)}, u32[]{:S(2)}, u32[]{:S(2)}) async-start(bf16[4,256,768]{2,1,0:T(8,128)(2,1)} %param.13), calls=%async_computation | async-start | bytes 3145728 | tf_op jit(solution)/shard_map/all_to_all | solution.py:857
  11.6 3.1 multiply_sine_fusion
  14.7 29.5 %all-to-all-done = bf16[4,256,768]{2,1,0:T(8,128)(2,1)S(1)} async-done(((bf16[4,256,768]{2,1,0:T(8,128)(2,1)}), bf16[4,256,768]{2,1,0:T(8,128)(2,1)S(1)}, u32[]{:S(2)}, u32[]{:S(2)}) %all-to-all-start) | async-done | bytes 1572896 | tf_op jit(solution)/shard_map/all_to_all | solution.py:857
  45.3 3.6 %all-to-all-start.1 = ((bf16[4,256,768]{2,1,0:T(8,128)(2,1)}), bf16[4,256,768]{2,1,0:T(8,128)(2,1)S(1)}, u32[]{:S(2)}, u32[]{:S(2)}) async-start(bf16[4,256,768]{2,1,0:T(8,128)(2,1)} %param.25), calls=%async_computation.1 | async-start | bytes 3145728 | tf_op jit(solution)/shard_map/all_to_all | solution.py:857
  48.8 8.7 %project_qkv.1 = (bf16[1024,768]{1,0:T(8,128)(2,1)}, bf16[1024,768]{1,0:T(8,128)(2,1)}, bf16[1024,768]{1,0:T(8,128)(2,1)}, bf16[1024,768]{1,0:T(8,128)(2,1)}) custom-call(bf16[1024,768]{1,0:T(8,128)(2,1)} %bitcast.31, f32[8,768]{1,0:T(8,128)} %get-tuple-element.116.mod_ref, bf16[768,2304]{1,0:T(8,128)(2,1)} %w_ref.3, ...), custom_call_target="tpu_custom_call" | custom-call | flops 40000000000 | bytes 100000000 | tf_op jit(solution)/shard_map/project_qkv/pallas_call | solution.py:90
  57.5 19.5 %attention_forward.1 = (bf16[1024,768]{1,0:T(8,128)(2,1)}, f32[6,2,1024]{2,1,0:T(2,128)}) custom-call(bf16[1024,768]{1,0:T(8,128)(2,1)} %get-tuple-element.117.q_ref, bf16[1024,768]{1,0:T(8,128)(2,1)} %get-tuple-element.118.k_ref, bf16[1024,768]{1,0:T(8,128)(2,1)} %get-tuple-element.119.v_ref), custom_call_target="tpu_custom_call" | custom-call | flops 40000000000 | bytes 100000000 | tf_op jit(solution)/shard_map/attention_forward/pallas_call | solution.py:141
  77.0 8.3 %all-to-all-done.1 = bf16[4,256,768]{2,1,0:T(8,128)(2,1)S(1)} async-done(((bf16[4,256,768]{2,1,0:T(8,128)(2,1)}), bf16[4,256,768]{2,1,0:T(8,128)(2,1)S(1)}, u32[]{:S(2)}, u32[]{:S(2)}) %all-to-all-start.1) | async-done | bytes 1572896 | tf_op jit(solution)/shard_map/all_to_all | solution.py:857
  86.4 36.0 %feed_forward.1 = (bf16[2,1024,768]{2,1,0:T(8,128)(2,1)}, bf16[1024,3072]{1,0:T(8,128)(2,1)}, bf16[1024,768]{1,0:T(8,128)(2,1)}, bf16[5,1024,768]{2,1,0:T(8,128)...) custom-call(bf16[1024,768]{1,0:T(8,128)(2,1)} %bitcast.32, ...), custom_call_target="tpu_custom_call" | custom-call | flops 40000000000 | bytes 100000000 | tf_op jit(solution)/shard_map/feed_forward/pallas_call | solution.py:279
  122.5 12.0 %column_grad.1 = (bf16[4,576,768]{2,1,0:T(8,128)(2,1)}, bf16[4,576,768]{2,1,0:T(8,128)(2,1)}, f32[4,768]{1,0:T(4,128)}) custom-call(s32[1]{0:T(128)} %bitcast.6.core_ref, f32[8,768]{1,0:T(8,128)} %get-tuple-element.125.sum_ref, f32[1,3072]{1,0:T(1,128)} %get-tuple-element.126.up_sum_ref, f32[8,768]{1,0:T(8,128)} %get-tuple-element.127.mod_ref, ...), custom_call_target="tpu_custom_call" | custom-call | flops 40000000000 | bytes 100000000 | tf_op jit(solution)/shard_map/column_grad/pallas_call | solution.py:516
  134.5 9.2 %row_grad.1 = (bf16[4,384,768]{2,1,0:T(8,128)(2,1)}, bf16[4,384,768]{2,1,0:T(8,128)(2,1)}) custom-call(s32[1]{0:T(128)} %bitcast.6.core_ref, bf16[1024,3072]{1,0:T(8,128)(2,1)} %get-tuple-element.132.a_ref, bf16[1024,768]{1,0:T(8,128)(2,1)} %get-tuple-element.133.b_ref), custom_call_target="tpu_custom_call" | custom-call | flops 40000000000 | bytes 100000000 | tf_op jit(solution)/shard_map/row_grad/pallas_call | solution.py:448
  144.2 3.6 %all-to-all-start.2 = ((bf16[4,256,768]{2,1,0:T(8,128)(2,1)}), bf16[4,256,768]{2,1,0:T(8,128)(2,1)S(1)}, u32[]{:S(2)}, u32[]{:S(2)}) async-start(bf16[4,256,768]{2,1,0:T(8,128)(2,1)} %bitcast.10), calls=%async_computation.2 | async-start | bytes 3145728 | tf_op jit(solution)/shard_map/all_to_all | solution.py:857
  148.7 7.8 %first_halves.1 = (bf16[4,480,384]{2,1,0:T(8,128)(2,1)}, bf16[4,480,384]{2,1,0:T(8,128)(2,1)}, bf16[4,480,384]{2,1,0:T(8,128)(2,1)}, bf16[4,480,384]{2,1,0:T(8,128)(2,1)}) custom-call(s32[3]{0:T(128)} %pad_add_fusion.at_ref, bf16[4,384,768]{2,1,0:T(8,128)(2,1)} %get-tuple-element.134.row_keep, bf16[4,384,768]{2,1,0:T(8,128)(2,1)} %collective-permute-done.row_got, ...), custom_call_target="tpu_custom_call" | custom-call | flops 40000000000 | bytes 100000000 | tf_op jit(solution)/shard_map/first_halves/pallas_call | solution.py:586
  159.6 34.3 %attention_backward.1.tile_ref.block_ref = bf16[3,1024,768]{2,1,0:T(8,128)(2,1)} custom-call(bf16[1024,768]{1,0:T(8,128)(2,1)} %get-tuple-element.117.q_ref, bf16[1024,768]{1,0:T(8,128)(2,1)} %get-tuple-element.118.k_ref, bf16[1024,768]{1,0:T(8,128)(2,1)} %get-tuple-element.119.v_ref, bf16[1024,768]{1,0:T(8,128)(2,1)} %get-tuple-element.143.do_ref, ...), custom_call_target="tpu_custom_call" | custom-call | flops 40000000000 | bytes 100000000 | tf_op jit(solution)/shard_map/attention_backward/pallas_call | solution.py:189
  195.1 4.6 %second_halves.1 = (bf16[4,240,384]{2,1,0:T(8,128)(2,1)}, bf16[4,240,384]{2,1,0:T(8,128)(2,1)}, bf16[4,240,384]{2,1,0:T(8,128)(2,1)}, bf16[4,240,384]{2,1,0:T(8,128)(2,1)}) custom-call(s32[3]{0:T(128)} %pad_add_fusion.at_ref, bf16[4,2,240,384]{3,2,1,0:T(8,128)(2,1)} %bitcast.43, bf16[4,2,240,384]{3,2,1,0:T(8,128)(2,1)} %bitcast.37, ...), custom_call_target="tpu_custom_call" | custom-call | flops 40000000000 | bytes 100000000 | tf_op jit(solution)/shard_map/second_halves/pallas_call | solution.py:612
  200.6 17.4 %late_grads.1 = (bf16[1,128]{1,0:T(2,128)(2,1)}, bf16[1024,768]{1,0:T(8,128)(2,1)}, bf16[4,384,768]{2,1,0:T(8,128)(2,1)}, bf16[4,384,768]{2,1,0:T(8,128)(2,1)}) custom-call(s32[1]{0:T(128)} %bitcast.6.core_ref, bf16[1024,768]{1,0:T(8,128)(2,1)} %bitcast.33, bf16[3,1024,768]{2,1,0:T(8,128)(2,1)} %attention_backward.1.tile_ref.block_ref, ...), custom_call_target="tpu_custom_call" | custom-call | flops 40000000000 | bytes 100000000 | tf_op jit(solution)/shard_map/late_grads/pallas_call | solution.py:397
  218.1 4.1 %all-to-all-start.3 = ((bf16[4,256,768]{2,1,0:T(8,128)(2,1)}), bf16[4,256,768]{2,1,0:T(8,128)(2,1)S(1)}, u32[]{:S(2)}, u32[]{:S(2)}) async-start(bf16[4,256,768]{2,1,0:T(8,128)(2,1)} %bitcast.34), calls=%async_computation.3 | async-start | bytes 3145728 | tf_op jit(solution)/shard_map/all_to_all | solution.py:857
  223.3 3.1 near_halves.2
  226.4 2.0 collective-permute-start.7
  228.5 4.3 %quarters.1 = (bf16[4,96,768]{2,1,0:T(8,128)(2,1)}, bf16[4,96,768]{2,1,0:T(8,128)(2,1)}, bf16[4,96,768]{2,1,0:T(8,128)(2,1)}, bf16[4,96,768]{2,1,0:T(8,128)(2,1)}) custom-call(s32[3]{0:T(128)} %pad_add_fusion.at_ref, bf16[4,4,96,768]{3,2,1,0:T(8,128)(2,1)} %bitcast.42, bf16[4,4,96,768]{3,2,1,0:T(8,128)(2,1)} %bitcast.16.got_ref), custom_call_target="tpu_custom_call" | custom-call | flops 40000000000 | bytes 100000000 | tf_op jit(solution)/shard_map/quarters/pallas_call | solution.py:717
  232.8 2.5 collective-permute-start.10
  236.3 3.6 %hand_over.1 = bf16[4,256,768]{2,1,0:T(8,128)(2,1)} custom-call(bf16[4,256,768]{2,1,0:T(8,128)(2,1)} %copy-done.3), custom_call_target="tpu_custom_call" | custom-call | flops 40000000000 | bytes 100000000 | tf_op jit(solution)/shard_map/hand_over/pallas_call | solution.py:681
  239.8 26.5 %collective-permute-done.7.got = bf16[2,240,768]{2,1,0:T(8,128)(2,1)S(1)} collective-permute-done((bf16[2,240,768]{2,1,0:T(8,128)(2,1)}, bf16[2,240,768]{2,1,0:T(8,128)(2,1)S(1)}, u32[]{:S(2)}, u32[]{:S(2)}) %collective-permute-start.7) | collective-permute-done | bytes 737312 | tf_op jit(solution)/shard_map/ppermute | solution.py:541
  267.2 2.7 far_halves.2
  269.8 2.7 near_halves.3
  272.9 2.6 collective-permute-start.13
  275.5 12.8 %collective-permute-done.11.got = bf16[2,96,768]{2,1,0:T(8,128)(2,1)S(1)} collective-permute-done((bf16[2,96,768]{2,1,0:T(8,128)(2,1)}, bf16[2,96,768]{2,1,0:T(8,128)(2,1)S(1)}, u32[]{:S(2)}, u32[]{:S(2)}) %collective-permute-start.11) | collective-permute-done | bytes 294944 | tf_op jit(solution)/shard_map/ppermute | solution.py:541
  301.1 4.2 %collective-permute-start.14 = (bf16[1,128]{1,0:T(2,128)(2,1)S(1)}, bf16[1,128]{1,0:T(2,128)(2,1)S(1)}, u32[]{:S(2)}, u32[]{:S(2)}) collective-permute-start(bf16[1,128]{1,0:T(2,128)(2,1)S(1)} %copy-done.11), channel_id=1, source_target_pairs={{0,1},{1,0},{2,3},{3,2},{4,5},{5,4},{6,7},{7,6},{8,9},{9,8},{10,11... | collective-permute-start | bytes 776 | tf_op jit(solution)/shard_map/ppermute | solution.py:541
  306.9 3.4 %collective-permute-start.15 = (bf16[2,128]{1,0:T(2,128)(2,1)S(1)}, bf16[2,128]{1,0:T(2,128)(2,1)S(1)}, u32[]{:S(2)}, u32[]{:S(2)}) collective-permute-start(bf16[2,128]{1,0:T(2,128)(2,1)S(1)} %pad_maximum_fusion.1), channel_id=1, source_target_pairs={{0,2},{1,3},{2,0},{3,1},{4,6},{5,7},{6,4},{7,5},{8,10},{9,11},{10,... | collective-permute-start | bytes 1544 | tf_op jit(solution)/shard_map/ppermute | solution.py:541
  313.9 2.6 four_chips.2
  321.2 4.6 %finish.2 = (f32[768,768]{1,0:T(8,128)}, f32[192,3072]{1,0:T(8,128)}, f32[192,768]{1,0:T(8,128)}, f32[192,768]{1,0:T(8,128)}) custom-call(s32[1]{0:T(128)} %bitcast.6.core_ref, bf16[960,768]{1,0:T(8,128)(2,1)} %bitcast.39, bf16[960,768]{1,0:T(8,128)(2,1)} %copy-done.14), custom_call_target="tpu_custom_call" | custom-call | flops 40000000000 | bytes 100000000 | tf_op jit(solution)/shard_map/finish/pallas_call | solution.py:768
  332.8 2.8 finish.3
  335.6 2.1 vector_outputs.1
  (136 shorter events, 46.1 us)
Async XLA Ops:
  0.7 6.8 %copy-start.7 = (bf16[768]{0:T(1024)(128)(2,1)S(1)}, bf16[768]{0:T(1024)(128)(2,1)}, u32[]{:S(2)}) copy-start(bf16[768]{0:T(1024)(128)(2,1)} %param.20) | copy-start | bytes 4612
  0.7 6.9 %copy-start.8 = (bf16[768]{0:T(1024)(128)(2,1)S(1)}, bf16[768]{0:T(1024)(128)(2,1)}, u32[]{:S(2)}) copy-start(bf16[768]{0:T(1024)(128)(2,1)} %param.17) | copy-start | bytes 4612
  0.7 43.4 %all-to-all-start = ((bf16[4,256,768]{2,1,0:T(8,128)(2,1)}), bf16[4,256,768]{2,1,0:T(8,128)(2,1)S(1)}, u32[]{:S(2)}, u32[]{:S(2)}) async-start(bf16[4,256,768]{2,1,0:T(8,128)(2,1)} %param.13), calls=%async_computation | async-start | bytes 3145728 | tf_op jit(solution)/shard_map/all_to_all | solution.py:857
  45.3 40.0 %all-to-all-start.1 = ((bf16[4,256,768]{2,1,0:T(8,128)(2,1)}), bf16[4,256,768]{2,1,0:T(8,128)(2,1)S(1)}, u32[]{:S(2)}, u32[]{:S(2)}) async-start(bf16[4,256,768]{2,1,0:T(8,128)(2,1)} %param.25), calls=%async_computation.1 | async-start | bytes 3145728 | tf_op jit(solution)/shard_map/all_to_all | solution.py:857
  134.5 14.2 %collective-permute-start.1 = (bf16[4,576,768]{2,1,0:T(8,128)(2,1)}, bf16[4,576,768]{2,1,0:T(8,128)(2,1)}, u32[]{:S(2)}, u32[]{:S(2)}) collective-permute-start(bf16[4,576,768]{2,1,0:T(8,128)(2,1)} %get-tuple-element.136), channel_id=1, source_target_pairs={{0,4},{4,0},{8,12},{12,8},{16,20},{20,16},{24,28},{28,24},{1,5},{5... | collective-permute-start | bytes 10616840 | tf_op jit(solution)/shard_map/ppermute | solution.py:541
  143.7 5.0 %collective-permute-start = (bf16[4,384,768]{2,1,0:T(8,128)(2,1)}, bf16[4,384,768]{2,1,0:T(8,128)(2,1)}, u32[]{:S(2)}, u32[]{:S(2)}) collective-permute-start(bf16[4,384,768]{2,1,0:T(8,128)(2,1)} %get-tuple-element.135), channel_id=1, source_target_pairs={{0,4},{4,0},{8,12},{12,8},{16,20},{20,16},{24,28},{28,24},{1,5},{5... | collective-permute-start | bytes 7077896 | tf_op jit(solution)/shard_map/ppermute | solution.py:541
  144.2 49.7 %all-to-all-start.2 = ((bf16[4,256,768]{2,1,0:T(8,128)(2,1)}), bf16[4,256,768]{2,1,0:T(8,128)(2,1)S(1)}, u32[]{:S(2)}, u32[]{:S(2)}) async-start(bf16[4,256,768]{2,1,0:T(8,128)(2,1)} %bitcast.10), calls=%async_computation.2 | async-start | bytes 3145728 | tf_op jit(solution)/shard_map/all_to_all | solution.py:857
  156.5 37.4 %collective-permute-start.2 = (bf16[4,480,384]{2,1,0:T(8,128)(2,1)}, bf16[4,480,384]{2,1,0:T(8,128)(2,1)S(1)}, u32[]{:S(2)}, u32[]{:S(2)}) collective-permute-start(bf16[4,480,384]{2,1,0:T(8,128)(2,1)} %get-tuple-element.137), channel_id=1, source_target_pairs={{0,8},{4,12},{8,0},{12,4},{16,24},{20,28},{24,16},{28,20},{1,9},{5... | collective-permute-start | bytes 4423688 | tf_op jit(solution)/shard_map/ppermute | solution.py:541
  158.0 35.9 %collective-permute-start.3 = (bf16[4,480,384]{2,1,0:T(8,128)(2,1)}, bf16[4,480,384]{2,1,0:T(8,128)(2,1)}, u32[]{:S(2)}, u32[]{:S(2)}) collective-permute-start(bf16[4,480,384]{2,1,0:T(8,128)(2,1)} %get-tuple-element.138), channel_id=1, source_target_pairs={{0,16},{4,20},{8,24},{12,28},{16,0},{20,4},{24,8},{28,12},{1,17},{... | collective-permute-start | bytes 4423688 | tf_op jit(solution)/shard_map/ppermute | solution.py:541
  199.6 22.6 %collective-permute-start.5 = (bf16[4,240,384]{2,1,0:T(8,128)(2,1)}, bf16[4,240,384]{2,1,0:T(8,128)(2,1)S(1)}, u32[]{:S(2)}, u32[]{:S(2)}) collective-permute-start(bf16[4,240,384]{2,1,0:T(8,128)(2,1)} %get-tuple-element.157), channel_id=1, source_target_pairs={{0,16},{4,20},{8,24},{12,28},{16,0},{20,4},{24,8},{28,12},{1,17},{... | collective-permute-start | bytes 2211848 | tf_op jit(solution)/shard_map/ppermute | solution.py:541
  200.1 22.1 %collective-permute-start.6 = (bf16[4,240,384]{2,1,0:T(8,128)(2,1)}, bf16[4,240,384]{2,1,0:T(8,128)(2,1)S(1)}, u32[]{:S(2)}, u32[]{:S(2)}) collective-permute-start(bf16[4,240,384]{2,1,0:T(8,128)(2,1)} %get-tuple-element.158), channel_id=1, source_target_pairs={{0,8},{4,12},{8,0},{12,4},{16,24},{20,28},{24,16},{28,20},{1,9},{5... | collective-permute-start | bytes 2211848 | tf_op jit(solution)/shard_map/ppermute | solution.py:541
  218.0 10.4 %collective-permute-start.4 = (bf16[4,384,768]{2,1,0:T(8,128)(2,1)}, bf16[4,384,768]{2,1,0:T(8,128)(2,1)}, u32[]{:S(2)}, u32[]{:S(2)}) collective-permute-start(bf16[4,384,768]{2,1,0:T(8,128)(2,1)} %get-tuple-element.156), channel_id=1, source_target_pairs={{0,4},{4,0},{8,12},{12,8},{16,20},{20,16},{24,28},{28,24},{1,5},{5... | collective-permute-start | bytes 7077896 | tf_op jit(solution)/shard_map/ppermute | solution.py:541
  218.1 48.2 %all-to-all-start.3 = ((bf16[4,256,768]{2,1,0:T(8,128)(2,1)}), bf16[4,256,768]{2,1,0:T(8,128)(2,1)S(1)}, u32[]{:S(2)}, u32[]{:S(2)}) async-start(bf16[4,256,768]{2,1,0:T(8,128)(2,1)} %bitcast.34), calls=%async_computation.3 | async-start | bytes 3145728 | tf_op jit(solution)/shard_map/all_to_all | solution.py:857
  226.4 39.9 %collective-permute-start.7 = (bf16[2,240,768]{2,1,0:T(8,128)(2,1)}, bf16[2,240,768]{2,1,0:T(8,128)(2,1)S(1)}, u32[]{:S(2)}, u32[]{:S(2)}) collective-permute-start(bf16[2,240,768]{2,1,0:T(8,128)(2,1)} %get-tuple-element.165), channel_id=1, source_target_pairs={{0,1},{1,0},{2,3},{3,2},{4,5},{5,4},{6,7},{7,6},{8,9},{9,8},{10,11... | collective-permute-start | bytes 2211848 | tf_op jit(solution)/shard_map/ppermute | solution.py:541
  232.8 33.5 %collective-permute-start.10 = (bf16[4,96,768]{2,1,0:T(8,128)(2,1)}, bf16[4,96,768]{2,1,0:T(8,128)(2,1)S(1)}, u32[]{:S(2)}, u32[]{:S(2)}) collective-permute-start(bf16[4,96,768]{2,1,0:T(8,128)(2,1)} %get-tuple-element.169), channel_id=1, source_target_pairs={{0,24},{4,28},{8,16},{12,20},{16,8},{20,12},{24,0},{28,4},{1,25},{... | collective-permute-start | bytes 1769480 | tf_op jit(solution)/shard_map/ppermute | solution.py:541
  235.2 31.1 %collective-permute-start.8 = (bf16[4,96,768]{2,1,0:T(8,128)(2,1)}, bf16[4,96,768]{2,1,0:T(8,128)(2,1)S(1)}, u32[]{:S(2)}, u32[]{:S(2)}) collective-permute-start(bf16[4,96,768]{2,1,0:T(8,128)(2,1)} %get-tuple-element.167), channel_id=1, source_target_pairs={{0,16},{4,20},{8,24},{12,28},{16,0},{20,4},{24,8},{28,12},{1,17},{... | collective-permute-start | bytes 1769480 | tf_op jit(solution)/shard_map/ppermute | solution.py:541
  235.7 30.6 %collective-permute-start.9 = (bf16[4,96,768]{2,1,0:T(8,128)(2,1)}, bf16[4,96,768]{2,1,0:T(8,128)(2,1)}, u32[]{:S(2)}, u32[]{:S(2)}) collective-permute-start(bf16[4,96,768]{2,1,0:T(8,128)(2,1)} %get-tuple-element.168), channel_id=1, source_target_pairs={{0,8},{4,12},{8,0},{12,4},{16,24},{20,28},{24,16},{28,20},{1,9},{5... | collective-permute-start | bytes 1769480 | tf_op jit(solution)/shard_map/ppermute | solution.py:541
  272.6 15.7 %collective-permute-start.11 = (bf16[2,96,768]{2,1,0:T(8,128)(2,1)}, bf16[2,96,768]{2,1,0:T(8,128)(2,1)S(1)}, u32[]{:S(2)}, u32[]{:S(2)}) collective-permute-start(bf16[2,96,768]{2,1,0:T(8,128)(2,1)} %get-tuple-element.184), channel_id=1, source_target_pairs={{0,1},{1,0},{2,3},{3,2},{4,5},{5,4},{6,7},{7,6},{8,9},{9,8},{10,11... | collective-permute-start | bytes 884744 | tf_op jit(solution)/shard_map/ppermute | solution.py:541
  272.9 18.8 %collective-permute-start.13 = (bf16[240,768]{1,0:T(8,128)(2,1)S(1)}, bf16[240,768]{1,0:T(8,128)(2,1)S(1)}, u32[]{:S(2)}, u32[]{:S(2)}) collective-permute-start(bf16[240,768]{1,0:T(8,128)(2,1)S(1)} %copy-done.24), channel_id=1, source_target_pairs={{0,2},{1,3},{2,0},{3,1},{4,6},{5,7},{6,4},{7,5},{8,10},{9,11},{10,... | collective-permute-start | bytes 1105928 | tf_op jit(solution)/shard_map/ppermute | solution.py:541
  290.8 8.0 %collective-permute-start.12 = (bf16[96,768]{1,0:T(8,128)(2,1)}, bf16[96,768]{1,0:T(8,128)(2,1)S(1)}, u32[]{:S(2)}, u32[]{:S(2)}) collective-permute-start(bf16[96,768]{1,0:T(8,128)(2,1)} %get-tuple-element.186), channel_id=1, source_target_pairs={{0,2},{1,3},{2,0},{3,1},{4,6},{5,7},{6,4},{7,5},{8,10},{9,11},{10,... | collective-permute-start | bytes 442376 | tf_op jit(solution)/shard_map/ppermute | solution.py:541
  294.3 6.8 %copy-start.11 = (bf16[1,128]{1,0:T(2,128)(2,1)S(1)}, bf16[1,128]{1,0:T(2,128)(2,1)}, u32[]{:S(2)}) copy-start(bf16[1,128]{1,0:T(2,128)(2,1)} %get-tuple-element.192) | copy-start | bytes 772
  294.3 16.0 %copy-start.1 = (bf16[4,256,768]{2,1,0:T(8,128)(2,1)S(1)}, bf16[4,256,768]{2,1,0:T(8,128)(2,1)}, u32[]{:S(2)}) copy-start(bf16[4,256,768]{2,1,0:T(8,128)(2,1)} %copy-done) | copy-start | bytes 4718596
  294.3 18.0 %collective-permute-start.16 = (bf16[240,768]{1,0:T(8,128)(2,1)}, bf16[240,768]{1,0:T(8,128)(2,1)S(1)}, u32[]{:S(2)}, u32[]{:S(2)}) collective-permute-start(bf16[240,768]{1,0:T(8,128)(2,1)} %own_sum.2.refs_0_), channel_id=1, source_target_pairs={{0,16},{4,20},{8,24},{12,28},{16,0},{20,4},{24,8},{28,12},{1,17},{... | collective-permute-start | bytes 1105928 | tf_op jit(solution)/shard_map/ppermute | solution.py:541
  295.8 16.5 %collective-permute-start.17 = (bf16[240,768]{1,0:T(8,128)(2,1)}, bf16[240,768]{1,0:T(8,128)(2,1)S(1)}, u32[]{:S(2)}, u32[]{:S(2)}) collective-permute-start(bf16[240,768]{1,0:T(8,128)(2,1)} %own_sum.2.refs_0_), channel_id=1, source_target_pairs={{0,8},{4,12},{8,0},{12,4},{16,24},{20,28},{24,16},{28,20},{1,9},{5... | collective-permute-start | bytes 1105928 | tf_op jit(solution)/shard_map/ppermute | solution.py:541
  297.3 15.0 %collective-permute-start.18 = (bf16[240,768]{1,0:T(8,128)(2,1)}, bf16[240,768]{1,0:T(8,128)(2,1)S(1)}, u32[]{:S(2)}, u32[]{:S(2)}) collective-permute-start(bf16[240,768]{1,0:T(8,128)(2,1)} %own_sum.2.refs_0_), channel_id=1, source_target_pairs={{0,24},{4,28},{8,16},{12,20},{16,8},{20,12},{24,0},{28,4},{1,25},{... | collective-permute-start | bytes 1105928 | tf_op jit(solution)/shard_map/ppermute | solution.py:541
  301.1 5.7 %collective-permute-start.14 = (bf16[1,128]{1,0:T(2,128)(2,1)S(1)}, bf16[1,128]{1,0:T(2,128)(2,1)S(1)}, u32[]{:S(2)}, u32[]{:S(2)}) collective-permute-start(bf16[1,128]{1,0:T(2,128)(2,1)S(1)} %copy-done.11), channel_id=1, source_target_pairs={{0,1},{1,0},{2,3},{3,2},{4,5},{5,4},{6,7},{7,6},{8,9},{9,8},{10,11... | collective-permute-start | bytes 776 | tf_op jit(solution)/shard_map/ppermute | solution.py:541
  306.9 5.4 %collective-permute-start.15 = (bf16[2,128]{1,0:T(2,128)(2,1)S(1)}, bf16[2,128]{1,0:T(2,128)(2,1)S(1)}, u32[]{:S(2)}, u32[]{:S(2)}) collective-permute-start(bf16[2,128]{1,0:T(2,128)(2,1)S(1)} %pad_maximum_fusion.1), channel_id=1, source_target_pairs={{0,2},{1,3},{2,0},{3,1},{4,6},{5,7},{6,4},{7,5},{8,10},{9,11},{10,... | collective-permute-start | bytes 1544 | tf_op jit(solution)/shard_map/ppermute | solution.py:541
  316.5 3.6 %collective-permute-start.19 = (bf16[960,768]{1,0:T(8,128)(2,1)}, bf16[960,768]{1,0:T(8,128)(2,1)S(1)}, u32[]{:S(2)}, u32[]{:S(2)}) collective-permute-start(bf16[960,768]{1,0:T(8,128)(2,1)} %bitcast.38), channel_id=1, source_target_pairs={{0,4},{4,0},{8,12},{12,8},{16,20},{20,16},{24,28},{28,24},{1,5},{5... | collective-permute-start | bytes 4423688 | tf_op jit(solution)/shard_map/ppermute | solution.py:541
  316.5 9.3 %collective-permute-start.20 = (bf16[96,768]{1,0:T(8,128)(2,1)S(1)}, bf16[96,768]{1,0:T(8,128)(2,1)S(1)}, u32[]{:S(2)}, u32[]{:S(2)}) collective-permute-start(bf16[96,768]{1,0:T(8,128)(2,1)S(1)} %copy-done.27), channel_id=1, source_target_pairs={{0,16},{4,20},{8,24},{12,28},{16,0},{20,4},{24,8},{28,12},{1,17},{... | collective-permute-start | bytes 442376 | tf_op jit(solution)/shard_map/ppermute | solution.py:541
  318.1 7.7 %collective-permute-start.21 = (bf16[96,768]{1,0:T(8,128)(2,1)S(1)}, bf16[96,768]{1,0:T(8,128)(2,1)S(1)}, u32[]{:S(2)}, u32[]{:S(2)}) collective-permute-start(bf16[96,768]{1,0:T(8,128)(2,1)S(1)} %copy-done.27), channel_id=1, source_target_pairs={{0,8},{4,12},{8,0},{12,4},{16,24},{20,28},{24,16},{28,20},{1,9},{5... | collective-permute-start | bytes 442376 | tf_op jit(solution)/shard_map/ppermute | solution.py:541
  319.5 7.5 %collective-permute-start.22 = (bf16[96,768]{1,0:T(8,128)(2,1)S(1)}, bf16[96,768]{1,0:T(8,128)(2,1)S(1)}, u32[]{:S(2)}, u32[]{:S(2)}) collective-permute-start(bf16[96,768]{1,0:T(8,128)(2,1)S(1)} %copy-done.27), channel_id=1, source_target_pairs={{0,24},{4,28},{8,16},{12,20},{16,8},{20,12},{24,0},{28,4},{1,25},{... | collective-permute-start | bytes 442376 | tf_op jit(solution)/shard_map/ppermute | solution.py:541
  329.7 2.2 collective-permute-start.23
  (28 other events, 69.1 us)

commit v2 on v1

--- a/solution.py
+++ b/solution.py
@@ -153,51 +153,95 @@
 
 
 def attention_backward_kernel(
-    q_ref, k_ref, v_ref, do_ref, o_ref, lse_ref, cos_ref, sin_ref, *rest
+    q_ref, k_ref, v_ref, do_ref, o_ref, lse_ref, cos_ref, sin_ref, x_ref, gm_ref, mod_ref, w_ref,
+    g_ref, hg_ref, sum_ref, held_ref, *, pairs,
 ):
-    g_ref = rest[-1]
-    first = lax.broadcasted_iota(jnp.int32, (1, LANES), 1) < HEAD_DIM
-    upper = lax.broadcasted_iota(jnp.int32, (LANES, 1), 0) < HEAD_DIM
-    c = LOG2E * SCALE
-    q, k, v, do = q_ref[...], k_ref[...], v_ref[...], do_ref[...]
-    prod = (do.astype(f32) * o_ref[...].astype(f32)).T
-    kt = k.T
-    zero = jnp.zeros_like(k)
-    dq = dk = dv = None
-    for h in range(2):
-        mine = first if h == 0 else ~first
-        row = column_sum(prod[h * HEAD_DIM : (h + 1) * HEAD_DIM])
-        st = dot_nt(jnp.where(mine, k, zero), q)
-        p = jnp.exp2(st * c - lse_ref[0, h : h + 1, :])
-        dp = dot_nt(jnp.where(mine, v, zero), do)
-        ds = (p * (dp - row)).astype(bf16)
-        dvh = dot_nn(p.astype(bf16), jnp.where(mine, do, zero))
-        dkh = dot_nn(ds, jnp.where(mine, q, zero))
-        dqh = dot_nn(jnp.where(upper if h == 0 else ~upper, kt, jnp.zeros_like(kt)), ds)
-        dq, dk, dv = (dqh, dkh, dvh) if h == 0 else (dq + dqh, dk + dkh, dv + dvh)
-    cos, sin = cos_ref[...], sin_ref[...]
-    g_ref[0] = unrotary(dq.T * SCALE, cos, sin).astype(bf16)
-    g_ref[1] = unrotary(dk * SCALE, cos, sin).astype(bf16)
-    g_ref[2] = dv.astype(bf16)
-
-
-def attention_backward(q, k, v, do, o, lse, cos, sin, start, count, into=None):
+    step = pl.program_id(0)
+    width = x_ref.shape[1]
+
+    @pl.when(step < pairs)
+    def _():
+        first = lax.broadcasted_iota(jnp.int32, (1, LANES), 1) < HEAD_DIM
+        upper = lax.broadcasted_iota(jnp.int32, (LANES, 1), 0) < HEAD_DIM
+        c = LOG2E * SCALE
+        q, k, v, do = q_ref[...], k_ref[...], v_ref[...], do_ref[...]
+        prod = (do.astype(f32) * o_ref[...].astype(f32)).T
+        kt = k.T
+        zero = jnp.zeros_like(k)
+        dq = dk = dv = None
+        for h in range(2):
+            mine = first if h == 0 else ~first
+            row = column_sum(prod[h * HEAD_DIM : (h + 1) * HEAD_DIM])
+            st = dot_nt(jnp.where(mine, k, zero), q)
+            p = jnp.exp2(st * c - lse_ref[0, h : h + 1, :])
+            dp = dot_nt(jnp.where(mine, v, zero), do)
+            ds = (p * (dp - row)).astype(bf16)
+            dvh = dot_nn(p.astype(bf16), jnp.where(mine, do, zero))
+            dkh = dot_nn(ds, jnp.where(mine, q, zero))
+            dqh = dot_nn(jnp.where(upper if h == 0 else ~upper, kt, jnp.zeros_like(kt)), ds)
+            dq, dk, dv = (dqh, dkh, dvh) if h == 0 else (dq + dqh, dk + dkh, dv + dvh)
+        cos, sin = cos_ref[...], sin_ref[...]
+        lanes = pl.ds(pl.multiple_of(step * LANES, LANES), LANES)
+        for part, value in enumerate(
+            (unrotary(dq.T * SCALE, cos, sin), unrotary(dk * SCALE, cos, sin), dv)
+        ):
+            value = value.astype(bf16)
+            g_ref[part] = value
+            held_ref[part, :, lanes] = value
+
+    @pl.when(step >= pairs)
+    def _():
+        rows = x_ref.shape[0]
+        tile = pl.ds(pl.multiple_of((step - pairs) * rows, rows), rows)
+        normed, inverse = norm_forward(x_ref[...].astype(f32))
+        grad = None
+        for part in range(3):
+            g = dot_nt(held_ref[part, tile, :], w_ref[:, part * width : (part + 1) * width])
+            grad = g if grad is None else grad + g
+        hg = gm_ref[...] + norm_backward(grad * mod_ref[0:1, :], normed, inverse)
+        hg_ref[...] = hg.astype(bf16)
+        sums = jnp.concatenate(
+            [column_sum(grad), column_sum(grad * normed), jnp.zeros((6, width), f32)], axis=0
+        )
+
+        @pl.when(step == pairs)
+        def _():
+            sum_ref[...] = sums
+
+        @pl.when(step > pairs)
+        def _():
+            sum_ref[...] += sums
+
+
+def attention_backward(q, k, v, do, o, lse, cos, sin, x, gm, mods, weight, rows):
     length, width = q.shape
-    block = pl.BlockSpec((length, LANES), lambda i: (0, start + i))
+    pairs = width // LANES
+
+    def pair(i):
+        return jnp.minimum(i, pairs - 1)
+
+    block = pl.BlockSpec((length, LANES), lambda i: (0, pair(i)))
     table = pl.BlockSpec((length, LANES), lambda i: (0, 0))
-    extra = [] if into is None else [into]
-    return pl.pallas_call(
-        attention_backward_kernel,
-        grid=(count,),
+    tile = pl.BlockSpec((rows, width), lambda i: (jnp.maximum(i - pairs, 0), 0))
+    return pl.pallas_call(
+        functools.partial(attention_backward_kernel, pairs=pairs),
+        grid=(pairs + length // rows,),
         in_specs=[block] * 5
-        + [pl.BlockSpec((1, 2, length), lambda i: (start + i, 0, 0)), table, table]
-        + [pl.BlockSpec(memory_space=pl.ANY)] * len(extra),
-        out_specs=pl.BlockSpec((3, length, LANES), lambda i: (0, 0, start + i)),
-        out_shape=jax.ShapeDtypeStruct((3, length, width), bf16),
-        input_output_aliases={8: 0} if extra else {},
+        + [pl.BlockSpec((1, 2, length), lambda i: (pair(i), 0, 0)), table, table, tile, tile, VMEM, VMEM],
+        out_specs=[
+            pl.BlockSpec((3, length, LANES), lambda i: (0, 0, pair(i))),
+            tile,
+            pl.BlockSpec((8, width), lambda i: (0, 0)),
+        ],
+        out_shape=[
+            jax.ShapeDtypeStruct((3, length, width), bf16),
+            jax.ShapeDtypeStruct((length, width), bf16),
+            jax.ShapeDtypeStruct((8, width), f32),
+        ],
+        scratch_shapes=[pltpu.VMEM((3, length, width), bf16)],
         cost_estimate=COVER,
         name="attention_backward",
-    )(q, k, v, do, o, lse, cos, sin, *extra)
+    )(q, k, v, do, o, lse, cos, sin, x, gm, mods, weight)
 
 
 def mlp_kernel(
@@ -304,51 +348,26 @@
 
 
 def late_grads_kernel(
-    core_ref, x_ref, tile_ref, gm_ref, mod_ref, w_ref, xm_ref, ada_ref, timing_ref, early_ref, block_ref,
-    time_ref, hg_ref, send_ref, keep_ref, turned_ref, sum_ref, *, tiles, parts,
+    core_ref, sum_ref, mod_ref, ada_ref, timing_ref, early_ref, xm_ref, block_ref,
+    time_ref, send_ref, keep_ref, *, parts,
 ):
     step = pl.program_id(0)
-    width = x_ref.shape[1]
-
-    @pl.when(step < tiles)
+    width = block_ref.shape[2]
+
+    @pl.when(step < parts)
     def _():
-        normed, inverse = norm_forward(x_ref[...].astype(f32))
-        grad = None
-        for part in range(3):
-            g = dot_nt(tile_ref[part], w_ref[:, part * width : (part + 1) * width])
-            grad = g if grad is None else grad + g
-        hg = gm_ref[...] + norm_backward(grad * mod_ref[0:1, :], normed, inverse)
-        hg_ref[...] = hg.astype(bf16)
-        sums = jnp.concatenate(
-            [column_sum(grad), column_sum(grad * normed), jnp.zeros((6, width), f32)], axis=0
-        )
-
-        @pl.when(step == 0)
-        def _():
-            sum_ref[...] = sums
-
-        @pl.when(step > 0)
-        def _():
-            sum_ref[...] += sums
-
-    @pl.when(step == tiles)
-    def _():
-        turned_ref[...] = xm_ref[...].T
-
-    @pl.when((step >= tiles) & (step < tiles + parts))
-    def _():
-        product = dot_nn(turned_ref[...], block_ref[0])
+        product = dot_tn(xm_ref[...], block_ref[0])
         half = send_ref.shape[1]
         for i, (send, keep) in enumerate(split_halves(product, half, core_ref[0] == 0)):
             send_ref[i] = send
             keep_ref[i] = keep
 
-    @pl.when(step == tiles + parts)
+    @pl.when(step == parts)
     def _():
         sp, half, _ = send_ref.shape
         shift, scaled = sum_ref[0:1, :], sum_ref[1:2, :]
-        scale = scaled * mod_ref[2:3, :]
-        gain = scaled * mod_ref[3:4, :]
+        scale = scaled * mod_ref[0:1, :]
+        gain = scaled * mod_ref[1:2, :]
         row = jnp.concatenate([shift, scale] + [early_ref[i : i + 1, :] for i in range(4)], axis=1)
         high = row.astype(bf16)
         low = (row - high.astype(f32)).astype(bf16)
@@ -374,55 +393,28 @@
                 ref[i, count:] = sums.astype(bf16)
 
 
-def late_grads(core, x, grads, gm, mods, weight, xm, ada, timing, early, sp, rows):
-    length, width = x.shape
-    tiles = length // rows
-    n = grads.shape[0]
+def late_grads(core, grads, xm, sums, mods, ada, timing, early, sp):
+    n, length, width = grads.shape
     half = width // sp // 2
-
-    def tile(i, c):
-        return (jnp.minimum(i, tiles - 1), 0)
-
-    def part(i):
-        return jnp.maximum(i - tiles, 0)
-
-    def piece(i, c):
-        return (jnp.minimum(part(i), n - 1), 0, 0)
-
-    block = pl.BlockSpec((rows, width), tile)
-
-    out = pl.BlockSpec((sp, half, width), lambda i, c: (0, part(i), 0))
+    out = pl.BlockSpec((sp, half, width), lambda i, c: (0, i, 0))
     shape = jax.ShapeDtypeStruct((sp, (n + 1) * half, width), bf16)
     cond = timing.shape[0]
     return pl.pallas_call(
-        functools.partial(late_grads_kernel, tiles=tiles, parts=n),
+        functools.partial(late_grads_kernel, parts=n),
         grid_spec=pltpu.PrefetchScalarGridSpec(
             num_scalar_prefetch=1,
-            grid=(tiles + n + 1,),
-            in_specs=[
-                block,
-                pl.BlockSpec((n, rows, width), lambda i, c: (0, jnp.minimum(i, tiles - 1), 0)),
-                block,
-                VMEM,
-                VMEM,
-                VMEM,
-                VMEM,
-                VMEM,
-                VMEM,
-                pl.BlockSpec((1, length, width), piece),
+            grid=(n + 1,),
+            in_specs=[VMEM] * 5
+            + [
+                pl.BlockSpec((length, width), lambda i, c: (0, 0)),
+                pl.BlockSpec((1, length, width), lambda i, c: (jnp.minimum(i, n - 1), 0, 0)),
             ],
-            out_specs=[pl.BlockSpec((1, cond), lambda i, c: (0, 0)), block, out, out],
-            scratch_shapes=[pltpu.VMEM((width, length), bf16), pltpu.VMEM((8, width), f32)],
+            out_specs=[pl.BlockSpec((1, cond), lambda i, c: (0, 0)), out, out],
         ),
-        out_shape=[
-            jax.ShapeDtypeStruct((1, cond), bf16),
-            jax.ShapeDtypeStruct((length, width), bf16),
-            shape,
-            shape,
-        ],
+        out_shape=[jax.ShapeDtypeStruct((1, cond), bf16), shape, shape],
         cost_estimate=COVER,
         name="late_grads",
-    )(core, x, grads, gm, mods, weight, xm, ada, timing, early, grads)
+    )(core, sums, mods, ada, timing, early, xm, grads)
 
 
 def split_halves(product, half, this_core):
@@ -776,43 +768,58 @@
     )(core, mine, other)
 
 
-def vector_outputs_kernel(
-    early_ref, late_ref, ada_ref, bias_ref, attn_gain_ref, mlp_gain_ref, up_ref, down_ref, *, half
+def late_finish_kernel(
+    core_ref, mine_ref, other_ref, early_ref, qkv_ref, ada_ref, bias_ref, attn_gain_ref, mlp_gain_ref, up_ref,
+    down_ref, *, half,
 ):
-    count, width = ada_ref.shape[0], early_ref.shape[1]
+    core_first = core_ref[0] == 0
+    width = mine_ref.shape[1]
+    for n in range(3):
+        cols = slice(n * width, (n + 1) * width)
+        mine = mine_ref[n * half : (n + 1) * half].astype(f32)
+        other = other_ref[n * half : (n + 1) * half].astype(f32)
+        qkv_ref[:half, cols] = jnp.where(core_first, mine, other)
+        qkv_ref[half:, cols] = jnp.where(core_first, other, mine)
+    mine, other = mine_ref[3 * half :].astype(f32), other_ref[3 * half :].astype(f32)
+    late = (jnp.where(core_first, mine, other), jnp.where(core_first, other, mine))
+    count = ada_ref.shape[0]
     quarter, own = attn_gain_ref.shape[1], bias_ref.size
     for p in range(2):
-        ada_ref[:, p * width : (p + 1) * width] = late_ref[p * half : p * half + count, :]
+        ada_ref[:, p * width : (p + 1) * width] = late[p][:count]
     for p in range(4):
         start = p // 2 * half + p % 2 * count
         ada_ref[:, (2 + p) * width : (3 + p) * width] = early_ref[start : start + count, :]
-    row, low = 2 * count, half + count
-    rest = own - width
-    attn_gain_ref[...] = late_ref[low : low + 1, rest : rest + quarter]
+    row, rest = 2 * count, own - width
+    sums = (late[0][count : count + 1], late[1][count : count + 1])
     for lane in range(0, own, LANES):
-        i, cols = lane // LANES, slice(lane % width, lane % width + LANES)
-        a, b = (row + 1, count) if lane < width else (half + row + 1, low)
-        bias_ref[i : i + 1, :] = early_ref[a : a + 1, cols] + late_ref[b : b + 1, cols]
+        i, side = lane // LANES, lane // width
+        cols = slice(lane % width, lane % width + LANES)
+        at = side * half + row + 1
+        bias_ref[i : i + 1, :] = early_ref[at : at + 1, cols] + sums[side][:, cols]
     for lane in range(0, width, LANES):
         i = lane // LANES
         up_ref[i : i + 1, :] = early_ref[row : row + 1, lane : lane + LANES]
+    attn_gain_ref[...] = sums[1][:, rest : rest + quarter]
     mlp_gain_ref[...] = early_ref[half + row : half + row + 1, :quarter]
     down_ref[...] = early_ref[half + row : half + row + 1, quarter : 2 * quarter]
 
 
-def vector_outputs(early, late, half, cond, sp):
+def late_finish(core, mine, other, early, half, cond, sp):
     width = early.shape[1]
-    quarter = width // sp
-    one = (1, quarter)
-    shapes = [(cond // sp, 6 * width), (6 * width // sp // LANES, LANES), one, one, (width // LANES, LANES), one]
-    return pl.pallas_call(
-        functools.partial(vector_outputs_kernel, half=half),
-        in_specs=[VMEM] * 2,
-        out_specs=[VMEM] * 6,
+    one = (1, width // sp)
+    shapes = [
+        (2 * half, 3 * width), (cond // sp, 6 * width), (6 * width // sp // LANES, LANES),
+        one, one, (width // LANES, LANES), one,
+    ]
+    return pl.pallas_call(
+        functools.partial(late_finish_kernel, half=half),
+        grid=(1,),
+        in_specs=[SMEM] + [VMEM] * 3,
+        out_specs=[pl.BlockSpec(s, lambda i: (0, 0)) for s in shapes],
         out_shape=[jax.ShapeDtypeStruct(s, f32) for s in shapes],
         cost_estimate=COVER,
-        name="vector_outputs",
-    )(early, late)
+        name="late_finish",
+    )(core, mine, other, early)
 
 
 def sum_over_rest(total):
@@ -878,7 +885,7 @@
         + [zero] * 3,
         axis=0,
     )
-    late_mods = jnp.concatenate([attn_mods[:2], gain_attn, 1.0 + scale_attn] + [zero] * 4, axis=0)
+    late_mods = jnp.concatenate([gain_attn, 1.0 + scale_attn] + [zero] * 6, axis=0)
     mlp_grad_mods = jnp.concatenate([gain_mlp, 1.0 + scale_mlp] + [zero] * 6, axis=0)
     column = timing.astype(f32).reshape(timing.shape[1], 1)
     attn_mods, mlp_mods, late_mods, mlp_grad_mods, column, at, core = lax.optimization_barrier(
@@ -917,25 +924,19 @@
     row_send, row_keep = row_grad(core, *after((act, gd), col_keep), sp)
     row_got = pair_permute(row_send, CORE)
 
-    pairs = width // LANES
-
-    def backward(start, stop, into=None):
-        return attention_backward(
-            q, k, v, gmix, mixed, lse, cos, sin, start, stop - start, into
-        )
-
     left_send, left, right_send, right = first_halves(at, row_keep, row_got, col_keep, col_got)
     left_got, right_got = pair_permute(left_send, FIRST), pair_permute(right_send, SECOND)
     gmix = after(gmix, left, right)
-    grads = backward(0, pairs)
+    grads, hg, attn_sums = attention_backward(
+        q, k, v, gmix, mixed, lse, cos, sin, x, gm, attn_mods, query_key_value_matrix, local_len
+    )
     left_got, right_got, output = after((left_got, right_got, output), grads)
     left_send, left, right_send, right = second_halves(at, left, left_got, right, right_got)
     left_got, right_got = pair_permute(left_send, SECOND), pair_permute(right_send, FIRST)
     grads = after(grads, left, right, output)
 
-    time_row, hg, late_send, late_keep = late_grads(
-        core, x, grads, gm, late_mods, query_key_value_matrix, xm_attn, ada_weight, column, early_parts,
-        sp, local_len,
+    time_row, late_send, late_keep = late_grads(
+        core, grads, xm_attn, attn_sums, late_mods, ada_weight, column, early_parts, sp
     )
     hidden_grad = exchange(hg)
     late_got = pair_permute(late_send, CORE)
@@ -954,21 +955,25 @@
         for p, bit in zip(other_quarters, (SECOND, FIRST, FIRST + SECOND))
     ]
     output = hand_over(after(output, own_quarter))
-    near_got, hidden_grad, quarter_parts = after((near_got, hidden_grad, quarter_parts), output)
-    near_got = after(near_got, quarter_parts)
-    far_send, far = far_halves(at, near, after(near_got, hidden_grad))
+    near_got, hidden_grad = after((near_got, hidden_grad), output)
+    near_got = after(near_got, hidden_grad)
+    upper = me // 2
+    far_send = add(pick(near, 1 - upper), pick(near_got, 1 - upper))
+    far = add(pick(near, upper), pick(near_got, upper))
     far_got = pair_permute(far_send, 2, "sp")
-    quarter_parts = after(quarter_parts, far)
+    quarter_parts = after(quarter_parts, far, far_send)
     if lax.axis_size("dp") > 2 * SECOND:
         total = sum(p.astype(f32) for p in quarter_parts).astype(bf16)
         quarter_parts = [sum_over_rest(total)]
     late_near_send, late_near = near_halves(at, [quarter_parts])
     late_near_got = pair_permute(late_near_send, 1, "sp")
-    late_far_send, late_far = far_halves(at, late_near, late_near_got)
+    early_own = add(far, after(far_got, late_near))
+    early_four = spread(early_own)
+    late_near_got = after(late_near_got, early_own)
+    late_far_send = add(pick(late_near, 1 - upper), pick(late_near_got, 1 - upper))
+    late_far = add(pick(late_near, upper), pick(late_near_got, upper))
     late_far_got = pair_permute(late_far_send, 2, "sp")
-    early_own = own_sum(far, after(far_got, late_far))
-    early_four = spread(early_own)
-    late_own = own_sum(late_far, after(late_far_got, early_own))
+    late_own = add(late_far, late_far_got)
     hidden_grad = after(hidden_grad, late_own).astype(f32)
     time_rows = after(time_row, late_own)
     for bit in bits("sp"):
@@ -995,10 +1000,9 @@
     )
     late_half = four_chips(at, after(late_four, down_grad), False)
     late_other = pair_permute(late_half, CORE)
-    qkv_grad, late_vectors = finish(
-        core, late_half, late_other, half, ((1, 3, [0, half, 2 * half]), (1, 1, [3 * half]))
-    )
-    ada_weight_grad, *small = vector_outputs(early_vectors, late_vectors, half, cond, sp)
+    qkv_grad, ada_weight_grad, *small = late_finish(
+        core, late_half, late_other, early_vectors, half, cond, sp
+    )
     ada_bias_grad, attn_gain_grad, mlp_gain_grad, up_bias_grad, down_bias_grad = (
         v.reshape(-1) for v in small
     )

time: 339 us -> 330 us (0.973)
  waiting for transfers between devices: 84.2 us -> 94.7 us
  Pallas kernels: 185 us -> 175 us
  starting transfers between devices: 45.4 us -> 36.5 us
    ppermute x24, waiting for transfers between devices: 46.4 us -> 56.4 us  [pair_permute(): return lax.ppermute(value, axis, [(i, i ^ bit) for i in range(n)])]
    ppermute x24, starting transfers between devices: 27.7 us -> 18.4 us  [pair_permute(): return lax.ppermute(value, axis, [(i, i ^ bit) for i in range(n)])]
    pallas_call x7 -> x3, Pallas kernels: 61.9 us -> 54.1 us  [the longest x1 42.2 us: attention_backward(): pl.pallas_call(functools.partial(attention_backward_kernel, pairs=pairs),...]
    pallas_call x2 -> x1, Pallas kernels: 7.47 us -> 4.61 us  [finish(): pl.pallas_call(functools.partial(finish_kernel, half=half, layout=layout)...]
    unnamed x64 -> x56, local copies, waits for them, and re-layouts: 11.7 us -> 9.66 us
  transfers between devices with their start and end apart: 28 -> 28, of which waited for: 10 -> 15; matrix products, arithmetic and copies ran while one was open for 3% -> 3% of each run, Pallas kernels for 35% -> 36%
where the time goes in v2:
time: 330 us; the launch traced here: 329 us
  Pallas kernels  175 us (53%)
  waiting for transfers between devices  94.7 us (29%)
  starting transfers between devices  36.5 us (11%)
  local copies, waits for them, and re-layouts  11.2 us (3%)
  other arithmetic  10.2 us (3%)
    ppermute x24, waiting for transfers between devices, pair_permute(): return lax.ppermute(value, axis, [(i, i ^ bit) for i in range(n)])  56.4 us
    pallas_call x1, Pallas kernels, attention_backward(): pl.pallas_call(functools.partial(attention_backward_kernel, pairs=pairs),...  42.2 us
    all_to_all x4, waiting for transfers between devices, exchange(): return lax.all_to_all(values, 'sp', split_axis=0, concat_axis=0, tiled=True)  38.3 us
    pallas_call x1, Pallas kernels, feed_forward(): pl.pallas_call(mlp_kernel, grid=(length // rows,), in_specs=[block, block...  36 us
    pallas_call x1, Pallas kernels, attention_forward(): pl.pallas_call(functools.partial(attention_forward_kernel, chunk=length /...  19.5 us
    ppermute x24, starting transfers between devices, pair_permute(): return lax.ppermute(value, axis, [(i, i ^ bit) for i in range(n)])  18.4 us
    all_to_all x4, starting transfers between devices, exchange(): return lax.all_to_all(values, 'sp', split_axis=0, concat_axis=0, tiled=True)  18.1 us
    pallas_call x1, Pallas kernels, column_grad(): pl.pallas_call(functools.partial(column_grad_kernel, blocks=n), grid_spec...  12.1 us
  transfers between devices with their start and end apart: 28, of which 15 were waited for; matrix products, arithmetic and copies ran while one was open for 3% of the time, Pallas kernels for 36%

profile of v2, /device:TPU:0, one launch (start us, length us, event | category | flops | bytes accessed | tf_op | source)
XLA Modules:
  0.0 328.8 jit_solution(13481531567762768782)
XLA Ops:
  0.7 6.5 %all-to-all-start = ((bf16[4,256,768]{2,1,0:T(8,128)(2,1)}), bf16[4,256,768]{2,1,0:T(8,128)(2,1)S(1)}, u32[]{:S(2)}, u32[]{:S(2)}) async-start(bf16[4,256,768]{2,1,0:T(8,128)(2,1)} %param.13), calls=%async_computation | async-start | bytes 3145728 | tf_op jit(solution)/shard_map/all_to_all | solution.py:864
  11.0 3.1 multiply_sine_fusion
  14.1 30.1 %all-to-all-done = bf16[4,256,768]{2,1,0:T(8,128)(2,1)S(1)} async-done(((bf16[4,256,768]{2,1,0:T(8,128)(2,1)}), bf16[4,256,768]{2,1,0:T(8,128)(2,1)S(1)}, u32[]{:S(2)}, u32[]{:S(2)}) %all-to-all-start) | async-done | bytes 1572896 | tf_op jit(solution)/shard_map/all_to_all | solution.py:864
  45.3 3.6 %all-to-all-start.1 = ((bf16[4,256,768]{2,1,0:T(8,128)(2,1)}), bf16[4,256,768]{2,1,0:T(8,128)(2,1)S(1)}, u32[]{:S(2)}, u32[]{:S(2)}) async-start(bf16[4,256,768]{2,1,0:T(8,128)(2,1)} %param.25), calls=%async_computation.1 | async-start | bytes 3145728 | tf_op jit(solution)/shard_map/all_to_all | solution.py:864
  48.8 8.7 %project_qkv.1 = (bf16[1024,768]{1,0:T(8,128)(2,1)}, bf16[1024,768]{1,0:T(8,128)(2,1)}, bf16[1024,768]{1,0:T(8,128)(2,1)}, bf16[1024,768]{1,0:T(8,128)(2,1)}) custom-call(bf16[1024,768]{1,0:T(8,128)(2,1)} %bitcast.42, f32[8,768]{1,0:T(8,128)} %get-tuple-element.108.mod_ref, bf16[768,2304]{1,0:T(8,128)(2,1)} %w_ref.3, ...), custom_call_target="tpu_custom_call" | custom-call | flops 40000000000 | bytes 100000000 | tf_op jit(solution)/shard_map/project_qkv/pallas_call | solution.py:90
  57.5 19.5 %attention_forward.1 = (bf16[1024,768]{1,0:T(8,128)(2,1)}, f32[6,2,1024]{2,1,0:T(2,128)}) custom-call(bf16[1024,768]{1,0:T(8,128)(2,1)} %get-tuple-element.109.q_ref, bf16[1024,768]{1,0:T(8,128)(2,1)} %get-tuple-element.110.k_ref, bf16[1024,768]{1,0:T(8,128)(2,1)} %get-tuple-element.111.v_ref), custom_call_target="tpu_custom_call" | custom-call | flops 40000000000 | bytes 100000000 | tf_op jit(solution)/shard_map/attention_forward/pallas_call | solution.py:141
  77.1 8.2 %all-to-all-done.1 = bf16[4,256,768]{2,1,0:T(8,128)(2,1)S(1)} async-done(((bf16[4,256,768]{2,1,0:T(8,128)(2,1)}), bf16[4,256,768]{2,1,0:T(8,128)(2,1)S(1)}, u32[]{:S(2)}, u32[]{:S(2)}) %all-to-all-start.1) | async-done | bytes 1572896 | tf_op jit(solution)/shard_map/all_to_all | solution.py:864
  86.4 36.0 %feed_forward.1 = (bf16[2,1024,768]{2,1,0:T(8,128)(2,1)}, bf16[1024,3072]{1,0:T(8,128)(2,1)}, bf16[1024,768]{1,0:T(8,128)(2,1)}, bf16[5,1024,768]{2,1,0:T(8,128)...) custom-call(bf16[1024,768]{1,0:T(8,128)(2,1)} %bitcast.43, ...), custom_call_target="tpu_custom_call" | custom-call | flops 40000000000 | bytes 100000000 | tf_op jit(solution)/shard_map/feed_forward/pallas_call | solution.py:323
  122.5 12.1 %column_grad.1 = (bf16[4,576,768]{2,1,0:T(8,128)(2,1)}, bf16[4,576,768]{2,1,0:T(8,128)(2,1)}, f32[4,768]{1,0:T(4,128)}) custom-call(s32[1]{0:T(128)} %bitcast.6.core_ref, f32[8,768]{1,0:T(8,128)} %get-tuple-element.117.sum_ref, f32[1,3072]{1,0:T(1,128)} %get-tuple-element.118.up_sum_ref, f32[8,768]{1,0:T(8,128)} %get-tuple-element.119.mod_ref, ...), custom_call_target="tpu_custom_call" | custom-call | flops 40000000000 | bytes 100000000 | tf_op jit(solution)/shard_map/column_grad/pallas_call | solution.py:508
  134.6 9.2 %row_grad.1 = (bf16[4,384,768]{2,1,0:T(8,128)(2,1)}, bf16[4,384,768]{2,1,0:T(8,128)(2,1)}) custom-call(s32[1]{0:T(128)} %bitcast.6.core_ref, bf16[1024,3072]{1,0:T(8,128)(2,1)} %get-tuple-element.124.a_ref, bf16[1024,768]{1,0:T(8,128)(2,1)} %get-tuple-element.125.b_ref), custom_call_target="tpu_custom_call" | custom-call | flops 40000000000 | bytes 100000000 | tf_op jit(solution)/shard_map/row_grad/pallas_call | solution.py:440
  144.3 3.6 %all-to-all-start.2 = ((bf16[4,256,768]{2,1,0:T(8,128)(2,1)}), bf16[4,256,768]{2,1,0:T(8,128)(2,1)S(1)}, u32[]{:S(2)}, u32[]{:S(2)}) async-start(bf16[4,256,768]{2,1,0:T(8,128)(2,1)} %bitcast.10), calls=%async_computation.2 | async-start | bytes 3145728 | tf_op jit(solution)/shard_map/all_to_all | solution.py:864
  148.8 7.8 %first_halves.1 = (bf16[4,480,384]{2,1,0:T(8,128)(2,1)}, bf16[4,480,384]{2,1,0:T(8,128)(2,1)}, bf16[4,480,384]{2,1,0:T(8,128)(2,1)}, bf16[4,480,384]{2,1,0:T(8,128)(2,1)}) custom-call(s32[3]{0:T(128)} %pad_add_fusion.at_ref, bf16[4,384,768]{2,1,0:T(8,128)(2,1)} %get-tuple-element.126.row_keep, bf16[4,384,768]{2,1,0:T(8,128)(2,1)} %collective-permute-done.row_got, ...), custom_call_target="tpu_custom_call" | custom-call | flops 40000000000 | bytes 100000000 | tf_op jit(solution)/shard_map/first_halves/pallas_call | solution.py:578
  159.7 42.2 %attention_backward.1 = (bf16[3,1024,768]{2,1,0:T(8,128)(2,1)}, bf16[1024,768]{1,0:T(8,128)(2,1)}, f32[8,768]{1,0:T(8,128)}) custom-call(bf16[1024,768]{1,0:T(8,128)(2,1)} %get-tuple-element.109.q_ref, bf16[1024,768]{1,0:T(8,128)(2,1)} %get-tuple-element.110.k_ref, bf16[1024,768]{1,0:T(8,128)(2,1)} %get-tuple-element.111.v_ref, ...), custom_call_target="tpu_custom_call" | custom-call | flops 40000000000 | bytes 100000000 | tf_op jit(solution)/shard_map/attention_backward/pallas_call | solution.py:226
  203.0 4.6 %all-to-all-start.3 = ((bf16[4,256,768]{2,1,0:T(8,128)(2,1)}), bf16[4,256,768]{2,1,0:T(8,128)(2,1)}, u32[]{:S(2)}, u32[]{:S(2)}) async-start(bf16[4,256,768]{2,1,0:T(8,128)(2,1)} %bitcast.45), calls=%async_computation.3 | async-start | bytes 3145728 | tf_op jit(solution)/shard_map/all_to_all | solution.py:864
  208.7 4.6 %second_halves.1 = (bf16[4,240,384]{2,1,0:T(8,128)(2,1)}, bf16[4,240,384]{2,1,0:T(8,128)(2,1)}, bf16[4,240,384]{2,1,0:T(8,128)(2,1)}, bf16[4,240,384]{2,1,0:T(8,128)(2,1)}) custom-call(s32[3]{0:T(128)} %pad_add_fusion.at_ref, bf16[4,2,240,384]{3,2,1,0:T(8,128)(2,1)} %bitcast.54, bf16[4,2,240,384]{3,2,1,0:T(8,128)(2,1)} %bitcast.48, ...), custom_call_target="tpu_custom_call" | custom-call | flops 40000000000 | bytes 100000000 | tf_op jit(solution)/shard_map/second_halves/pallas_call | solution.py:604
  214.3 8.8 %late_grads.1 = (bf16[1,128]{1,0:T(2,128)(2,1)}, bf16[4,384,768]{2,1,0:T(8,128)(2,1)}, bf16[4,384,768]{2,1,0:T(8,128)(2,1)}) custom-call(s32[1]{0:T(128)} %bitcast.6.core_ref, f32[8,768]{1,0:T(8,128)} %get-tuple-element.140.sum_ref, f32[8,768]{1,0:T(8,128)} %get-tuple-element.141.mod_ref, bf16[128,4608]{1,0:T(8,128)(2,1)} %ada_ref.1, ...), custom_call_target="tpu_custom_call" | custom-call | flops 40000000000 | bytes 100000000 | tf_op jit(solution)/shard_map/late_grads/pallas_call | solution.py:402
  223.2 8.5 %collective-permute-done.5.refs_1_ = bf16[4,240,384]{2,1,0:T(8,128)(2,1)S(1)} collective-permute-done((bf16[4,240,384]{2,1,0:T(8,128)(2,1)}, bf16[4,240,384]{2,1,0:T(8,128)(2,1)S(1)}, u32[]{:S(2)}, u32[]{:S(2)}) %collective-permute-start.5) | collective-permute-done | bytes 737312 | tf_op jit(solution)/shard_map/ppermute | solution.py:533
  232.8 3.1 near_halves.2
  237.4 4.2 %quarters.1 = (bf16[4,96,768]{2,1,0:T(8,128)(2,1)}, bf16[4,96,768]{2,1,0:T(8,128)(2,1)}, bf16[4,96,768]{2,1,0:T(8,128)(2,1)}, bf16[4,96,768]{2,1,0:T(8,128)(2,1)}) custom-call(s32[3]{0:T(128)} %pad_add_fusion.at_ref, bf16[4,4,96,768]{3,2,1,0:T(8,128)(2,1)} %bitcast.53, bf16[4,4,96,768]{3,2,1,0:T(8,128)(2,1)} %bitcast.16.got_ref), custom_call_target="tpu_custom_call" | custom-call | flops 40000000000 | bytes 100000000 | tf_op jit(solution)/shard_map/quarters/pallas_call | solution.py:709
  245.1 3.6 %hand_over.1 = bf16[4,256,768]{2,1,0:T(8,128)(2,1)} custom-call(bf16[4,256,768]{2,1,0:T(8,128)(2,1)} %copy-done.1), custom_call_target="tpu_custom_call" | custom-call | flops 40000000000 | bytes 100000000 | tf_op jit(solution)/shard_map/hand_over/pallas_call | solution.py:673
  248.7 11.7 %collective-permute-done.7 = bf16[2,240,768]{2,1,0:T(8,128)(2,1)S(1)} collective-permute-done((bf16[2,240,768]{2,1,0:T(8,128)(2,1)}, bf16[2,240,768]{2,1,0:T(8,128)(2,1)S(1)}, u32[]{:S(2)}, u32[]{:S(2)}) %collective-permute-start.7) | collective-permute-done | bytes 737312 | tf_op jit(solution)/shard_map/ppermute | solution.py:533
  260.6 8.4 %collective-permute-done.8.refs_1_ = bf16[4,96,768]{2,1,0:T(8,128)(2,1)S(1)} collective-permute-done((bf16[4,96,768]{2,1,0:T(8,128)(2,1)}, bf16[4,96,768]{2,1,0:T(8,128)(2,1)S(1)}, u32[]{:S(2)}, u32[]{:S(2)}) %collective-permute-start.8) | collective-permute-done | bytes 589856 | tf_op jit(solution)/shard_map/ppermute | solution.py:533
  269.8 2.7 near_halves.3
  273.4 5.7 %collective-permute-done.12 = bf16[240,768]{1,0:T(8,128)(2,1)S(1)} collective-permute-done((bf16[240,768]{1,0:T(8,128)(2,1)S(1)}, bf16[240,768]{1,0:T(8,128)(2,1)S(1)}, u32[]{:S(2)}, u32[]{:S(2)}) %collective-permute-start.12) | collective-permute-done | bytes 368672 | tf_op jit(solution)/shard_map/ppermute | solution.py:533
  279.2 6.1 %collective-permute-done.11 = bf16[2,96,768]{2,1,0:T(8,128)(2,1)S(1)} collective-permute-done((bf16[2,96,768]{2,1,0:T(8,128)(2,1)}, bf16[2,96,768]{2,1,0:T(8,128)(2,1)S(1)}, u32[]{:S(2)}, u32[]{:S(2)}) %collective-permute-start.11) | collective-permute-done | bytes 294944 | tf_op jit(solution)/shard_map/ppermute | solution.py:533
  287.8 2.5 collective-permute-start.18
  290.2 5.5 %collective-permute-done.13 = bf16[96,768]{1,0:T(8,128)(2,1)S(1)} collective-permute-done((bf16[96,768]{1,0:T(8,128)(2,1)S(1)}, bf16[96,768]{1,0:T(8,128)(2,1)S(1)}, u32[]{:S(2)}, u32[]{:S(2)}) %collective-permute-start.13) | collective-permute-done | bytes 147488 | tf_op jit(solution)/shard_map/ppermute | solution.py:533
  295.9 3.5 %collective-permute-done.14 = bf16[1,128]{1,0:T(2,128)(2,1)S(1)} collective-permute-done((bf16[1,128]{1,0:T(2,128)(2,1)S(1)}, bf16[1,128]{1,0:T(2,128)(2,1)S(1)}, u32[]{:S(2)}, u32[]{:S(2)}) %collective-permute-start.14) | collective-permute-done | bytes 288 | tf_op jit(solution)/shard_map/ppermute | solution.py:533
  299.8 3.3 %convert_element_type.142 = f32[4,256,768]{2,1,0:T(8,128)} convert(bf16[4,256,768]{2,1,0:T(8,128)(2,1)} %all-to-all-done.3) | non-fusion elementwise | flops 786432 | bytes 4718592 | tf_op jit(solution)/shard_map/convert_element_type | solution.py:977
  306.8 2.6 four_chips.2
  314.0 4.6 %finish.1 = (f32[768,768]{1,0:T(8,128)}, f32[192,3072]{1,0:T(8,128)}, f32[192,768]{1,0:T(8,128)}, f32[192,768]{1,0:T(8,128)}) custom-call(s32[1]{0:T(128)} %bitcast.6.core_ref, bf16[960,768]{1,0:T(8,128)(2,1)} %bitcast.50, bf16[960,768]{1,0:T(8,128)(2,1)} %copy-done.16), custom_call_target="tpu_custom_call" | custom-call | flops 40000000000 | bytes 100000000 | tf_op jit(solution)/shard_map/finish/pallas_call | solution.py:760
  325.7 3.0 late_finish.1
  (125 shorter events, 40.2 us)
Async XLA Ops:
  0.7 43.4 %all-to-all-start = ((bf16[4,256,768]{2,1,0:T(8,128)(2,1)}), bf16[4,256,768]{2,1,0:T(8,128)(2,1)S(1)}, u32[]{:S(2)}, u32[]{:S(2)}) async-start(bf16[4,256,768]{2,1,0:T(8,128)(2,1)} %param.13), calls=%async_computation | async-start | bytes 3145728 | tf_op jit(solution)/shard_map/all_to_all | solution.py:864
  45.3 40.0 %all-to-all-start.1 = ((bf16[4,256,768]{2,1,0:T(8,128)(2,1)}), bf16[4,256,768]{2,1,0:T(8,128)(2,1)S(1)}, u32[]{:S(2)}, u32[]{:S(2)}) async-start(bf16[4,256,768]{2,1,0:T(8,128)(2,1)} %param.25), calls=%async_computation.1 | async-start | bytes 3145728 | tf_op jit(solution)/shard_map/all_to_all | solution.py:864
  134.6 14.2 %collective-permute-start.1 = (bf16[4,576,768]{2,1,0:T(8,128)(2,1)}, bf16[4,576,768]{2,1,0:T(8,128)(2,1)}, u32[]{:S(2)}, u32[]{:S(2)}) collective-permute-start(bf16[4,576,768]{2,1,0:T(8,128)(2,1)} %get-tuple-element.128), channel_id=1, source_target_pairs={{0,4},{4,0},{8,12},{12,8},{16,20},{20,16},{24,28},{28,24},{1,5},{5... | collective-permute-start | bytes 10616840 | tf_op jit(solution)/shard_map/ppermute | solution.py:533
  143.8 5.0 %collective-permute-start = (bf16[4,384,768]{2,1,0:T(8,128)(2,1)}, bf16[4,384,768]{2,1,0:T(8,128)(2,1)}, u32[]{:S(2)}, u32[]{:S(2)}) collective-permute-start(bf16[4,384,768]{2,1,0:T(8,128)(2,1)} %get-tuple-element.127), channel_id=1, source_target_pairs={{0,4},{4,0},{8,12},{12,8},{16,20},{20,16},{24,28},{28,24},{1,5},{5... | collective-permute-start | bytes 7077896 | tf_op jit(solution)/shard_map/ppermute | solution.py:533
  144.3 57.6 %all-to-all-start.2 = ((bf16[4,256,768]{2,1,0:T(8,128)(2,1)}), bf16[4,256,768]{2,1,0:T(8,128)(2,1)S(1)}, u32[]{:S(2)}, u32[]{:S(2)}) async-start(bf16[4,256,768]{2,1,0:T(8,128)(2,1)} %bitcast.10), calls=%async_computation.2 | async-start | bytes 3145728 | tf_op jit(solution)/shard_map/all_to_all | solution.py:864
  156.6 51.0 %collective-permute-start.2 = (bf16[4,480,384]{2,1,0:T(8,128)(2,1)}, bf16[4,480,384]{2,1,0:T(8,128)(2,1)S(1)}, u32[]{:S(2)}, u32[]{:S(2)}) collective-permute-start(bf16[4,480,384]{2,1,0:T(8,128)(2,1)} %get-tuple-element.129), channel_id=1, source_target_pairs={{0,8},{4,12},{8,0},{12,4},{16,24},{20,28},{24,16},{28,20},{1,9},{5... | collective-permute-start | bytes 4423688 | tf_op jit(solution)/shard_map/ppermute | solution.py:533
  158.1 49.5 %collective-permute-start.3 = (bf16[4,480,384]{2,1,0:T(8,128)(2,1)}, bf16[4,480,384]{2,1,0:T(8,128)(2,1)}, u32[]{:S(2)}, u32[]{:S(2)}) collective-permute-start(bf16[4,480,384]{2,1,0:T(8,128)(2,1)} %get-tuple-element.130), channel_id=1, source_target_pairs={{0,16},{4,20},{8,24},{12,28},{16,0},{20,4},{24,8},{28,12},{1,17},{... | collective-permute-start | bytes 4423688 | tf_op jit(solution)/shard_map/ppermute | solution.py:533
  203.0 45.6 %all-to-all-start.3 = ((bf16[4,256,768]{2,1,0:T(8,128)(2,1)}), bf16[4,256,768]{2,1,0:T(8,128)(2,1)}, u32[]{:S(2)}, u32[]{:S(2)}) async-start(bf16[4,256,768]{2,1,0:T(8,128)(2,1)} %bitcast.45), calls=%async_computation.3 | async-start | bytes 3145728 | tf_op jit(solution)/shard_map/all_to_all | solution.py:864
  213.3 18.4 %collective-permute-start.5 = (bf16[4,240,384]{2,1,0:T(8,128)(2,1)}, bf16[4,240,384]{2,1,0:T(8,128)(2,1)S(1)}, u32[]{:S(2)}, u32[]{:S(2)}) collective-permute-start(bf16[4,240,384]{2,1,0:T(8,128)(2,1)} %get-tuple-element.151), channel_id=1, source_target_pairs={{0,16},{4,20},{8,24},{12,28},{16,0},{20,4},{24,8},{28,12},{1,17},{... | collective-permute-start | bytes 2211848 | tf_op jit(solution)/shard_map/ppermute | solution.py:533
  213.8 18.1 %collective-permute-start.6 = (bf16[4,240,384]{2,1,0:T(8,128)(2,1)}, bf16[4,240,384]{2,1,0:T(8,128)(2,1)S(1)}, u32[]{:S(2)}, u32[]{:S(2)}) collective-permute-start(bf16[4,240,384]{2,1,0:T(8,128)(2,1)} %get-tuple-element.152), channel_id=1, source_target_pairs={{0,8},{4,12},{8,0},{12,4},{16,24},{20,28},{24,16},{28,20},{1,9},{5... | collective-permute-start | bytes 2211848 | tf_op jit(solution)/shard_map/ppermute | solution.py:533
  223.2 14.2 %collective-permute-start.4 = (bf16[4,384,768]{2,1,0:T(8,128)(2,1)}, bf16[4,384,768]{2,1,0:T(8,128)(2,1)}, u32[]{:S(2)}, u32[]{:S(2)}) collective-permute-start(bf16[4,384,768]{2,1,0:T(8,128)(2,1)} %get-tuple-element.150), channel_id=1, source_target_pairs={{0,4},{4,0},{8,12},{12,8},{16,20},{20,16},{24,28},{28,24},{1,5},{5... | collective-permute-start | bytes 7077896 | tf_op jit(solution)/shard_map/ppermute | solution.py:533
  235.9 24.4 %collective-permute-start.7 = (bf16[2,240,768]{2,1,0:T(8,128)(2,1)}, bf16[2,240,768]{2,1,0:T(8,128)(2,1)S(1)}, u32[]{:S(2)}, u32[]{:S(2)}) collective-permute-start(bf16[2,240,768]{2,1,0:T(8,128)(2,1)} %get-tuple-element.159), channel_id=1, source_target_pairs={{0,1},{1,0},{2,3},{3,2},{4,5},{5,4},{6,7},{7,6},{8,9},{9,8},{10,11... | collective-permute-start | bytes 2211848 | tf_op jit(solution)/shard_map/ppermute | solution.py:533
  241.6 19.0 %collective-permute-start.10 = (bf16[4,96,768]{2,1,0:T(8,128)(2,1)}, bf16[4,96,768]{2,1,0:T(8,128)(2,1)S(1)}, u32[]{:S(2)}, u32[]{:S(2)}) collective-permute-start(bf16[4,96,768]{2,1,0:T(8,128)(2,1)} %get-tuple-element.164), channel_id=1, source_target_pairs={{0,24},{4,28},{8,16},{12,20},{16,8},{20,12},{24,0},{28,4},{1,25},{... | collective-permute-start | bytes 1769480 | tf_op jit(solution)/shard_map/ppermute | solution.py:533
  243.1 25.9 %collective-permute-start.8 = (bf16[4,96,768]{2,1,0:T(8,128)(2,1)}, bf16[4,96,768]{2,1,0:T(8,128)(2,1)S(1)}, u32[]{:S(2)}, u32[]{:S(2)}) collective-permute-start(bf16[4,96,768]{2,1,0:T(8,128)(2,1)} %get-tuple-element.162), channel_id=1, source_target_pairs={{0,16},{4,20},{8,24},{12,28},{16,0},{20,4},{24,8},{28,12},{1,17},{... | collective-permute-start | bytes 1769480 | tf_op jit(solution)/shard_map/ppermute | solution.py:533
  243.6 16.7 %copy-start.4 = (bf16[2,240,768]{2,1,0:T(8,128)(2,1)S(1)}, bf16[2,240,768]{2,1,0:T(8,128)(2,1)}, u32[]{:S(2)}) copy-start(bf16[2,240,768]{2,1,0:T(8,128)(2,1)} %get-tuple-element.155) | copy-start | bytes 2211844
  243.6 25.4 %collective-permute-start.9 = (bf16[4,96,768]{2,1,0:T(8,128)(2,1)}, bf16[4,96,768]{2,1,0:T(8,128)(2,1)}, u32[]{:S(2)}, u32[]{:S(2)}) collective-permute-start(bf16[4,96,768]{2,1,0:T(8,128)(2,1)} %get-tuple-element.163), channel_id=1, source_target_pairs={{0,8},{4,12},{8,0},{12,4},{16,24},{20,28},{24,16},{28,20},{1,9},{5... | collective-permute-start | bytes 1769480 | tf_op jit(solution)/shard_map/ppermute | solution.py:533
  260.5 18.6 %collective-permute-start.12 = (bf16[240,768]{1,0:T(8,128)(2,1)S(1)}, bf16[240,768]{1,0:T(8,128)(2,1)S(1)}, u32[]{:S(2)}, u32[]{:S(2)}) collective-permute-start(bf16[240,768]{1,0:T(8,128)(2,1)S(1)} %get-tuple-element.199), channel_id=1, source_target_pairs={{0,2},{1,3},{2,0},{3,1},{4,6},{5,7},{6,4},{7,5},{8,10},{9,11},{10,... | collective-permute-start | bytes 1105928 | tf_op jit(solution)/shard_map/ppermute | solution.py:533
  272.5 23.2 %copy-start.6 = (bf16[2,96,768]{2,1,0:T(8,128)(2,1)S(1)}, bf16[2,96,768]{2,1,0:T(8,128)(2,1)}, u32[]{:S(2)}) copy-start(bf16[2,96,768]{2,1,0:T(8,128)(2,1)} %get-tuple-element.171) | copy-start | bytes 884740
  272.5 23.3 %copy-start.13 = (bf16[1,128]{1,0:T(2,128)(2,1)S(1)}, bf16[1,128]{1,0:T(2,128)(2,1)}, u32[]{:S(2)}) copy-start(bf16[1,128]{1,0:T(2,128)(2,1)} %get-tuple-element.177) | copy-start | bytes 772
  272.5 12.8 %collective-permute-start.11 = (bf16[2,96,768]{2,1,0:T(8,128)(2,1)}, bf16[2,96,768]{2,1,0:T(8,128)(2,1)S(1)}, u32[]{:S(2)}, u32[]{:S(2)}) collective-permute-start(bf16[2,96,768]{2,1,0:T(8,128)(2,1)} %get-tuple-element.172), channel_id=1, source_target_pairs={{0,1},{1,0},{2,3},{3,2},{4,5},{5,4},{6,7},{7,6},{8,9},{9,8},{10,11... | collective-permute-start | bytes 884744 | tf_op jit(solution)/shard_map/ppermute | solution.py:533
  279.2 23.9 %copy-start.5 = (bf16[240,768]{1,0:T(8,128)(2,1)}, bf16[240,768]{1,0:T(8,128)(2,1)S(1)}, u32[]{:S(2)}) copy-start(bf16[240,768]{1,0:T(8,128)(2,1)S(1)} %add_convert_fusion.refs_0_) | copy-start | bytes 1105924
  286.3 9.5 %collective-permute-start.13 = (bf16[96,768]{1,0:T(8,128)(2,1)S(1)}, bf16[96,768]{1,0:T(8,128)(2,1)S(1)}, u32[]{:S(2)}, u32[]{:S(2)}) collective-permute-start(bf16[96,768]{1,0:T(8,128)(2,1)S(1)} %fusion.4), channel_id=1, source_target_pairs={{0,2},{1,3},{2,0},{3,1},{4,6},{5,7},{6,4},{7,5},{8,10},{9,11},{10,... | collective-permute-start | bytes 442376 | tf_op jit(solution)/shard_map/ppermute | solution.py:533
  286.7 17.2 %collective-permute-start.16 = (bf16[240,768]{1,0:T(8,128)(2,1)S(1)}, bf16[240,768]{1,0:T(8,128)(2,1)S(1)}, u32[]{:S(2)}, u32[]{:S(2)}) collective-permute-start(bf16[240,768]{1,0:T(8,128)(2,1)S(1)} %add_convert_fusion.refs_0_), channel_id=1, source_target_pairs={{0,16},{4,20},{8,24},{12,28},{16,0},{20,4},{24,8},{28,12},{1,17},{... | collective-permute-start | bytes 1105928 | tf_op jit(solution)/shard_map/ppermute | solution.py:533
  287.2 16.7 %collective-permute-start.17 = (bf16[240,768]{1,0:T(8,128)(2,1)S(1)}, bf16[240,768]{1,0:T(8,128)(2,1)S(1)}, u32[]{:S(2)}, u32[]{:S(2)}) collective-permute-start(bf16[240,768]{1,0:T(8,128)(2,1)S(1)} %add_convert_fusion.refs_0_), channel_id=1, source_target_pairs={{0,8},{4,12},{8,0},{12,4},{16,24},{20,28},{24,16},{28,20},{1,9},{5... | collective-permute-start | bytes 1105928 | tf_op jit(solution)/shard_map/ppermute | solution.py:533
  287.8 18.3 %collective-permute-start.18 = (bf16[240,768]{1,0:T(8,128)(2,1)S(1)}, bf16[240,768]{1,0:T(8,128)(2,1)S(1)}, u32[]{:S(2)}, u32[]{:S(2)}) collective-permute-start(bf16[240,768]{1,0:T(8,128)(2,1)S(1)} %add_convert_fusion.refs_0_), channel_id=1, source_target_pairs={{0,24},{4,28},{8,16},{12,20},{16,8},{20,12},{24,0},{28,4},{1,25},{... | collective-permute-start | bytes 1105928 | tf_op jit(solution)/shard_map/ppermute | solution.py:533
  295.8 3.6 %collective-permute-start.14 = (bf16[1,128]{1,0:T(2,128)(2,1)S(1)}, bf16[1,128]{1,0:T(2,128)(2,1)S(1)}, u32[]{:S(2)}, u32[]{:S(2)}) collective-permute-start(bf16[1,128]{1,0:T(2,128)(2,1)S(1)} %copy-done.13), channel_id=1, source_target_pairs={{0,1},{1,0},{2,3},{3,2},{4,5},{5,4},{6,7},{7,6},{8,9},{9,8},{10,11... | collective-permute-start | bytes 776 | tf_op jit(solution)/shard_map/ppermute | solution.py:533
  299.4 4.5 %collective-permute-start.15 = (bf16[2,128]{1,0:T(2,128)(2,1)S(1)}, bf16[2,128]{1,0:T(2,128)(2,1)S(1)}, u32[]{:S(2)}, u32[]{:S(2)}) collective-permute-start(bf16[2,128]{1,0:T(2,128)(2,1)S(1)} %pad_maximum_fusion.1), channel_id=1, source_target_pairs={{0,2},{1,3},{2,0},{3,1},{4,6},{5,7},{6,4},{7,5},{8,10},{9,11},{10,... | collective-permute-start | bytes 1544 | tf_op jit(solution)/shard_map/ppermute | solution.py:533
  309.4 3.5 %collective-permute-start.22 = (bf16[960,768]{1,0:T(8,128)(2,1)}, bf16[960,768]{1,0:T(8,128)(2,1)S(1)}, u32[]{:S(2)}, u32[]{:S(2)}) collective-permute-start(bf16[960,768]{1,0:T(8,128)(2,1)} %bitcast.49), channel_id=1, source_target_pairs={{0,4},{4,0},{8,12},{12,8},{16,20},{20,16},{24,28},{28,24},{1,5},{5... | collective-permute-start | bytes 4423688 | tf_op jit(solution)/shard_map/ppermute | solution.py:533
  309.4 9.3 %collective-permute-start.19 = (bf16[96,768]{1,0:T(8,128)(2,1)S(1)}, bf16[96,768]{1,0:T(8,128)(2,1)S(1)}, u32[]{:S(2)}, u32[]{:S(2)}) collective-permute-start(bf16[96,768]{1,0:T(8,128)(2,1)S(1)} %fusion.2.refs_0_), channel_id=1, source_target_pairs={{0,16},{4,20},{8,24},{12,28},{16,0},{20,4},{24,8},{28,12},{1,17},{... | collective-permute-start | bytes 442376 | tf_op jit(solution)/shard_map/ppermute | solution.py:533
  309.9 8.8 %collective-permute-start.20 = (bf16[96,768]{1,0:T(8,128)(2,1)S(1)}, bf16[96,768]{1,0:T(8,128)(2,1)S(1)}, u32[]{:S(2)}, u32[]{:S(2)}) collective-permute-start(bf16[96,768]{1,0:T(8,128)(2,1)S(1)} %fusion.2.refs_0_), channel_id=1, source_target_pairs={{0,8},{4,12},{8,0},{12,4},{16,24},{20,28},{24,16},{28,20},{1,9},{5... | collective-permute-start | bytes 442376 | tf_op jit(solution)/shard_map/ppermute | solution.py:533
  310.4 9.6 %collective-permute-start.21 = (bf16[96,768]{1,0:T(8,128)(2,1)S(1)}, bf16[96,768]{1,0:T(8,128)(2,1)S(1)}, u32[]{:S(2)}, u32[]{:S(2)}) collective-permute-start(bf16[96,768]{1,0:T(8,128)(2,1)S(1)} %fusion.2.refs_0_), channel_id=1, source_target_pairs={{0,24},{4,28},{8,16},{12,20},{16,8},{20,12},{24,0},{28,4},{1,25},{... | collective-permute-start | bytes 442376 | tf_op jit(solution)/shard_map/ppermute | solution.py:533
  322.7 2.2 collective-permute-start.23
  (24 other events, 83.1 us)

commit v3 on v2

--- a/solution.py
+++ b/solution.py
@@ -8,6 +8,7 @@
 from jax.sharding import PartitionSpec as P
 
 HEAD_DIM = 64
+MIB = 1 << 20
 VMEM = pl.BlockSpec(memory_space=pltpu.VMEM)
 SMEM = pl.BlockSpec(memory_space=pltpu.SMEM)
 HALF = HEAD_DIM // 2
@@ -18,6 +19,14 @@
 f32 = jnp.float32
 COVER = pl.CostEstimate(flops=40_000_000_000, bytes_accessed=100_000_000, transcendentals=0)
 bf16 = jnp.bfloat16
+
+
+def on_chip(arrays):
+    return [pltpu.with_memory_space_constraint(a, pltpu.VMEM) for a in arrays]
+
+
+def streamed(*arrays):
+    return [pltpu.with_memory_space_constraint(a, pltpu.HBM) for a in arrays]
 
 
 def dot_nn(a, b):
@@ -86,22 +95,23 @@
     length, width = x.shape
     block = pl.BlockSpec((rows, width), lambda i: (i, 0))
     table = pl.BlockSpec((rows, LANES), lambda i: (i, 0))
-    shape = jax.ShapeDtypeStruct((length, width), bf16)
+    shape = pltpu.HBM((length, width), bf16)
     return pl.pallas_call(
         qkv_kernel,
         grid=(length // rows,),
         in_specs=[
             block,
             VMEM,
-            VMEM,
+            pl.BlockSpec(weight.shape, lambda i: (0, 0)),
             table,
             table,
         ],
         out_specs=[block] * 4,
         out_shape=[shape] * 4,
         cost_estimate=COVER,
+        compiler_params=pltpu.CompilerParams(vmem_limit_bytes=18 * MIB),
         name="project_qkv",
-    )(x, mods, weight, cos, sin)
+    )(*streamed(x), mods, *streamed(weight, cos, sin))
 
 
 def attention_forward_kernel(q_ref, k_ref, v_ref, o_ref, lse_ref, *, chunk, ahead):
@@ -144,12 +154,13 @@
         in_specs=[block] * 3,
         out_specs=[block, pl.BlockSpec((1, 2, length), lambda i: (i, 0, 0))],
         out_shape=[
-            jax.ShapeDtypeStruct((length, width), bf16),
-            jax.ShapeDtypeStruct((pairs, 2, length), f32),
+            pltpu.HBM((length, width), bf16),
+            pltpu.HBM((pairs, 2, length), f32),
         ],
         cost_estimate=COVER,
+        compiler_params=pltpu.CompilerParams(vmem_limit_bytes=14 * MIB),
         name="attention_forward",
-    )(q, k, v)
+    )(*streamed(q, k, v))
 
 
 def attention_backward_kernel(
@@ -234,12 +245,13 @@
             pl.BlockSpec((8, width), lambda i: (0, 0)),
         ],
         out_shape=[
-            jax.ShapeDtypeStruct((3, length, width), bf16),
-            jax.ShapeDtypeStruct((length, width), bf16),
+            pltpu.HBM((3, length, width), bf16),
+            pltpu.HBM((length, width), bf16),
             jax.ShapeDtypeStruct((8, width), f32),
         ],
         scratch_shapes=[pltpu.VMEM((3, length, width), bf16)],
         cost_estimate=COVER,
+        compiler_params=pltpu.CompilerParams(vmem_limit_bytes=34 * MIB),
         name="attention_backward",
     )(q, k, v, do, o, lse, cos, sin, x, gm, mods, weight)
 
@@ -318,8 +330,8 @@
     block = pl.BlockSpec((rows, width), lambda i: (i, 0))
     wide = pl.BlockSpec((rows, ff), lambda i: (i, 0))
 
-    narrow = jax.ShapeDtypeStruct((length, width), bf16)
-    broad = jax.ShapeDtypeStruct((length, ff), bf16)
+    narrow = pltpu.HBM((length, width), bf16)
+    broad = pltpu.HBM((length, ff), bf16)
     return pl.pallas_call(
         mlp_kernel,
         grid=(length // rows,),
@@ -336,15 +348,16 @@
         ]
         + [block],
         out_shape=[
-            jax.ShapeDtypeStruct((2, length, width), bf16), broad, narrow,
-            jax.ShapeDtypeStruct((ff // width + 1, length, width), bf16),
-            jax.ShapeDtypeStruct((length, width), f32), narrow,
+            pltpu.HBM((2, length, width), bf16), broad, narrow,
+            pltpu.HBM((ff // width + 1, length, width), bf16),
+            pltpu.HBM((length, width), f32), narrow,
             jax.ShapeDtypeStruct((8, width), f32), jax.ShapeDtypeStruct((1, ff), f32),
         ]
         + [narrow],
         cost_estimate=COVER,
+        compiler_params=pltpu.CompilerParams(vmem_limit_bytes=40 * MIB),
         name="feed_forward",
-    )(x, mixed, cot, mods, up_bias, wo, wu, wd)
+    )(x, *streamed(mixed, cot), mods, up_bias, wo, *streamed(wu, wd))
 
 
 def late_grads_kernel(
@@ -413,6 +426,7 @@
         ),
         out_shape=[jax.ShapeDtypeStruct((1, cond), bf16), shape, shape],
         cost_estimate=COVER,
+        compiler_params=pltpu.CompilerParams(vmem_limit_bytes=18 * MIB),
         name="late_grads",
     )(core, sums, mods, ada, timing, early, xm, grads)
 
@@ -435,7 +449,7 @@
 
 def row_grad(core, a, b, sp):
     length, width = b.shape
-    out = jax.ShapeDtypeStruct((sp, width // 2, width), bf16)
+    out = pltpu.HBM((sp, width // 2, width), bf16)
     block = pl.BlockSpec((1, width // 2, width), lambda j, c: (j, 0, 0))
     return pl.pallas_call(
         functools.partial(row_grad_kernel, half=width // sp // 2),
@@ -450,8 +464,9 @@
         ),
         out_shape=[out, out],
         cost_estimate=COVER,
+        compiler_params=pltpu.CompilerParams(vmem_limit_bytes=18 * MIB),
         name="row_grad",
-    )(core, a, b)
+    )(core, *streamed(a, b))
 
 
 def column_grad_kernel(
@@ -503,7 +518,7 @@
     _, length, width = a.shape
     n = b.shape[0]
     half = width // sp // 2
-    out = jax.ShapeDtypeStruct((sp, (n + 1) * half, width), bf16)
+    out = pltpu.HBM((sp, (n + 1) * half, width), bf16)
     block = pl.BlockSpec((sp, half, width), lambda j, c: (0, j, 0))
     return pl.pallas_call(
         functools.partial(column_grad_kernel, blocks=n),
@@ -519,8 +534,9 @@
         ),
         out_shape=[out, out, jax.ShapeDtypeStruct((4, width), f32)],
         cost_estimate=COVER,
+        compiler_params=pltpu.CompilerParams(vmem_limit_bytes=18 * MIB),
         name="column_grad",
-    )(core, sums, up_sum, mods, timing, a, b)
+    )(core, sums, up_sum, mods, timing, *streamed(a, b))
 
 
 def shift_permute(value, axis, by):
@@ -574,7 +590,7 @@
     def spec(a):
         return pl.BlockSpec((1,) + a.shape[1:], lambda s, t: (s, 0, 0))
 
-    out = jax.ShapeDtypeStruct((sp, (rows + cols) // 2, width // 2), bf16)
+    out = pltpu.HBM((sp, (rows + cols) // 2, width // 2), bf16)
     return pl.pallas_call(
         first_halves_kernel,
         grid_spec=pltpu.PrefetchScalarGridSpec(
@@ -585,8 +601,9 @@
         ),
         out_shape=[out] * 4,
         cost_estimate=COVER,
+        compiler_params=pltpu.CompilerParams(vmem_limit_bytes=12 * MIB),
         name="first_halves",
-    )(at, row_keep, row_got, col_keep, col_got)
+    )(at, *streamed(row_keep, row_got, col_keep, col_got))
 
 
 def second_halves_kernel(at_ref, *refs):
@@ -607,8 +624,9 @@
         out_specs=[VMEM] * 4,
         out_shape=[out] * 4,
         cost_estimate=COVER,
+        compiler_params=pltpu.CompilerParams(vmem_limit_bytes=10 * MIB),
         name="second_halves",
-    )(at, *[a.reshape(sp, 2, rows // 2, columns) for a in arrays])
+    )(at, *streamed(*[a.reshape(sp, 2, rows // 2, columns) for a in arrays]))
 
 
 def near_halves_kernel(at_ref, *refs, terms, sides):
@@ -638,8 +656,9 @@
         out_specs=[VMEM] * 2,
         out_shape=[out] * 2,
         cost_estimate=COVER,
+        compiler_params=pltpu.CompilerParams(vmem_limit_bytes=8 * MIB),
         name="near_halves",
-    )(at, *flat)
+    )(at, *on_chip(flat))
 
 
 def far_halves_kernel(at_ref, keep, got, send_ref, keep_ref):
@@ -677,6 +696,7 @@
         out_specs=block,
         out_shape=jax.ShapeDtypeStruct(value.shape, dtype),
         cost_estimate=COVER,
+        compiler_params=pltpu.CompilerParams(vmem_limit_bytes=6 * MIB),
         name="hand_over",
     )(value)
 
@@ -712,8 +732,9 @@
         out_specs=[VMEM] * 4,
         out_shape=[out] * 4,
         cost_estimate=COVER,
+        compiler_params=pltpu.CompilerParams(vmem_limit_bytes=10 * MIB),
         name="quarters",
-    )(at, keep.reshape(sp, 4, rows // 4, width), got.reshape(sp, 4, rows // 4, width))
+    )(at, *on_chip([a.reshape(sp, 4, rows // 4, width) for a in (keep, got)]))
 
 
 def four_chips_kernel(at_ref, *refs, crossed):
@@ -733,8 +754,9 @@
         out_specs=VMEM,
         out_shape=jax.ShapeDtypeStruct((4, rows, width), bf16),
         cost_estimate=COVER,
+        compiler_params=pltpu.CompilerParams(vmem_limit_bytes=8 * MIB),
         name="four_chips",
-    )(at, *pieces).reshape(4 * rows, width)
+    )(at, *on_chip(pieces)).reshape(4 * rows, width)
 
 
 def spread(own):
@@ -764,8 +786,9 @@
         out_specs=[pl.BlockSpec(s, lambda i: (0, 0)) for s in shapes],
         out_shape=[jax.ShapeDtypeStruct(s, f32) for s in shapes],
         cost_estimate=COVER,
+        compiler_params=pltpu.CompilerParams(vmem_limit_bytes=16 * MIB),
         name="finish",
-    )(core, mine, other)
+    )(core, *on_chip([mine, other]))
 
 
 def late_finish_kernel(
@@ -818,8 +841,9 @@
         out_specs=[pl.BlockSpec(s, lambda i: (0, 0)) for s in shapes],
         out_shape=[jax.ShapeDtypeStruct(s, f32) for s in shapes],
         cost_estimate=COVER,
+        compiler_params=pltpu.CompilerParams(vmem_limit_bytes=12 * MIB),
         name="late_finish",
-    )(core, mine, other, early)
+    )(core, *on_chip([mine, other, early]))
 
 
 def sum_over_rest(total):

time: 330 us -> 315 us (0.955)
  Pallas kernels: 175 us -> 155 us
  waiting for transfers between devices: 94.7 us -> 106 us
  local copies, waits for them, and re-layouts: 11.2 us -> 2.36 us
  starting transfers between devices: 36.5 us -> 40.9 us
    unnamed x56 -> x60, local copies, waits for them, and re-layouts: 9.66 us -> 2.08 us
    all_to_all x4, waiting for transfers between devices: 38.3 us -> 45 us  [exchange(): return lax.all_to_all(values, 'sp', split_axis=0, concat_axis=0, tiled=True)]
    ppermute x24, waiting for transfers between devices: 56.4 us -> 61.1 us  [pair_permute(): return lax.ppermute(value, axis, [(i, i ^ bit) for i in range(n)])]
    ppermute x24, starting transfers between devices: 18.4 us -> 21.8 us  [pair_permute(): return lax.ppermute(value, axis, [(i, i ^ bit) for i in range(n)])]
    pallas_call x1, Pallas kernels: 8.84 us -> 5.45 us  [late_grads(): pl.pallas_call(functools.partial(late_grads_kernel, parts=n), grid_spec=p...]
    pallas_call x2, Pallas kernels: 4.61 us -> 1.27 us  [four_chips(): pl.pallas_call(functools.partial(four_chips_kernel, crossed=crossed), in_...]
  transfers between devices with their start and end apart: 28 -> 28, of which waited for: 15 -> 18; matrix products, arithmetic and copies ran while one was open for 3% -> 3% of each run, Pallas kernels for 36% -> 33%
where the time goes in v3:
time: 315 us
  Pallas kernels  155 us (49%)
  waiting for transfers between devices  106 us (34%)
  starting transfers between devices  40.9 us (13%)
  other arithmetic  8.68 us (3%)
    ppermute x24, waiting for transfers between devices, pair_permute(): return lax.ppermute(value, axis, [(i, i ^ bit) for i in range(n)])  61.1 us
    all_to_all x4, waiting for transfers between devices, exchange(): return lax.all_to_all(values, 'sp', split_axis=0, concat_axis=0, tiled=True)  45 us
    pallas_call x1, Pallas kernels, attention_backward(): pl.pallas_call(functools.partial(attention_backward_kernel, pairs=pairs),...  40.5 us
    pallas_call x1, Pallas kernels, feed_forward(): pl.pallas_call(mlp_kernel, grid=(length // rows,), in_specs=[block, block...  35.6 us
    ppermute x24, starting transfers between devices, pair_permute(): return lax.ppermute(value, axis, [(i, i ^ bit) for i in range(n)])  21.8 us
    pallas_call x1, Pallas kernels, attention_forward(): pl.pallas_call(functools.partial(attention_forward_kernel, chunk=length /...  19.7 us
    all_to_all x4, starting transfers between devices, exchange(): return lax.all_to_all(values, 'sp', split_axis=0, concat_axis=0, tiled=True)  19.1 us
    pallas_call x1, Pallas kernels, column_grad(): pl.pallas_call(functools.partial(column_grad_kernel, blocks=n), grid_spec...  11.9 us
  transfers between devices with their start and end apart: 28, of which 18 were waited for; matrix products, arithmetic and copies ran while one was open for 3% of the time, Pallas kernels for 33%

profile of v3, /device:TPU:0, one launch (start us, length us, event | category | flops | bytes accessed | tf_op | source)
XLA Modules:
  0.0 314.7 jit_solution(15897141343902687299)
XLA Ops:
  0.7 6.5 %all-to-all-start = ((bf16[4,256,768]{2,1,0:T(8,128)(2,1)}), bf16[4,256,768]{2,1,0:T(8,128)(2,1)S(1)}, u32[]{:S(2)}, u32[]{:S(2)}) async-start(bf16[4,256,768]{2,1,0:T(8,128)(2,1)} %param.13), calls=%async_computation | async-start | bytes 3145728 | tf_op jit(solution)/shard_map/all_to_all | solution.py:888
  8.1 3.1 multiply_sine_fusion
  11.1 33.0 %all-to-all-done = bf16[4,256,768]{2,1,0:T(8,128)(2,1)S(1)} async-done(((bf16[4,256,768]{2,1,0:T(8,128)(2,1)}), bf16[4,256,768]{2,1,0:T(8,128)(2,1)S(1)}, u32[]{:S(2)}, u32[]{:S(2)}) %all-to-all-start) | async-done | bytes 1572896 | tf_op jit(solution)/shard_map/all_to_all | solution.py:888
  45.3 4.3 %all-to-all-start.1 = ((bf16[4,256,768]{2,1,0:T(8,128)(2,1)}), bf16[4,256,768]{2,1,0:T(8,128)(2,1)}, u32[]{:S(2)}, u32[]{:S(2)}) async-start(bf16[4,256,768]{2,1,0:T(8,128)(2,1)} %param.25), calls=%async_computation.1 | async-start | bytes 3145728 | tf_op jit(solution)/shard_map/all_to_all | solution.py:888
  49.6 8.6 %project_qkv.1 = (bf16[1024,768]{1,0:T(8,128)(2,1)}, bf16[1024,768]{1,0:T(8,128)(2,1)}, bf16[1024,768]{1,0:T(8,128)(2,1)}, bf16[1024,768]{1,0:T(8,128)(2,1)}) custom-call(bf16[1024,768]{1,0:T(8,128)(2,1)} %bitcast.42, f32[8,768]{1,0:T(8,128)S(1)} %get-tuple-element.108.mod_ref, bf16[768,2304]{1,0:T(8,128)(2,1)} %w_ref.3, ...), custom_call_target="tpu_custom_call" | custom-call | flops 40000000000 | bytes 100000000 | tf_op jit(solution)/shard_map/project_qkv/pallas_call | solution.py:99
  58.2 19.7 %attention_forward.1 = (bf16[1024,768]{1,0:T(8,128)(2,1)}, f32[6,2,1024]{2,1,0:T(2,128)}) custom-call(bf16[1024,768]{1,0:T(8,128)(2,1)} %get-tuple-element.109.q_ref, bf16[1024,768]{1,0:T(8,128)(2,1)} %get-tuple-element.110.k_ref, bf16[1024,768]{1,0:T(8,128)(2,1)} %get-tuple-element.111.v_ref), custom_call_target="tpu_custom_call" | custom-call | flops 40000000000 | bytes 100000000 | tf_op jit(solution)/shard_map/attention_forward/pallas_call | solution.py:151
  77.9 8.2 %all-to-all-done.1 = bf16[4,256,768]{2,1,0:T(8,128)(2,1)} async-done(((bf16[4,256,768]{2,1,0:T(8,128)(2,1)}), bf16[4,256,768]{2,1,0:T(8,128)(2,1)}, u32[]{:S(2)}, u32[]{:S(2)}) %all-to-all-start.1) | async-done | bytes 1572896 | tf_op jit(solution)/shard_map/all_to_all | solution.py:888
  86.2 35.6 %feed_forward.1 = (bf16[2,1024,768]{2,1,0:T(8,128)(2,1)}, bf16[1024,3072]{1,0:T(8,128)(2,1)}, bf16[1024,768]{1,0:T(8,128)(2,1)}, bf16[5,1024,768]{2,1,0:T(8,128)...) custom-call(bf16[1024,768]{1,0:T(8,128)(2,1)S(1)} %bitcast.43, ...), custom_call_target="tpu_custom_call" | custom-call | flops 40000000000 | bytes 100000000 | tf_op jit(solution)/shard_map/feed_forward/pallas_call | solution.py:335
  121.8 11.9 %column_grad.1 = (bf16[4,576,768]{2,1,0:T(8,128)(2,1)}, bf16[4,576,768]{2,1,0:T(8,128)(2,1)}, f32[4,768]{1,0:T(4,128)S(1)}) custom-call(s32[1]{0:T(128)} %bitcast.6.core_ref, f32[8,768]{1,0:T(8,128)S(1)} %get-tuple-element.117.sum_ref, f32[1,3072]{1,0:T(1,128)S(1)} %get-tuple-element.118.up_sum_ref, f32[8,768]{1,0:T(8,128)S(1)} %get-tuple-element.119.mod_ref, ...), custom_call_target="tpu_custom_call" | custom-call | flops 40000000000 | bytes 100000000 | tf_op jit(solution)/shard_map/column_grad/pallas_call | solution.py:523
  133.6 9.2 %row_grad.1 = (bf16[4,384,768]{2,1,0:T(8,128)(2,1)}, bf16[4,384,768]{2,1,0:T(8,128)(2,1)}) custom-call(s32[1]{0:T(128)} %bitcast.6.core_ref, bf16[1024,3072]{1,0:T(8,128)(2,1)} %get-tuple-element.124.a_ref, bf16[1024,768]{1,0:T(8,128)(2,1)} %get-tuple-element.125.b_ref), custom_call_target="tpu_custom_call" | custom-call | flops 40000000000 | bytes 100000000 | tf_op jit(solution)/shard_map/row_grad/pallas_call | solution.py:454
  143.3 3.6 %all-to-all-start.2 = ((bf16[4,256,768]{2,1,0:T(8,128)(2,1)}), bf16[4,256,768]{2,1,0:T(8,128)(2,1)S(1)}, u32[]{:S(2)}, u32[]{:S(2)}) async-start(bf16[4,256,768]{2,1,0:T(8,128)(2,1)} %bitcast.54), calls=%async_computation.2 | async-start | bytes 3145728 | tf_op jit(solution)/shard_map/all_to_all | solution.py:888
  147.9 8.8 %first_halves.1 = (bf16[4,480,384]{2,1,0:T(8,128)(2,1)}, bf16[4,480,384]{2,1,0:T(8,128)(2,1)}, bf16[4,480,384]{2,1,0:T(8,128)(2,1)}, bf16[4,480,384]{2,1,0:T(8,128)(2,1)}) custom-call(s32[3]{0:T(128)S(1)} %pad_add_fusion.at_ref, bf16[4,384,768]{2,1,0:T(8,128)(2,1)} %get-tuple-element.126.row_keep, bf16[4,384,768]{2,1,0:T(8,128)(2,1)} %collective-permute-done.row_got, ...), custom_call_target="tpu_custom_call" | custom-call | flops 40000000000 | bytes 100000000 | tf_op jit(solution)/shard_map/first_halves/pallas_call | solution.py:594
  159.8 40.5 %attention_backward.1 = (bf16[3,1024,768]{2,1,0:T(8,128)(2,1)}, bf16[1024,768]{1,0:T(8,128)(2,1)}, f32[8,768]{1,0:T(8,128)S(1)}) custom-call(bf16[1024,768]{1,0:T(8,128)(2,1)S(1)} %copy-done.13, bf16[1024,768]{1,0:T(8,128)(2,1)S(1)} %copy-done.14, bf16[1024,768]{1,0:T(8,128)(2,1)S(1)} %copy-done.15, bf16[1024,768]{1,0:T(8,128)(2,1)S(1)} %copy-done.17, ...), custom_call_target="tpu_custom_call" | custom-call | flops 40000000000 | bytes 100000000 | tf_op jit(solution)/shard_map/attention_backward/pallas_call | solution.py:237
  200.3 4.7 %all-to-all-start.3 = ((bf16[4,256,768]{2,1,0:T(8,128)(2,1)}), bf16[4,256,768]{2,1,0:T(8,128)(2,1)}, u32[]{:S(2)}, u32[]{:S(2)}) async-start(bf16[4,256,768]{2,1,0:T(8,128)(2,1)} %bitcast.55), calls=%async_computation.3 | async-start | bytes 3145728 | tf_op jit(solution)/shard_map/all_to_all | solution.py:888
  205.1 3.6 %second_halves.1 = (bf16[4,240,384]{2,1,0:T(8,128)(2,1)S(1)}, bf16[4,240,384]{2,1,0:T(8,128)(2,1)S(1)}, bf16[4,240,384]{2,1,0:T(8,128)(2,1)S(1)}, bf16[4,240,384]{2,1,0:T(8,128)(2,1)S(1)}) custom-call(s32[3]{0:T(128)S(1)} %pad_add_fusion.at_ref, bf16[4,2,240,384]{3,2,1,0:T(8,128)(2,1)} %bitcast.56, bf16[4,2,240,384]{3,2,1,0:T(8,128)(2,1)} %bitcast.12.refs_1_, ...), custom_call_target="tpu_custom_call" | custom-call | flops 40000000000 | bytes 100000000 | tf_op jit(solution)/shard_map/second_halves/pallas_call | solution.py:621
  210.9 5.4 %late_grads.1 = (bf16[1,128]{1,0:T(2,128)(2,1)S(1)}, bf16[4,384,768]{2,1,0:T(8,128)(2,1)S(1)}, bf16[4,384,768]{2,1,0:T(8,128)(2,1)S(1)}) custom-call(s32[1]{0:T(128)} %bitcast.6.core_ref, f32[8,768]{1,0:T(8,128)S(1)} %get-tuple-element.140.sum_ref, f32[8,768]{1,0:T(8,128)S(1)} %get-tuple-element.141.mod_ref, bf16[128,4608]{1,0:T(8,128)(2,1)S(1)} %copy-done.3, ...), custom_call_target="tpu_custom_call" | custom-call | flops 40000000000 | bytes 100000000 | tf_op jit(solution)/shard_map/late_grads/pallas_call | solution.py:415
  216.4 10.5 %collective-permute-done.5.refs_1_ = bf16[4,240,384]{2,1,0:T(8,128)(2,1)S(1)} collective-permute-done((bf16[4,240,384]{2,1,0:T(8,128)(2,1)S(1)}, bf16[4,240,384]{2,1,0:T(8,128)(2,1)S(1)}, u32[]{:S(2)}, u32[]{:S(2)}) %collective-permute-start.5) | collective-permute-done | bytes 737312 | tf_op jit(solution)/shard_map/ppermute | solution.py:549
  230.3 2.1 quarters.1
  238.4 3.8 %all-to-all-done.3 = bf16[4,256,768]{2,1,0:T(8,128)(2,1)} async-done(((bf16[4,256,768]{2,1,0:T(8,128)(2,1)}), bf16[4,256,768]{2,1,0:T(8,128)(2,1)}, u32[]{:S(2)}, u32[]{:S(2)}) %all-to-all-start.3) | async-done | bytes 1572896 | tf_op jit(solution)/shard_map/all_to_all | solution.py:888
  242.2 11.8 %collective-permute-done.7 = bf16[2,240,768]{2,1,0:T(8,128)(2,1)} collective-permute-done((bf16[2,240,768]{2,1,0:T(8,128)(2,1)S(1)}, bf16[2,240,768]{2,1,0:T(8,128)(2,1)}, u32[]{:S(2)}, u32[]{:S(2)}) %collective-permute-start.7) | collective-permute-done | bytes 737312 | tf_op jit(solution)/shard_map/ppermute | solution.py:549
  256.7 4.4 %collective-permute-done.8.refs_1_ = bf16[4,96,768]{2,1,0:T(8,128)(2,1)} collective-permute-done((bf16[4,96,768]{2,1,0:T(8,128)(2,1)}, bf16[4,96,768]{2,1,0:T(8,128)(2,1)}, u32[]{:S(2)}, u32[]{:S(2)}) %collective-permute-start.8) | collective-permute-done | bytes 589856 | tf_op jit(solution)/shard_map/ppermute | solution.py:549
  261.1 1.7 near_halves.3
  263.7 9.4 %collective-permute-done.12 = bf16[240,768]{1,0:T(8,128)(2,1)S(1)} collective-permute-done((bf16[240,768]{1,0:T(8,128)(2,1)S(1)}, bf16[240,768]{1,0:T(8,128)(2,1)S(1)}, u32[]{:S(2)}, u32[]{:S(2)}) %collective-permute-start.12) | collective-permute-done | bytes 368672 | tf_op jit(solution)/shard_map/ppermute | solution.py:549
  273.2 5.7 %collective-permute-done.11 = bf16[2,96,768]{2,1,0:T(8,128)(2,1)S(1)} collective-permute-done((bf16[2,96,768]{2,1,0:T(8,128)(2,1)S(1)}, bf16[2,96,768]{2,1,0:T(8,128)(2,1)S(1)}, u32[]{:S(2)}, u32[]{:S(2)}) %collective-permute-start.11) | collective-permute-done | bytes 294944 | tf_op jit(solution)/shard_map/ppermute | solution.py:549
  280.2 1.7 collective-permute-start.17
  283.2 5.2 %collective-permute-done.13 = bf16[96,768]{1,0:T(8,128)(2,1)S(1)} collective-permute-done((bf16[96,768]{1,0:T(8,128)(2,1)S(1)}, bf16[96,768]{1,0:T(8,128)(2,1)S(1)}, u32[]{:S(2)}, u32[]{:S(2)}) %collective-permute-start.13) | collective-permute-done | bytes 147488 | tf_op jit(solution)/shard_map/ppermute | solution.py:549
  288.5 3.5 %collective-permute-done.14 = bf16[1,128]{1,0:T(2,128)(2,1)S(1)} collective-permute-done((bf16[1,128]{1,0:T(2,128)(2,1)S(1)}, bf16[1,128]{1,0:T(2,128)(2,1)S(1)}, u32[]{:S(2)}, u32[]{:S(2)}) %collective-permute-start.14) | collective-permute-done | bytes 288 | tf_op jit(solution)/shard_map/ppermute | solution.py:549
  292.8 3.3 %convert_element_type.142 = f32[4,256,768]{2,1,0:T(8,128)} convert(bf16[4,256,768]{2,1,0:T(8,128)(2,1)} %all-to-all-done.3) | non-fusion elementwise | flops 786432 | bytes 4718592 | tf_op jit(solution)/shard_map/convert_element_type | solution.py:1001
  296.6 2.4 collective-permute-done.18.refs_3_
  300.4 1.7 collective-permute-start.20
  303.4 2.6 finish.1
  307.0 3.4 %collective-permute-done.21.refs_3_ = bf16[96,768]{1,0:T(8,128)(2,1)S(1)} collective-permute-done((bf16[96,768]{1,0:T(8,128)(2,1)S(1)}, bf16[96,768]{1,0:T(8,128)(2,1)S(1)}, u32[]{:S(2)}, u32[]{:S(2)}) %collective-permute-start.21) | collective-permute-done | bytes 147488 | tf_op jit(solution)/shard_map/ppermute | solution.py:549
  (130 shorter events, 33.6 us)
Async XLA Ops:
  0.7 43.4 %all-to-all-start = ((bf16[4,256,768]{2,1,0:T(8,128)(2,1)}), bf16[4,256,768]{2,1,0:T(8,128)(2,1)S(1)}, u32[]{:S(2)}, u32[]{:S(2)}) async-start(bf16[4,256,768]{2,1,0:T(8,128)(2,1)} %param.13), calls=%async_computation | async-start | bytes 3145728 | tf_op jit(solution)/shard_map/all_to_all | solution.py:888
  7.9 41.7 %copy-start.8 = (f32[8,768]{1,0:T(8,128)}, f32[8,768]{1,0:T(8,128)S(1)}, u32[]{:S(2)}) copy-start(f32[8,768]{1,0:T(8,128)S(1)} %get-tuple-element.108.mod_ref) | copy-start | bytes 73732
  8.1 113.7 %copy-start.6 = (f32[128,1]{1,0:T(8,128)}, f32[128,1]{1,0:T(8,128)S(1)}, u32[]{:S(2)}) copy-start(f32[128,1]{1,0:T(8,128)S(1)} %copy.26.timing_ref) | copy-start | bytes 1540
  45.3 40.9 %all-to-all-start.1 = ((bf16[4,256,768]{2,1,0:T(8,128)(2,1)}), bf16[4,256,768]{2,1,0:T(8,128)(2,1)}, u32[]{:S(2)}, u32[]{:S(2)}) async-start(bf16[4,256,768]{2,1,0:T(8,128)(2,1)} %param.25), calls=%async_computation.1 | async-start | bytes 3145728 | tf_op jit(solution)/shard_map/all_to_all | solution.py:888
  58.2 27.9 %copy-start.1 = (bf16[4,256,768]{2,1,0:T(8,128)(2,1)S(1)}, bf16[4,256,768]{2,1,0:T(8,128)(2,1)}, u32[]{:S(2)}) copy-start(bf16[4,256,768]{2,1,0:T(8,128)(2,1)} %copy-done) | copy-start | bytes 4718596
  58.2 27.9 %copy-start.11 = (bf16[768,768]{1,0:T(8,128)(2,1)S(1)}, bf16[768,768]{1,0:T(8,128)(2,1)}, u32[]{:S(2)}) copy-start(bf16[768,768]{1,0:T(8,128)(2,1)} %wo_ref.1) | copy-start | bytes 3538948
  133.6 14.2 %collective-permute-start.1 = (bf16[4,576,768]{2,1,0:T(8,128)(2,1)}, bf16[4,576,768]{2,1,0:T(8,128)(2,1)}, u32[]{:S(2)}, u32[]{:S(2)}) collective-permute-start(bf16[4,576,768]{2,1,0:T(8,128)(2,1)} %get-tuple-element.128), channel_id=1, source_target_pairs={{0,4},{4,0},{8,12},{12,8},{16,20},{20,16},{24,28},{28,24},{1,5},{5... | collective-permute-start | bytes 10616840 | tf_op jit(solution)/shard_map/ppermute | solution.py:549
  142.8 5.0 %collective-permute-start = (bf16[4,384,768]{2,1,0:T(8,128)(2,1)}, bf16[4,384,768]{2,1,0:T(8,128)(2,1)}, u32[]{:S(2)}, u32[]{:S(2)}) collective-permute-start(bf16[4,384,768]{2,1,0:T(8,128)(2,1)} %get-tuple-element.127), channel_id=1, source_target_pairs={{0,4},{4,0},{8,12},{12,8},{16,20},{20,16},{24,28},{28,24},{1,5},{5... | collective-permute-start | bytes 7077896 | tf_op jit(solution)/shard_map/ppermute | solution.py:549
  143.3 57.1 %all-to-all-start.2 = ((bf16[4,256,768]{2,1,0:T(8,128)(2,1)}), bf16[4,256,768]{2,1,0:T(8,128)(2,1)S(1)}, u32[]{:S(2)}, u32[]{:S(2)}) async-start(bf16[4,256,768]{2,1,0:T(8,128)(2,1)} %bitcast.54), calls=%async_computation.2 | async-start | bytes 3145728 | tf_op jit(solution)/shard_map/all_to_all | solution.py:888
  156.7 48.3 %collective-permute-start.2 = (bf16[4,480,384]{2,1,0:T(8,128)(2,1)}, bf16[4,480,384]{2,1,0:T(8,128)(2,1)}, u32[]{:S(2)}, u32[]{:S(2)}) collective-permute-start(bf16[4,480,384]{2,1,0:T(8,128)(2,1)} %get-tuple-element.129), channel_id=1, source_target_pairs={{0,8},{4,12},{8,0},{12,4},{16,24},{20,28},{24,16},{28,20},{1,9},{5... | collective-permute-start | bytes 4423688 | tf_op jit(solution)/shard_map/ppermute | solution.py:549
  158.2 46.8 %collective-permute-start.3 = (bf16[4,480,384]{2,1,0:T(8,128)(2,1)}, bf16[4,480,384]{2,1,0:T(8,128)(2,1)}, u32[]{:S(2)}, u32[]{:S(2)}) collective-permute-start(bf16[4,480,384]{2,1,0:T(8,128)(2,1)} %get-tuple-element.130), channel_id=1, source_target_pairs={{0,16},{4,20},{8,24},{12,28},{16,0},{20,4},{24,8},{28,12},{1,17},{... | collective-permute-start | bytes 4423688 | tf_op jit(solution)/shard_map/ppermute | solution.py:549
  200.3 41.8 %all-to-all-start.3 = ((bf16[4,256,768]{2,1,0:T(8,128)(2,1)}), bf16[4,256,768]{2,1,0:T(8,128)(2,1)}, u32[]{:S(2)}, u32[]{:S(2)}) async-start(bf16[4,256,768]{2,1,0:T(8,128)(2,1)} %bitcast.55), calls=%async_computation.3 | async-start | bytes 3145728 | tf_op jit(solution)/shard_map/all_to_all | solution.py:888
  208.7 18.3 %collective-permute-start.5 = (bf16[4,240,384]{2,1,0:T(8,128)(2,1)S(1)}, bf16[4,240,384]{2,1,0:T(8,128)(2,1)S(1)}, u32[]{:S(2)}, u32[]{:S(2)}) collective-permute-start(bf16[4,240,384]{2,1,0:T(8,128)(2,1)S(1)} %get-tuple-element.151), channel_id=1, source_target_pairs={{0,16},{4,20},{8,24},{12,28},{16,0},{20,4},{24,8},{28,12},{1,17},{... | collective-permute-start | bytes 2211848 | tf_op jit(solution)/shard_map/ppermute | solution.py:549
  209.4 18.5 %collective-permute-start.6 = (bf16[4,240,384]{2,1,0:T(8,128)(2,1)S(1)}, bf16[4,240,384]{2,1,0:T(8,128)(2,1)S(1)}, u32[]{:S(2)}, u32[]{:S(2)}) collective-permute-start(bf16[4,240,384]{2,1,0:T(8,128)(2,1)S(1)} %get-tuple-element.152), channel_id=1, source_target_pairs={{0,8},{4,12},{8,0},{12,4},{16,24},{20,28},{24,16},{28,20},{1,9},{5... | collective-permute-start | bytes 2211848 | tf_op jit(solution)/shard_map/ppermute | solution.py:549
  216.4 14.0 %collective-permute-start.4 = (bf16[4,384,768]{2,1,0:T(8,128)(2,1)S(1)}, bf16[4,384,768]{2,1,0:T(8,128)(2,1)S(1)}, u32[]{:S(2)}, u32[]{:S(2)}) collective-permute-start(bf16[4,384,768]{2,1,0:T(8,128)(2,1)S(1)} %get-tuple-element.150), channel_id=1, source_target_pairs={{0,4},{4,0},{8,12},{12,8},{16,20},{20,16},{24,28},{28,24},{1,5},{5... | collective-permute-start | bytes 7077896 | tf_op jit(solution)/shard_map/ppermute | solution.py:549
  228.8 25.2 %collective-permute-start.7 = (bf16[2,240,768]{2,1,0:T(8,128)(2,1)S(1)}, bf16[2,240,768]{2,1,0:T(8,128)(2,1)}, u32[]{:S(2)}, u32[]{:S(2)}) collective-permute-start(bf16[2,240,768]{2,1,0:T(8,128)(2,1)S(1)} %get-tuple-element.159), channel_id=1, source_target_pairs={{0,1},{1,0},{2,3},{3,2},{4,5},{5,4},{6,7},{7,6},{8,9},{9,8},{10,11... | collective-permute-start | bytes 2211848 | tf_op jit(solution)/shard_map/ppermute | solution.py:549
  233.3 23.4 %collective-permute-start.10 = (bf16[4,96,768]{2,1,0:T(8,128)(2,1)}, bf16[4,96,768]{2,1,0:T(8,128)(2,1)}, u32[]{:S(2)}, u32[]{:S(2)}) collective-permute-start(bf16[4,96,768]{2,1,0:T(8,128)(2,1)} %get-tuple-element.164), channel_id=1, source_target_pairs={{0,24},{4,28},{8,16},{12,20},{16,8},{20,12},{24,0},{28,4},{1,25},{... | collective-permute-start | bytes 1769480 | tf_op jit(solution)/shard_map/ppermute | solution.py:549
  234.7 26.4 %collective-permute-start.8 = (bf16[4,96,768]{2,1,0:T(8,128)(2,1)}, bf16[4,96,768]{2,1,0:T(8,128)(2,1)}, u32[]{:S(2)}, u32[]{:S(2)}) collective-permute-start(bf16[4,96,768]{2,1,0:T(8,128)(2,1)} %get-tuple-element.162), channel_id=1, source_target_pairs={{0,16},{4,20},{8,24},{12,28},{16,0},{20,4},{24,8},{28,12},{1,17},{... | collective-permute-start | bytes 1769480 | tf_op jit(solution)/shard_map/ppermute | solution.py:549
  236.2 24.9 %collective-permute-start.9 = (bf16[4,96,768]{2,1,0:T(8,128)(2,1)}, bf16[4,96,768]{2,1,0:T(8,128)(2,1)}, u32[]{:S(2)}, u32[]{:S(2)}) collective-permute-start(bf16[4,96,768]{2,1,0:T(8,128)(2,1)} %get-tuple-element.163), channel_id=1, source_target_pairs={{0,8},{4,12},{8,0},{12,4},{16,24},{20,28},{24,16},{28,20},{1,9},{5... | collective-permute-start | bytes 1769480 | tf_op jit(solution)/shard_map/ppermute | solution.py:549
  255.3 17.8 %collective-permute-start.12 = (bf16[240,768]{1,0:T(8,128)(2,1)S(1)}, bf16[240,768]{1,0:T(8,128)(2,1)S(1)}, u32[]{:S(2)}, u32[]{:S(2)}) collective-permute-start(bf16[240,768]{1,0:T(8,128)(2,1)S(1)} %get-tuple-element.199), channel_id=1, source_target_pairs={{0,2},{1,3},{2,0},{3,1},{4,6},{5,7},{6,4},{7,5},{8,10},{9,11},{10,... | collective-permute-start | bytes 1105928 | tf_op jit(solution)/shard_map/ppermute | solution.py:549
  262.8 16.0 %collective-permute-start.11 = (bf16[2,96,768]{2,1,0:T(8,128)(2,1)S(1)}, bf16[2,96,768]{2,1,0:T(8,128)(2,1)S(1)}, u32[]{:S(2)}, u32[]{:S(2)}) collective-permute-start(bf16[2,96,768]{2,1,0:T(8,128)(2,1)S(1)} %get-tuple-element.172), channel_id=1, source_target_pairs={{0,1},{1,0},{2,3},{3,2},{4,5},{5,4},{6,7},{7,6},{8,9},{9,8},{10,11... | collective-permute-start | bytes 884744 | tf_op jit(solution)/shard_map/ppermute | solution.py:549
  278.9 9.5 %collective-permute-start.13 = (bf16[96,768]{1,0:T(8,128)(2,1)S(1)}, bf16[96,768]{1,0:T(8,128)(2,1)S(1)}, u32[]{:S(2)}, u32[]{:S(2)}) collective-permute-start(bf16[96,768]{1,0:T(8,128)(2,1)S(1)} %fusion.4), channel_id=1, source_target_pairs={{0,2},{1,3},{2,0},{3,1},{4,6},{5,7},{6,4},{7,5},{8,10},{9,11},{10,... | collective-permute-start | bytes 442376 | tf_op jit(solution)/shard_map/ppermute | solution.py:549
  279.7 16.9 %collective-permute-start.16 = (bf16[240,768]{1,0:T(8,128)(2,1)S(1)}, bf16[240,768]{1,0:T(8,128)(2,1)S(1)}, u32[]{:S(2)}, u32[]{:S(2)}) collective-permute-start(bf16[240,768]{1,0:T(8,128)(2,1)S(1)} %add_convert_fusion.refs_0_), channel_id=1, source_target_pairs={{0,16},{4,20},{8,24},{12,28},{16,0},{20,4},{24,8},{28,12},{1,17},{... | collective-permute-start | bytes 1105928 | tf_op jit(solution)/shard_map/ppermute | solution.py:549
  280.2 16.4 %collective-permute-start.17 = (bf16[240,768]{1,0:T(8,128)(2,1)S(1)}, bf16[240,768]{1,0:T(8,128)(2,1)S(1)}, u32[]{:S(2)}, u32[]{:S(2)}) collective-permute-start(bf16[240,768]{1,0:T(8,128)(2,1)S(1)} %add_convert_fusion.refs_0_), channel_id=1, source_target_pairs={{0,8},{4,12},{8,0},{12,4},{16,24},{20,28},{24,16},{28,20},{1,9},{5... | collective-permute-start | bytes 1105928 | tf_op jit(solution)/shard_map/ppermute | solution.py:549
  281.9 17.1 %collective-permute-start.18 = (bf16[240,768]{1,0:T(8,128)(2,1)S(1)}, bf16[240,768]{1,0:T(8,128)(2,1)S(1)}, u32[]{:S(2)}, u32[]{:S(2)}) collective-permute-start(bf16[240,768]{1,0:T(8,128)(2,1)S(1)} %add_convert_fusion.refs_0_), channel_id=1, source_target_pairs={{0,24},{4,28},{8,16},{12,20},{16,8},{20,12},{24,0},{28,4},{1,25},{... | collective-permute-start | bytes 1105928 | tf_op jit(solution)/shard_map/ppermute | solution.py:549
  288.5 3.6 %collective-permute-start.14 = (bf16[1,128]{1,0:T(2,128)(2,1)S(1)}, bf16[1,128]{1,0:T(2,128)(2,1)S(1)}, u32[]{:S(2)}, u32[]{:S(2)}) collective-permute-start(bf16[1,128]{1,0:T(2,128)(2,1)S(1)} %get-tuple-element.177), channel_id=1, source_target_pairs={{0,1},{1,0},{2,3},{3,2},{4,5},{5,4},{6,7},{7,6},{8,9},{9,8},{10,11... | collective-permute-start | bytes 776 | tf_op jit(solution)/shard_map/ppermute | solution.py:549
  292.1 4.5 %collective-permute-start.15 = (bf16[2,128]{1,0:T(2,128)(2,1)S(1)}, bf16[2,128]{1,0:T(2,128)(2,1)S(1)}, u32[]{:S(2)}, u32[]{:S(2)}) collective-permute-start(bf16[2,128]{1,0:T(2,128)(2,1)S(1)} %pad_maximum_fusion.1), channel_id=1, source_target_pairs={{0,2},{1,3},{2,0},{3,1},{4,6},{5,7},{6,4},{7,5},{8,10},{9,11},{10,... | collective-permute-start | bytes 1544 | tf_op jit(solution)/shard_map/ppermute | solution.py:549
  299.7 3.6 %collective-permute-start.22 = (bf16[960,768]{1,0:T(8,128)(2,1)S(1)}, bf16[960,768]{1,0:T(8,128)(2,1)S(1)}, u32[]{:S(2)}, u32[]{:S(2)}) collective-permute-start(bf16[960,768]{1,0:T(8,128)(2,1)S(1)} %bitcast.47), channel_id=1, source_target_pairs={{0,4},{4,0},{8,12},{12,8},{16,20},{20,16},{24,28},{28,24},{1,5},{5... | collective-permute-start | bytes 4423688 | tf_op jit(solution)/shard_map/ppermute | solution.py:549
  299.8 6.3 %collective-permute-start.19 = (bf16[96,768]{1,0:T(8,128)(2,1)S(1)}, bf16[96,768]{1,0:T(8,128)(2,1)S(1)}, u32[]{:S(2)}, u32[]{:S(2)}) collective-permute-start(bf16[96,768]{1,0:T(8,128)(2,1)S(1)} %fusion.2.refs_0_), channel_id=1, source_target_pairs={{0,16},{4,20},{8,24},{12,28},{16,0},{20,4},{24,8},{28,12},{1,17},{... | collective-permute-start | bytes 442376 | tf_op jit(solution)/shard_map/ppermute | solution.py:549
  300.4 6.7 %collective-permute-start.20 = (bf16[96,768]{1,0:T(8,128)(2,1)S(1)}, bf16[96,768]{1,0:T(8,128)(2,1)S(1)}, u32[]{:S(2)}, u32[]{:S(2)}) collective-permute-start(bf16[96,768]{1,0:T(8,128)(2,1)S(1)} %fusion.2.refs_0_), channel_id=1, source_target_pairs={{0,8},{4,12},{8,0},{12,4},{16,24},{20,28},{24,16},{28,20},{1,9},{5... | collective-permute-start | bytes 442376 | tf_op jit(solution)/shard_map/ppermute | solution.py:549
  302.1 8.3 %collective-permute-start.21 = (bf16[96,768]{1,0:T(8,128)(2,1)S(1)}, bf16[96,768]{1,0:T(8,128)(2,1)S(1)}, u32[]{:S(2)}, u32[]{:S(2)}) collective-permute-start(bf16[96,768]{1,0:T(8,128)(2,1)S(1)} %fusion.2.refs_0_), channel_id=1, source_target_pairs={{0,24},{4,28},{8,16},{12,20},{16,8},{20,12},{24,0},{28,4},{1,25},{... | collective-permute-start | bytes 442376 | tf_op jit(solution)/shard_map/ppermute | solution.py:549
  311.0 2.1 collective-permute-start.23
  (26 other events, 230.9 us)

commit v4 on v3

--- a/solution.py
+++ b/solution.py
@@ -111,7 +111,7 @@
         cost_estimate=COVER,
         compiler_params=pltpu.CompilerParams(vmem_limit_bytes=18 * MIB),
         name="project_qkv",
-    )(*streamed(x), mods, *streamed(weight, cos, sin))
+    )(x, mods, *streamed(weight, cos, sin))
 
 
 def attention_forward_kernel(q_ref, k_ref, v_ref, o_ref, lse_ref, *, chunk, ahead):

time: 315 us -> 314 us (level)
  no operation moved by 1% of the time
where the time goes in v4:
time: 314 us
  Pallas kernels  155 us (49%)
  waiting for transfers between devices  106 us (34%)
  starting transfers between devices  41 us (13%)
  other arithmetic  8.68 us (3%)
    ppermute x24, waiting for transfers between devices, pair_permute(): return lax.ppermute(value, axis, [(i, i ^ bit) for i in range(n)])  61 us
    all_to_all x4, waiting for transfers between devices, exchange(): return lax.all_to_all(values, 'sp', split_axis=0, concat_axis=0, tiled=True)  45 us
    pallas_call x1, Pallas kernels, attention_backward(): pl.pallas_call(functools.partial(attention_backward_kernel, pairs=pairs),...  40.5 us
    pallas_call x1, Pallas kernels, feed_forward(): pl.pallas_call(mlp_kernel, grid=(length // rows,), in_specs=[block, block...  35.6 us
    ppermute x24, starting transfers between devices, pair_permute(): return lax.ppermute(value, axis, [(i, i ^ bit) for i in range(n)])  21.9 us
    pallas_call x1, Pallas kernels, attention_forward(): pl.pallas_call(functools.partial(attention_forward_kernel, chunk=length /...  19.6 us
    all_to_all x4, starting transfers between devices, exchange(): return lax.all_to_all(values, 'sp', split_axis=0, concat_axis=0, tiled=True)  19.1 us
    pallas_call x1, Pallas kernels, column_grad(): pl.pallas_call(functools.partial(column_grad_kernel, blocks=n), grid_spec...  11.9 us
  transfers between devices with their start and end apart: 28, of which 18 were waited for; matrix products, arithmetic and copies ran while one was open for 3% of the time, Pallas kernels for 33%

profile of v4, /device:TPU:0, one launch (start us, length us, event | category | flops | bytes accessed | tf_op | source)
XLA Modules:
  0.0 313.7 jit_solution(329095197767297652)
XLA Ops:
  0.7 6.5 %all-to-all-start = ((bf16[4,256,768]{2,1,0:T(8,128)(2,1)}), bf16[4,256,768]{2,1,0:T(8,128)(2,1)S(1)}, u32[]{:S(2)}, u32[]{:S(2)}) async-start(bf16[4,256,768]{2,1,0:T(8,128)(2,1)} %param.13), calls=%async_computation | async-start | bytes 3145728 | tf_op jit(solution)/shard_map/all_to_all | solution.py:888
  8.1 3.1 multiply_sine_fusion
  11.1 33.0 %all-to-all-done = bf16[4,256,768]{2,1,0:T(8,128)(2,1)S(1)} async-done(((bf16[4,256,768]{2,1,0:T(8,128)(2,1)}), bf16[4,256,768]{2,1,0:T(8,128)(2,1)S(1)}, u32[]{:S(2)}, u32[]{:S(2)}) %all-to-all-start) | async-done | bytes 1572896 | tf_op jit(solution)/shard_map/all_to_all | solution.py:888
  44.1 4.4 %all-to-all-start.1 = ((bf16[4,256,768]{2,1,0:T(8,128)(2,1)}), bf16[4,256,768]{2,1,0:T(8,128)(2,1)}, u32[]{:S(2)}, u32[]{:S(2)}) async-start(bf16[4,256,768]{2,1,0:T(8,128)(2,1)} %param.25), calls=%async_computation.1 | async-start | bytes 3145728 | tf_op jit(solution)/shard_map/all_to_all | solution.py:888
  48.5 8.6 %project_qkv.1 = (bf16[1024,768]{1,0:T(8,128)(2,1)}, bf16[1024,768]{1,0:T(8,128)(2,1)}, bf16[1024,768]{1,0:T(8,128)(2,1)}, bf16[1024,768]{1,0:T(8,128)(2,1)}) custom-call(bf16[1024,768]{1,0:T(8,128)(2,1)S(1)} %bitcast.42, f32[8,768]{1,0:T(8,128)S(1)} %get-tuple-element.108.mod_ref, bf16[768,2304]{1,0:T(8,128)(2,1)} %w_ref.3, ...), custom_call_target="tpu_custom_call" | custom-call | flops 40000000000 | bytes 100000000 | tf_op jit(solution)/shard_map/project_qkv/pallas_call | solution.py:99
  57.1 19.6 %attention_forward.1 = (bf16[1024,768]{1,0:T(8,128)(2,1)}, f32[6,2,1024]{2,1,0:T(2,128)}) custom-call(bf16[1024,768]{1,0:T(8,128)(2,1)} %get-tuple-element.109.q_ref, bf16[1024,768]{1,0:T(8,128)(2,1)} %get-tuple-element.110.k_ref, bf16[1024,768]{1,0:T(8,128)(2,1)} %get-tuple-element.111.v_ref), custom_call_target="tpu_custom_call" | custom-call | flops 40000000000 | bytes 100000000 | tf_op jit(solution)/shard_map/attention_forward/pallas_call | solution.py:151
  76.7 8.3 %all-to-all-done.1 = bf16[4,256,768]{2,1,0:T(8,128)(2,1)} async-done(((bf16[4,256,768]{2,1,0:T(8,128)(2,1)}), bf16[4,256,768]{2,1,0:T(8,128)(2,1)}, u32[]{:S(2)}, u32[]{:S(2)}) %all-to-all-start.1) | async-done | bytes 1572896 | tf_op jit(solution)/shard_map/all_to_all | solution.py:888
  85.0 35.6 %feed_forward.1 = (bf16[2,1024,768]{2,1,0:T(8,128)(2,1)}, bf16[1024,3072]{1,0:T(8,128)(2,1)}, bf16[1024,768]{1,0:T(8,128)(2,1)}, bf16[5,1024,768]{2,1,0:T(8,128)...) custom-call(bf16[1024,768]{1,0:T(8,128)(2,1)S(1)} %bitcast.43, ...), custom_call_target="tpu_custom_call" | custom-call | flops 40000000000 | bytes 100000000 | tf_op jit(solution)/shard_map/feed_forward/pallas_call | solution.py:335
  120.6 11.9 %column_grad.1 = (bf16[4,576,768]{2,1,0:T(8,128)(2,1)}, bf16[4,576,768]{2,1,0:T(8,128)(2,1)}, f32[4,768]{1,0:T(4,128)S(1)}) custom-call(s32[1]{0:T(128)} %bitcast.6.core_ref, f32[8,768]{1,0:T(8,128)S(1)} %get-tuple-element.117.sum_ref, f32[1,3072]{1,0:T(1,128)S(1)} %get-tuple-element.118.up_sum_ref, f32[8,768]{1,0:T(8,128)S(1)} %get-tuple-element.119.mod_ref, ...), custom_call_target="tpu_custom_call" | custom-call | flops 40000000000 | bytes 100000000 | tf_op jit(solution)/shard_map/column_grad/pallas_call | solution.py:523
  132.5 9.2 %row_grad.1 = (bf16[4,384,768]{2,1,0:T(8,128)(2,1)}, bf16[4,384,768]{2,1,0:T(8,128)(2,1)}) custom-call(s32[1]{0:T(128)} %bitcast.6.core_ref, bf16[1024,3072]{1,0:T(8,128)(2,1)} %get-tuple-element.124.a_ref, bf16[1024,768]{1,0:T(8,128)(2,1)} %get-tuple-element.125.b_ref), custom_call_target="tpu_custom_call" | custom-call | flops 40000000000 | bytes 100000000 | tf_op jit(solution)/shard_map/row_grad/pallas_call | solution.py:454
  142.2 3.6 %all-to-all-start.2 = ((bf16[4,256,768]{2,1,0:T(8,128)(2,1)}), bf16[4,256,768]{2,1,0:T(8,128)(2,1)S(1)}, u32[]{:S(2)}, u32[]{:S(2)}) async-start(bf16[4,256,768]{2,1,0:T(8,128)(2,1)} %bitcast.54), calls=%async_computation.2 | async-start | bytes 3145728 | tf_op jit(solution)/shard_map/all_to_all | solution.py:888
  146.8 8.8 %first_halves.1 = (bf16[4,480,384]{2,1,0:T(8,128)(2,1)}, bf16[4,480,384]{2,1,0:T(8,128)(2,1)}, bf16[4,480,384]{2,1,0:T(8,128)(2,1)}, bf16[4,480,384]{2,1,0:T(8,128)(2,1)}) custom-call(s32[3]{0:T(128)S(1)} %pad_add_fusion.at_ref, bf16[4,384,768]{2,1,0:T(8,128)(2,1)} %get-tuple-element.126.row_keep, bf16[4,384,768]{2,1,0:T(8,128)(2,1)} %collective-permute-done.row_got, ...), custom_call_target="tpu_custom_call" | custom-call | flops 40000000000 | bytes 100000000 | tf_op jit(solution)/shard_map/first_halves/pallas_call | solution.py:594
  158.7 40.5 %attention_backward.1 = (bf16[3,1024,768]{2,1,0:T(8,128)(2,1)}, bf16[1024,768]{1,0:T(8,128)(2,1)}, f32[8,768]{1,0:T(8,128)S(1)}) custom-call(bf16[1024,768]{1,0:T(8,128)(2,1)S(1)} %copy-done.11, bf16[1024,768]{1,0:T(8,128)(2,1)S(1)} %copy-done.12, bf16[1024,768]{1,0:T(8,128)(2,1)S(1)} %copy-done.13, bf16[1024,768]{1,0:T(8,128)(2,1)S(1)} %copy-done.15, ...), custom_call_target="tpu_custom_call" | custom-call | flops 40000000000 | bytes 100000000 | tf_op jit(solution)/shard_map/attention_backward/pallas_call | solution.py:237
  199.2 4.7 %all-to-all-start.3 = ((bf16[4,256,768]{2,1,0:T(8,128)(2,1)}), bf16[4,256,768]{2,1,0:T(8,128)(2,1)}, u32[]{:S(2)}, u32[]{:S(2)}) async-start(bf16[4,256,768]{2,1,0:T(8,128)(2,1)} %bitcast.55), calls=%async_computation.3 | async-start | bytes 3145728 | tf_op jit(solution)/shard_map/all_to_all | solution.py:888
  204.0 3.6 %second_halves.1 = (bf16[4,240,384]{2,1,0:T(8,128)(2,1)S(1)}, bf16[4,240,384]{2,1,0:T(8,128)(2,1)S(1)}, bf16[4,240,384]{2,1,0:T(8,128)(2,1)S(1)}, bf16[4,240,384]{2,1,0:T(8,128)(2,1)S(1)}) custom-call(s32[3]{0:T(128)S(1)} %pad_add_fusion.at_ref, bf16[4,2,240,384]{3,2,1,0:T(8,128)(2,1)} %bitcast.56, bf16[4,2,240,384]{3,2,1,0:T(8,128)(2,1)} %bitcast.12.refs_1_, ...), custom_call_target="tpu_custom_call" | custom-call | flops 40000000000 | bytes 100000000 | tf_op jit(solution)/shard_map/second_halves/pallas_call | solution.py:621
  209.9 5.4 %late_grads.1 = (bf16[1,128]{1,0:T(2,128)(2,1)S(1)}, bf16[4,384,768]{2,1,0:T(8,128)(2,1)S(1)}, bf16[4,384,768]{2,1,0:T(8,128)(2,1)S(1)}) custom-call(s32[1]{0:T(128)} %bitcast.6.core_ref, f32[8,768]{1,0:T(8,128)S(1)} %get-tuple-element.140.sum_ref, f32[8,768]{1,0:T(8,128)S(1)} %get-tuple-element.141.mod_ref, bf16[128,4608]{1,0:T(8,128)(2,1)S(1)} %copy-done.1, ...), custom_call_target="tpu_custom_call" | custom-call | flops 40000000000 | bytes 100000000 | tf_op jit(solution)/shard_map/late_grads/pallas_call | solution.py:415
  215.4 10.5 %collective-permute-done.5.refs_1_ = bf16[4,240,384]{2,1,0:T(8,128)(2,1)S(1)} collective-permute-done((bf16[4,240,384]{2,1,0:T(8,128)(2,1)S(1)}, bf16[4,240,384]{2,1,0:T(8,128)(2,1)S(1)}, u32[]{:S(2)}, u32[]{:S(2)}) %collective-permute-start.5) | collective-permute-done | bytes 737312 | tf_op jit(solution)/shard_map/ppermute | solution.py:549
  229.3 2.1 quarters.1
  237.4 3.7 %all-to-all-done.3 = bf16[4,256,768]{2,1,0:T(8,128)(2,1)} async-done(((bf16[4,256,768]{2,1,0:T(8,128)(2,1)}), bf16[4,256,768]{2,1,0:T(8,128)(2,1)}, u32[]{:S(2)}, u32[]{:S(2)}) %all-to-all-start.3) | async-done | bytes 1572896 | tf_op jit(solution)/shard_map/all_to_all | solution.py:888
  241.1 11.8 %collective-permute-done.7 = bf16[2,240,768]{2,1,0:T(8,128)(2,1)} collective-permute-done((bf16[2,240,768]{2,1,0:T(8,128)(2,1)S(1)}, bf16[2,240,768]{2,1,0:T(8,128)(2,1)}, u32[]{:S(2)}, u32[]{:S(2)}) %collective-permute-start.7) | collective-permute-done | bytes 737312 | tf_op jit(solution)/shard_map/ppermute | solution.py:549
  255.6 4.4 %collective-permute-done.8.refs_1_ = bf16[4,96,768]{2,1,0:T(8,128)(2,1)} collective-permute-done((bf16[4,96,768]{2,1,0:T(8,128)(2,1)}, bf16[4,96,768]{2,1,0:T(8,128)(2,1)}, u32[]{:S(2)}, u32[]{:S(2)}) %collective-permute-start.8) | collective-permute-done | bytes 589856 | tf_op jit(solution)/shard_map/ppermute | solution.py:549
  260.0 1.7 near_halves.3
  262.6 9.4 %collective-permute-done.12 = bf16[240,768]{1,0:T(8,128)(2,1)S(1)} collective-permute-done((bf16[240,768]{1,0:T(8,128)(2,1)S(1)}, bf16[240,768]{1,0:T(8,128)(2,1)S(1)}, u32[]{:S(2)}, u32[]{:S(2)}) %collective-permute-start.12) | collective-permute-done | bytes 368672 | tf_op jit(solution)/shard_map/ppermute | solution.py:549
  272.1 5.7 %collective-permute-done.11 = bf16[2,96,768]{2,1,0:T(8,128)(2,1)S(1)} collective-permute-done((bf16[2,96,768]{2,1,0:T(8,128)(2,1)S(1)}, bf16[2,96,768]{2,1,0:T(8,128)(2,1)S(1)}, u32[]{:S(2)}, u32[]{:S(2)}) %collective-permute-start.11) | collective-permute-done | bytes 294944 | tf_op jit(solution)/shard_map/ppermute | solution.py:549
  279.2 1.7 collective-permute-start.17
  282.2 5.1 %collective-permute-done.13 = bf16[96,768]{1,0:T(8,128)(2,1)S(1)} collective-permute-done((bf16[96,768]{1,0:T(8,128)(2,1)S(1)}, bf16[96,768]{1,0:T(8,128)(2,1)S(1)}, u32[]{:S(2)}, u32[]{:S(2)}) %collective-permute-start.13) | collective-permute-done | bytes 147488 | tf_op jit(solution)/shard_map/ppermute | solution.py:549
  287.5 3.5 %collective-permute-done.14 = bf16[1,128]{1,0:T(2,128)(2,1)S(1)} collective-permute-done((bf16[1,128]{1,0:T(2,128)(2,1)S(1)}, bf16[1,128]{1,0:T(2,128)(2,1)S(1)}, u32[]{:S(2)}, u32[]{:S(2)}) %collective-permute-start.14) | collective-permute-done | bytes 288 | tf_op jit(solution)/shard_map/ppermute | solution.py:549
  291.7 3.3 %convert_element_type.142 = f32[4,256,768]{2,1,0:T(8,128)} convert(bf16[4,256,768]{2,1,0:T(8,128)(2,1)} %all-to-all-done.3) | non-fusion elementwise | flops 786432 | bytes 4718592 | tf_op jit(solution)/shard_map/convert_element_type | solution.py:1001
  295.5 2.5 collective-permute-done.18.refs_3_
  299.3 1.7 collective-permute-start.20
  302.3 2.6 finish.1
  306.0 3.4 %collective-permute-done.21.refs_3_ = bf16[96,768]{1,0:T(8,128)(2,1)S(1)} collective-permute-done((bf16[96,768]{1,0:T(8,128)(2,1)S(1)}, bf16[96,768]{1,0:T(8,128)(2,1)S(1)}, u32[]{:S(2)}, u32[]{:S(2)}) %collective-permute-start.21) | collective-permute-done | bytes 147488 | tf_op jit(solution)/shard_map/ppermute | solution.py:549
  (126 shorter events, 32.5 us)
Async XLA Ops:
  0.7 43.4 %all-to-all-start = ((bf16[4,256,768]{2,1,0:T(8,128)(2,1)}), bf16[4,256,768]{2,1,0:T(8,128)(2,1)S(1)}, u32[]{:S(2)}, u32[]{:S(2)}) async-start(bf16[4,256,768]{2,1,0:T(8,128)(2,1)} %param.13), calls=%async_computation | async-start | bytes 3145728 | tf_op jit(solution)/shard_map/all_to_all | solution.py:888
  7.9 40.6 %copy-start.6 = (f32[8,768]{1,0:T(8,128)}, f32[8,768]{1,0:T(8,128)S(1)}, u32[]{:S(2)}) copy-start(f32[8,768]{1,0:T(8,128)S(1)} %get-tuple-element.108.mod_ref) | copy-start | bytes 73732
  8.1 112.6 %copy-start.4 = (f32[128,1]{1,0:T(8,128)}, f32[128,1]{1,0:T(8,128)S(1)}, u32[]{:S(2)}) copy-start(f32[128,1]{1,0:T(8,128)S(1)} %copy.26.timing_ref) | copy-start | bytes 1540
  44.1 40.9 %all-to-all-start.1 = ((bf16[4,256,768]{2,1,0:T(8,128)(2,1)}), bf16[4,256,768]{2,1,0:T(8,128)(2,1)}, u32[]{:S(2)}, u32[]{:S(2)}) async-start(bf16[4,256,768]{2,1,0:T(8,128)(2,1)} %param.25), calls=%async_computation.1 | async-start | bytes 3145728 | tf_op jit(solution)/shard_map/all_to_all | solution.py:888
  57.1 27.9 %copy-start.9 = (bf16[768,768]{1,0:T(8,128)(2,1)S(1)}, bf16[768,768]{1,0:T(8,128)(2,1)}, u32[]{:S(2)}) copy-start(bf16[768,768]{1,0:T(8,128)(2,1)} %wo_ref.1) | copy-start | bytes 3538948
  132.5 14.2 %collective-permute-start.1 = (bf16[4,576,768]{2,1,0:T(8,128)(2,1)}, bf16[4,576,768]{2,1,0:T(8,128)(2,1)}, u32[]{:S(2)}, u32[]{:S(2)}) collective-permute-start(bf16[4,576,768]{2,1,0:T(8,128)(2,1)} %get-tuple-element.128), channel_id=1, source_target_pairs={{0,4},{4,0},{8,12},{12,8},{16,20},{20,16},{24,28},{28,24},{1,5},{5... | collective-permute-start | bytes 10616840 | tf_op jit(solution)/shard_map/ppermute | solution.py:549
  141.7 5.0 %collective-permute-start = (bf16[4,384,768]{2,1,0:T(8,128)(2,1)}, bf16[4,384,768]{2,1,0:T(8,128)(2,1)}, u32[]{:S(2)}, u32[]{:S(2)}) collective-permute-start(bf16[4,384,768]{2,1,0:T(8,128)(2,1)} %get-tuple-element.127), channel_id=1, source_target_pairs={{0,4},{4,0},{8,12},{12,8},{16,20},{20,16},{24,28},{28,24},{1,5},{5... | collective-permute-start | bytes 7077896 | tf_op jit(solution)/shard_map/ppermute | solution.py:549
  142.2 57.0 %all-to-all-start.2 = ((bf16[4,256,768]{2,1,0:T(8,128)(2,1)}), bf16[4,256,768]{2,1,0:T(8,128)(2,1)S(1)}, u32[]{:S(2)}, u32[]{:S(2)}) async-start(bf16[4,256,768]{2,1,0:T(8,128)(2,1)} %bitcast.54), calls=%async_computation.2 | async-start | bytes 3145728 | tf_op jit(solution)/shard_map/all_to_all | solution.py:888
  155.6 48.3 %collective-permute-start.2 = (bf16[4,480,384]{2,1,0:T(8,128)(2,1)}, bf16[4,480,384]{2,1,0:T(8,128)(2,1)}, u32[]{:S(2)}, u32[]{:S(2)}) collective-permute-start(bf16[4,480,384]{2,1,0:T(8,128)(2,1)} %get-tuple-element.129), channel_id=1, source_target_pairs={{0,8},{4,12},{8,0},{12,4},{16,24},{20,28},{24,16},{28,20},{1,9},{5... | collective-permute-start | bytes 4423688 | tf_op jit(solution)/shard_map/ppermute | solution.py:549
  157.1 46.8 %collective-permute-start.3 = (bf16[4,480,384]{2,1,0:T(8,128)(2,1)}, bf16[4,480,384]{2,1,0:T(8,128)(2,1)}, u32[]{:S(2)}, u32[]{:S(2)}) collective-permute-start(bf16[4,480,384]{2,1,0:T(8,128)(2,1)} %get-tuple-element.130), channel_id=1, source_target_pairs={{0,16},{4,20},{8,24},{12,28},{16,0},{20,4},{24,8},{28,12},{1,17},{... | collective-permute-start | bytes 4423688 | tf_op jit(solution)/shard_map/ppermute | solution.py:549
  199.2 41.9 %all-to-all-start.3 = ((bf16[4,256,768]{2,1,0:T(8,128)(2,1)}), bf16[4,256,768]{2,1,0:T(8,128)(2,1)}, u32[]{:S(2)}, u32[]{:S(2)}) async-start(bf16[4,256,768]{2,1,0:T(8,128)(2,1)} %bitcast.55), calls=%async_computation.3 | async-start | bytes 3145728 | tf_op jit(solution)/shard_map/all_to_all | solution.py:888
  207.6 18.3 %collective-permute-start.5 = (bf16[4,240,384]{2,1,0:T(8,128)(2,1)S(1)}, bf16[4,240,384]{2,1,0:T(8,128)(2,1)S(1)}, u32[]{:S(2)}, u32[]{:S(2)}) collective-permute-start(bf16[4,240,384]{2,1,0:T(8,128)(2,1)S(1)} %get-tuple-element.151), channel_id=1, source_target_pairs={{0,16},{4,20},{8,24},{12,28},{16,0},{20,4},{24,8},{28,12},{1,17},{... | collective-permute-start | bytes 2211848 | tf_op jit(solution)/shard_map/ppermute | solution.py:549
  208.3 18.5 %collective-permute-start.6 = (bf16[4,240,384]{2,1,0:T(8,128)(2,1)S(1)}, bf16[4,240,384]{2,1,0:T(8,128)(2,1)S(1)}, u32[]{:S(2)}, u32[]{:S(2)}) collective-permute-start(bf16[4,240,384]{2,1,0:T(8,128)(2,1)S(1)} %get-tuple-element.152), channel_id=1, source_target_pairs={{0,8},{4,12},{8,0},{12,4},{16,24},{20,28},{24,16},{28,20},{1,9},{5... | collective-permute-start | bytes 2211848 | tf_op jit(solution)/shard_map/ppermute | solution.py:549
  215.3 14.0 %collective-permute-start.4 = (bf16[4,384,768]{2,1,0:T(8,128)(2,1)S(1)}, bf16[4,384,768]{2,1,0:T(8,128)(2,1)S(1)}, u32[]{:S(2)}, u32[]{:S(2)}) collective-permute-start(bf16[4,384,768]{2,1,0:T(8,128)(2,1)S(1)} %get-tuple-element.150), channel_id=1, source_target_pairs={{0,4},{4,0},{8,12},{12,8},{16,20},{20,16},{24,28},{28,24},{1,5},{5... | collective-permute-start | bytes 7077896 | tf_op jit(solution)/shard_map/ppermute | solution.py:549
  227.7 25.2 %collective-permute-start.7 = (bf16[2,240,768]{2,1,0:T(8,128)(2,1)S(1)}, bf16[2,240,768]{2,1,0:T(8,128)(2,1)}, u32[]{:S(2)}, u32[]{:S(2)}) collective-permute-start(bf16[2,240,768]{2,1,0:T(8,128)(2,1)S(1)} %get-tuple-element.159), channel_id=1, source_target_pairs={{0,1},{1,0},{2,3},{3,2},{4,5},{5,4},{6,7},{7,6},{8,9},{9,8},{10,11... | collective-permute-start | bytes 2211848 | tf_op jit(solution)/shard_map/ppermute | solution.py:549
  232.2 23.4 %collective-permute-start.10 = (bf16[4,96,768]{2,1,0:T(8,128)(2,1)}, bf16[4,96,768]{2,1,0:T(8,128)(2,1)}, u32[]{:S(2)}, u32[]{:S(2)}) collective-permute-start(bf16[4,96,768]{2,1,0:T(8,128)(2,1)} %get-tuple-element.164), channel_id=1, source_target_pairs={{0,24},{4,28},{8,16},{12,20},{16,8},{20,12},{24,0},{28,4},{1,25},{... | collective-permute-start | bytes 1769480 | tf_op jit(solution)/shard_map/ppermute | solution.py:549
  233.6 26.4 %collective-permute-start.8 = (bf16[4,96,768]{2,1,0:T(8,128)(2,1)}, bf16[4,96,768]{2,1,0:T(8,128)(2,1)}, u32[]{:S(2)}, u32[]{:S(2)}) collective-permute-start(bf16[4,96,768]{2,1,0:T(8,128)(2,1)} %get-tuple-element.162), channel_id=1, source_target_pairs={{0,16},{4,20},{8,24},{12,28},{16,0},{20,4},{24,8},{28,12},{1,17},{... | collective-permute-start | bytes 1769480 | tf_op jit(solution)/shard_map/ppermute | solution.py:549
  235.2 24.9 %collective-permute-start.9 = (bf16[4,96,768]{2,1,0:T(8,128)(2,1)}, bf16[4,96,768]{2,1,0:T(8,128)(2,1)}, u32[]{:S(2)}, u32[]{:S(2)}) collective-permute-start(bf16[4,96,768]{2,1,0:T(8,128)(2,1)} %get-tuple-element.163), channel_id=1, source_target_pairs={{0,8},{4,12},{8,0},{12,4},{16,24},{20,28},{24,16},{28,20},{1,9},{5... | collective-permute-start | bytes 1769480 | tf_op jit(solution)/shard_map/ppermute | solution.py:549
  237.4 22.7 %copy-start.18 = (bf16[4,96,768]{2,1,0:T(8,128)(2,1)S(1)}, bf16[4,96,768]{2,1,0:T(8,128)(2,1)}, u32[]{:S(2)}) copy-start(bf16[4,96,768]{2,1,0:T(8,128)(2,1)} %copy-done.17) | copy-start | bytes 1769476
  254.2 17.8 %collective-permute-start.12 = (bf16[240,768]{1,0:T(8,128)(2,1)S(1)}, bf16[240,768]{1,0:T(8,128)(2,1)S(1)}, u32[]{:S(2)}, u32[]{:S(2)}) collective-permute-start(bf16[240,768]{1,0:T(8,128)(2,1)S(1)} %get-tuple-element.199), channel_id=1, source_target_pairs={{0,2},{1,3},{2,0},{3,1},{4,6},{5,7},{6,4},{7,5},{8,10},{9,11},{10,... | collective-permute-start | bytes 1105928 | tf_op jit(solution)/shard_map/ppermute | solution.py:549
  261.8 16.0 %collective-permute-start.11 = (bf16[2,96,768]{2,1,0:T(8,128)(2,1)S(1)}, bf16[2,96,768]{2,1,0:T(8,128)(2,1)S(1)}, u32[]{:S(2)}, u32[]{:S(2)}) collective-permute-start(bf16[2,96,768]{2,1,0:T(8,128)(2,1)S(1)} %get-tuple-element.172), channel_id=1, source_target_pairs={{0,1},{1,0},{2,3},{3,2},{4,5},{5,4},{6,7},{7,6},{8,9},{9,8},{10,11... | collective-permute-start | bytes 884744 | tf_op jit(solution)/shard_map/ppermute | solution.py:549
  277.8 9.5 %collective-permute-start.13 = (bf16[96,768]{1,0:T(8,128)(2,1)S(1)}, bf16[96,768]{1,0:T(8,128)(2,1)S(1)}, u32[]{:S(2)}, u32[]{:S(2)}) collective-permute-start(bf16[96,768]{1,0:T(8,128)(2,1)S(1)} %fusion.4), channel_id=1, source_target_pairs={{0,2},{1,3},{2,0},{3,1},{4,6},{5,7},{6,4},{7,5},{8,10},{9,11},{10,... | collective-permute-start | bytes 442376 | tf_op jit(solution)/shard_map/ppermute | solution.py:549
  278.7 16.8 %collective-permute-start.16 = (bf16[240,768]{1,0:T(8,128)(2,1)S(1)}, bf16[240,768]{1,0:T(8,128)(2,1)S(1)}, u32[]{:S(2)}, u32[]{:S(2)}) collective-permute-start(bf16[240,768]{1,0:T(8,128)(2,1)S(1)} %add_convert_fusion.refs_0_), channel_id=1, source_target_pairs={{0,16},{4,20},{8,24},{12,28},{16,0},{20,4},{24,8},{28,12},{1,17},{... | collective-permute-start | bytes 1105928 | tf_op jit(solution)/shard_map/ppermute | solution.py:549
  279.2 16.4 %collective-permute-start.17 = (bf16[240,768]{1,0:T(8,128)(2,1)S(1)}, bf16[240,768]{1,0:T(8,128)(2,1)S(1)}, u32[]{:S(2)}, u32[]{:S(2)}) collective-permute-start(bf16[240,768]{1,0:T(8,128)(2,1)S(1)} %add_convert_fusion.refs_0_), channel_id=1, source_target_pairs={{0,8},{4,12},{8,0},{12,4},{16,24},{20,28},{24,16},{28,20},{1,9},{5... | collective-permute-start | bytes 1105928 | tf_op jit(solution)/shard_map/ppermute | solution.py:549
  280.9 17.1 %collective-permute-start.18 = (bf16[240,768]{1,0:T(8,128)(2,1)S(1)}, bf16[240,768]{1,0:T(8,128)(2,1)S(1)}, u32[]{:S(2)}, u32[]{:S(2)}) collective-permute-start(bf16[240,768]{1,0:T(8,128)(2,1)S(1)} %add_convert_fusion.refs_0_), channel_id=1, source_target_pairs={{0,24},{4,28},{8,16},{12,20},{16,8},{20,12},{24,0},{28,4},{1,25},{... | collective-permute-start | bytes 1105928 | tf_op jit(solution)/shard_map/ppermute | solution.py:549
  287.4 3.6 %collective-permute-start.14 = (bf16[1,128]{1,0:T(2,128)(2,1)S(1)}, bf16[1,128]{1,0:T(2,128)(2,1)S(1)}, u32[]{:S(2)}, u32[]{:S(2)}) collective-permute-start(bf16[1,128]{1,0:T(2,128)(2,1)S(1)} %get-tuple-element.177), channel_id=1, source_target_pairs={{0,1},{1,0},{2,3},{3,2},{4,5},{5,4},{6,7},{7,6},{8,9},{9,8},{10,11... | collective-permute-start | bytes 776 | tf_op jit(solution)/shard_map/ppermute | solution.py:549
  291.0 4.5 %collective-permute-start.15 = (bf16[2,128]{1,0:T(2,128)(2,1)S(1)}, bf16[2,128]{1,0:T(2,128)(2,1)S(1)}, u32[]{:S(2)}, u32[]{:S(2)}) collective-permute-start(bf16[2,128]{1,0:T(2,128)(2,1)S(1)} %pad_maximum_fusion.1), channel_id=1, source_target_pairs={{0,2},{1,3},{2,0},{3,1},{4,6},{5,7},{6,4},{7,5},{8,10},{9,11},{10,... | collective-permute-start | bytes 1544 | tf_op jit(solution)/shard_map/ppermute | solution.py:549
  298.7 3.6 %collective-permute-start.22 = (bf16[960,768]{1,0:T(8,128)(2,1)S(1)}, bf16[960,768]{1,0:T(8,128)(2,1)S(1)}, u32[]{:S(2)}, u32[]{:S(2)}) collective-permute-start(bf16[960,768]{1,0:T(8,128)(2,1)S(1)} %bitcast.47), channel_id=1, source_target_pairs={{0,4},{4,0},{8,12},{12,8},{16,20},{20,16},{24,28},{28,24},{1,5},{5... | collective-permute-start | bytes 4423688 | tf_op jit(solution)/shard_map/ppermute | solution.py:549
  298.8 6.3 %collective-permute-start.19 = (bf16[96,768]{1,0:T(8,128)(2,1)S(1)}, bf16[96,768]{1,0:T(8,128)(2,1)S(1)}, u32[]{:S(2)}, u32[]{:S(2)}) collective-permute-start(bf16[96,768]{1,0:T(8,128)(2,1)S(1)} %fusion.2.refs_0_), channel_id=1, source_target_pairs={{0,16},{4,20},{8,24},{12,28},{16,0},{20,4},{24,8},{28,12},{1,17},{... | collective-permute-start | bytes 442376 | tf_op jit(solution)/shard_map/ppermute | solution.py:549
  299.3 6.7 %collective-permute-start.20 = (bf16[96,768]{1,0:T(8,128)(2,1)S(1)}, bf16[96,768]{1,0:T(8,128)(2,1)S(1)}, u32[]{:S(2)}, u32[]{:S(2)}) collective-permute-start(bf16[96,768]{1,0:T(8,128)(2,1)S(1)} %fusion.2.refs_0_), channel_id=1, source_target_pairs={{0,8},{4,12},{8,0},{12,4},{16,24},{20,28},{24,16},{28,20},{1,9},{5... | collective-permute-start | bytes 442376 | tf_op jit(solution)/shard_map/ppermute | solution.py:549
  301.0 8.4 %collective-permute-start.21 = (bf16[96,768]{1,0:T(8,128)(2,1)S(1)}, bf16[96,768]{1,0:T(8,128)(2,1)S(1)}, u32[]{:S(2)}, u32[]{:S(2)}) collective-permute-start(bf16[96,768]{1,0:T(8,128)(2,1)S(1)} %fusion.2.refs_0_), channel_id=1, source_target_pairs={{0,24},{4,28},{8,16},{12,20},{16,8},{20,12},{24,0},{28,4},{1,25},{... | collective-permute-start | bytes 442376 | tf_op jit(solution)/shard_map/ppermute | solution.py:549
  310.0 2.1 collective-permute-start.23
  (24 other events, 207.2 us)

commit v5 on v4

--- a/solution.py
+++ b/solution.py
@@ -617,7 +617,7 @@
 
 def second_halves(at, *arrays):
     sp, rows, columns = arrays[0].shape
-    out = jax.ShapeDtypeStruct((sp, rows // 2, columns), bf16)
+    out = pltpu.HBM((sp, rows // 2, columns), bf16)
     return pl.pallas_call(
         second_halves_kernel,
         in_specs=[SMEM] + [VMEM] * 4,
@@ -962,7 +962,7 @@
     time_row, late_send, late_keep = late_grads(
         core, grads, xm_attn, attn_sums, late_mods, ada_weight, column, early_parts, sp
     )
-    hidden_grad = exchange(hg)
+    hidden_grad = exchange(after(hg, left, right))
     late_got = pair_permute(late_send, CORE)
     left_got, right_got = after((left_got, right_got), late_keep)
     if lax.axis_size("dp") > 2 * SECOND:

time: 314 us -> 315 us (level)
  waiting for transfers between devices: 106 us -> 102 us
    all_to_all x4, waiting for transfers between devices: 45 us -> 41.3 us  [exchange(): return lax.all_to_all(values, 'sp', split_axis=0, concat_axis=0, tiled=True)]
  transfers between devices with their start and end apart: 28 -> 28, of which waited for: 18 -> 17; matrix products, arithmetic and copies ran while one was open for 3% -> 3% of each run, Pallas kernels for 33% -> 32%
where the time goes in v5:
time: 315 us; the launch traced here: 314 us
  Pallas kernels  156 us (50%)
  waiting for transfers between devices  102 us (32%)
  starting transfers between devices  41.2 us (13%)
  other arithmetic  8.74 us (3%)
  local copies, waits for them, and re-layouts  4.14 us (1%)
    ppermute x24, waiting for transfers between devices, pair_permute(): return lax.ppermute(value, axis, [(i, i ^ bit) for i in range(n)])  61.1 us
    all_to_all x4, waiting for transfers between devices, exchange(): return lax.all_to_all(values, 'sp', split_axis=0, concat_axis=0, tiled=True)  41.3 us
    pallas_call x1, Pallas kernels, attention_backward(): pl.pallas_call(functools.partial(attention_backward_kernel, pairs=pairs),...  40.4 us
    pallas_call x1, Pallas kernels, feed_forward(): pl.pallas_call(mlp_kernel, grid=(length // rows,), in_specs=[block, block...  35.7 us
    ppermute x24, starting transfers between devices, pair_permute(): return lax.ppermute(value, axis, [(i, i ^ bit) for i in range(n)])  22.1 us
    pallas_call x1, Pallas kernels, attention_forward(): pl.pallas_call(functools.partial(attention_forward_kernel, chunk=length /...  19.6 us
    all_to_all x4, starting transfers between devices, exchange(): return lax.all_to_all(values, 'sp', split_axis=0, concat_axis=0, tiled=True)  19.1 us
    pallas_call x1, Pallas kernels, column_grad(): pl.pallas_call(functools.partial(column_grad_kernel, blocks=n), grid_spec...  11.9 us
  transfers between devices with their start and end apart: 28, of which 17 were waited for; matrix products, arithmetic and copies ran while one was open for 3% of the time, Pallas kernels for 32%

profile of v5, /device:TPU:0, one launch (start us, length us, event | category | flops | bytes accessed | tf_op | source)
XLA Modules:
  0.0 314.0 jit_solution(13910686293614482684)
XLA Ops:
  0.7 6.5 %all-to-all-start = ((bf16[4,256,768]{2,1,0:T(8,128)(2,1)}), bf16[4,256,768]{2,1,0:T(8,128)(2,1)S(1)}, u32[]{:S(2)}, u32[]{:S(2)}) async-start(bf16[4,256,768]{2,1,0:T(8,128)(2,1)} %param.13), calls=%async_computation | async-start | bytes 3145728 | tf_op jit(solution)/shard_map/all_to_all | solution.py:888
  8.1 3.1 multiply_sine_fusion
  11.1 33.0 %all-to-all-done = bf16[4,256,768]{2,1,0:T(8,128)(2,1)S(1)} async-done(((bf16[4,256,768]{2,1,0:T(8,128)(2,1)}), bf16[4,256,768]{2,1,0:T(8,128)(2,1)S(1)}, u32[]{:S(2)}, u32[]{:S(2)}) %all-to-all-start) | async-done | bytes 1572896 | tf_op jit(solution)/shard_map/all_to_all | solution.py:888
  44.1 4.4 %all-to-all-start.1 = ((bf16[4,256,768]{2,1,0:T(8,128)(2,1)}), bf16[4,256,768]{2,1,0:T(8,128)(2,1)}, u32[]{:S(2)}, u32[]{:S(2)}) async-start(bf16[4,256,768]{2,1,0:T(8,128)(2,1)} %param.25), calls=%async_computation.1 | async-start | bytes 3145728 | tf_op jit(solution)/shard_map/all_to_all | solution.py:888
  48.5 8.6 %project_qkv.1 = (bf16[1024,768]{1,0:T(8,128)(2,1)}, bf16[1024,768]{1,0:T(8,128)(2,1)}, bf16[1024,768]{1,0:T(8,128)(2,1)}, bf16[1024,768]{1,0:T(8,128)(2,1)}) custom-call(bf16[1024,768]{1,0:T(8,128)(2,1)S(1)} %bitcast.42, f32[8,768]{1,0:T(8,128)S(1)} %get-tuple-element.109.mod_ref, bf16[768,2304]{1,0:T(8,128)(2,1)} %w_ref.3, ...), custom_call_target="tpu_custom_call" | custom-call | flops 40000000000 | bytes 100000000 | tf_op jit(solution)/shard_map/project_qkv/pallas_call | solution.py:99
  57.1 19.6 %attention_forward.1 = (bf16[1024,768]{1,0:T(8,128)(2,1)}, f32[6,2,1024]{2,1,0:T(2,128)}) custom-call(bf16[1024,768]{1,0:T(8,128)(2,1)} %get-tuple-element.110.q_ref, bf16[1024,768]{1,0:T(8,128)(2,1)} %get-tuple-element.111.k_ref, bf16[1024,768]{1,0:T(8,128)(2,1)} %get-tuple-element.112.v_ref), custom_call_target="tpu_custom_call" | custom-call | flops 40000000000 | bytes 100000000 | tf_op jit(solution)/shard_map/attention_forward/pallas_call | solution.py:151
  76.7 8.3 %all-to-all-done.1 = bf16[4,256,768]{2,1,0:T(8,128)(2,1)} async-done(((bf16[4,256,768]{2,1,0:T(8,128)(2,1)}), bf16[4,256,768]{2,1,0:T(8,128)(2,1)}, u32[]{:S(2)}, u32[]{:S(2)}) %all-to-all-start.1) | async-done | bytes 1572896 | tf_op jit(solution)/shard_map/all_to_all | solution.py:888
  85.0 35.7 %feed_forward.1 = (bf16[2,1024,768]{2,1,0:T(8,128)(2,1)}, bf16[1024,3072]{1,0:T(8,128)(2,1)}, bf16[1024,768]{1,0:T(8,128)(2,1)}, bf16[5,1024,768]{2,1,0:T(8,128)...) custom-call(bf16[1024,768]{1,0:T(8,128)(2,1)S(1)} %bitcast.43, ...), custom_call_target="tpu_custom_call" | custom-call | flops 40000000000 | bytes 100000000 | tf_op jit(solution)/shard_map/feed_forward/pallas_call | solution.py:335
  120.8 11.9 %column_grad.1 = (bf16[4,576,768]{2,1,0:T(8,128)(2,1)}, bf16[4,576,768]{2,1,0:T(8,128)(2,1)}, f32[4,768]{1,0:T(4,128)S(1)}) custom-call(s32[1]{0:T(128)} %bitcast.6.core_ref, f32[8,768]{1,0:T(8,128)S(1)} %get-tuple-element.118.sum_ref, f32[1,3072]{1,0:T(1,128)S(1)} %get-tuple-element.119.up_sum_ref, f32[8,768]{1,0:T(8,128)S(1)} %get-tuple-element.120.mod_ref, ...), custom_call_target="tpu_custom_call" | custom-call | flops 40000000000 | bytes 100000000 | tf_op jit(solution)/shard_map/column_grad/pallas_call | solution.py:523
  132.6 9.2 %row_grad.1 = (bf16[4,384,768]{2,1,0:T(8,128)(2,1)}, bf16[4,384,768]{2,1,0:T(8,128)(2,1)}) custom-call(s32[1]{0:T(128)} %bitcast.6.core_ref, bf16[1024,3072]{1,0:T(8,128)(2,1)} %get-tuple-element.125.a_ref, bf16[1024,768]{1,0:T(8,128)(2,1)} %get-tuple-element.126.b_ref), custom_call_target="tpu_custom_call" | custom-call | flops 40000000000 | bytes 100000000 | tf_op jit(solution)/shard_map/row_grad/pallas_call | solution.py:454
  142.3 3.6 %all-to-all-start.2 = ((bf16[4,256,768]{2,1,0:T(8,128)(2,1)}), bf16[4,256,768]{2,1,0:T(8,128)(2,1)S(1)}, u32[]{:S(2)}, u32[]{:S(2)}) async-start(bf16[4,256,768]{2,1,0:T(8,128)(2,1)} %bitcast.52), calls=%async_computation.2 | async-start | bytes 3145728 | tf_op jit(solution)/shard_map/all_to_all | solution.py:888
  146.9 8.8 %first_halves.1 = (bf16[4,480,384]{2,1,0:T(8,128)(2,1)}, bf16[4,480,384]{2,1,0:T(8,128)(2,1)}, bf16[4,480,384]{2,1,0:T(8,128)(2,1)}, bf16[4,480,384]{2,1,0:T(8,128)(2,1)}) custom-call(s32[3]{0:T(128)S(1)} %pad_add_fusion.at_ref, bf16[4,384,768]{2,1,0:T(8,128)(2,1)} %get-tuple-element.127.row_keep, bf16[4,384,768]{2,1,0:T(8,128)(2,1)} %collective-permute-done.row_got, ...), custom_call_target="tpu_custom_call" | custom-call | flops 40000000000 | bytes 100000000 | tf_op jit(solution)/shard_map/first_halves/pallas_call | solution.py:594
  158.8 40.4 %attention_backward.1 = (bf16[3,1024,768]{2,1,0:T(8,128)(2,1)}, bf16[1024,768]{1,0:T(8,128)(2,1)}, f32[8,768]{1,0:T(8,128)S(1)}) custom-call(bf16[1024,768]{1,0:T(8,128)(2,1)S(1)} %copy-done.12, bf16[1024,768]{1,0:T(8,128)(2,1)S(1)} %copy-done.13, bf16[1024,768]{1,0:T(8,128)(2,1)S(1)} %copy-done.14, bf16[1024,768]{1,0:T(8,128)(2,1)S(1)} %copy-done.16, ...), custom_call_target="tpu_custom_call" | custom-call | flops 40000000000 | bytes 100000000 | tf_op jit(solution)/shard_map/attention_backward/pallas_call | solution.py:237
  199.3 4.5 %second_halves.1 = (bf16[4,240,384]{2,1,0:T(8,128)(2,1)}, bf16[4,240,384]{2,1,0:T(8,128)(2,1)}, bf16[4,240,384]{2,1,0:T(8,128)(2,1)}, bf16[4,240,384]{2,1,0:T(8,128)(2,1)}) custom-call(s32[3]{0:T(128)S(1)} %pad_add_fusion.at_ref, bf16[4,2,240,384]{3,2,1,0:T(8,128)(2,1)} %bitcast.54, bf16[4,2,240,384]{3,2,1,0:T(8,128)(2,1)} %bitcast.12.refs_1_, ...), custom_call_target="tpu_custom_call" | custom-call | flops 40000000000 | bytes 100000000 | tf_op jit(solution)/shard_map/second_halves/pallas_call | solution.py:621
  203.8 4.7 %all-to-all-start.3 = ((bf16[4,256,768]{2,1,0:T(8,128)(2,1)}), bf16[4,256,768]{2,1,0:T(8,128)(2,1)}, u32[]{:S(2)}, u32[]{:S(2)}) async-start(bf16[4,256,768]{2,1,0:T(8,128)(2,1)} %bitcast.53), calls=%async_computation.3 | async-start | bytes 3145728 | tf_op jit(solution)/shard_map/all_to_all | solution.py:888
  210.7 2.3 copy-done.10
  214.5 5.4 %late_grads.1 = (bf16[1,128]{1,0:T(2,128)(2,1)S(1)}, bf16[4,384,768]{2,1,0:T(8,128)(2,1)S(1)}, bf16[4,384,768]{2,1,0:T(8,128)(2,1)S(1)}) custom-call(s32[1]{0:T(128)} %bitcast.6.core_ref, f32[8,768]{1,0:T(8,128)S(1)} %get-tuple-element.141.sum_ref, f32[8,768]{1,0:T(8,128)S(1)} %get-tuple-element.142.mod_ref, bf16[128,4608]{1,0:T(8,128)(2,1)S(1)} %copy-done.1, ...), custom_call_target="tpu_custom_call" | custom-call | flops 40000000000 | bytes 100000000 | tf_op jit(solution)/shard_map/late_grads/pallas_call | solution.py:415
  220.0 7.0 %collective-permute-done.5.refs_1_ = bf16[4,240,384]{2,1,0:T(8,128)(2,1)S(1)} collective-permute-done((bf16[4,240,384]{2,1,0:T(8,128)(2,1)}, bf16[4,240,384]{2,1,0:T(8,128)(2,1)S(1)}, u32[]{:S(2)}, u32[]{:S(2)}) %collective-permute-start.5) | collective-permute-done | bytes 737312 | tf_op jit(solution)/shard_map/ppermute | solution.py:549
  230.3 2.1 quarters.1
  235.9 1.7 hand_over.1
  237.5 16.6 %collective-permute-done.7 = bf16[2,240,768]{2,1,0:T(8,128)(2,1)} collective-permute-done((bf16[2,240,768]{2,1,0:T(8,128)(2,1)S(1)}, bf16[2,240,768]{2,1,0:T(8,128)(2,1)}, u32[]{:S(2)}, u32[]{:S(2)}) %collective-permute-start.7) | collective-permute-done | bytes 737312 | tf_op jit(solution)/shard_map/ppermute | solution.py:549
  256.8 3.4 %collective-permute-done.8.refs_1_ = bf16[4,96,768]{2,1,0:T(8,128)(2,1)} collective-permute-done((bf16[4,96,768]{2,1,0:T(8,128)(2,1)}, bf16[4,96,768]{2,1,0:T(8,128)(2,1)}, u32[]{:S(2)}, u32[]{:S(2)}) %collective-permute-start.8) | collective-permute-done | bytes 589856 | tf_op jit(solution)/shard_map/ppermute | solution.py:549
  260.2 1.7 near_halves.3
  263.0 10.4 %collective-permute-done.12 = bf16[240,768]{1,0:T(8,128)(2,1)S(1)} collective-permute-done((bf16[240,768]{1,0:T(8,128)(2,1)S(1)}, bf16[240,768]{1,0:T(8,128)(2,1)S(1)}, u32[]{:S(2)}, u32[]{:S(2)}) %collective-permute-start.12) | collective-permute-done | bytes 368672 | tf_op jit(solution)/shard_map/ppermute | solution.py:549
  273.4 4.9 %collective-permute-done.11 = bf16[2,96,768]{2,1,0:T(8,128)(2,1)S(1)} collective-permute-done((bf16[2,96,768]{2,1,0:T(8,128)(2,1)S(1)}, bf16[2,96,768]{2,1,0:T(8,128)(2,1)S(1)}, u32[]{:S(2)}, u32[]{:S(2)}) %collective-permute-start.11) | collective-permute-done | bytes 294944 | tf_op jit(solution)/shard_map/ppermute | solution.py:549
  282.8 4.7 %collective-permute-done.13 = bf16[96,768]{1,0:T(8,128)(2,1)S(1)} collective-permute-done((bf16[96,768]{1,0:T(8,128)(2,1)S(1)}, bf16[96,768]{1,0:T(8,128)(2,1)S(1)}, u32[]{:S(2)}, u32[]{:S(2)}) %collective-permute-start.13) | collective-permute-done | bytes 147488 | tf_op jit(solution)/shard_map/ppermute | solution.py:549
  287.6 3.5 %collective-permute-done.14 = bf16[1,128]{1,0:T(2,128)(2,1)S(1)} collective-permute-done((bf16[1,128]{1,0:T(2,128)(2,1)S(1)}, bf16[1,128]{1,0:T(2,128)(2,1)S(1)}, u32[]{:S(2)}, u32[]{:S(2)}) %collective-permute-start.14) | collective-permute-done | bytes 288 | tf_op jit(solution)/shard_map/ppermute | solution.py:549
  292.0 3.3 %convert_element_type.142 = f32[4,256,768]{2,1,0:T(8,128)} convert(bf16[4,256,768]{2,1,0:T(8,128)(2,1)} %all-to-all-done.3) | non-fusion elementwise | flops 786432 | bytes 4718592 | tf_op jit(solution)/shard_map/convert_element_type | solution.py:1001
  295.7 2.6 collective-permute-done.18.refs_3_
  300.9 1.7 collective-permute-start.21
  302.6 2.6 finish.1
  306.1 3.6 %collective-permute-done.21.refs_3_ = bf16[96,768]{1,0:T(8,128)(2,1)S(1)} collective-permute-done((bf16[96,768]{1,0:T(8,128)(2,1)S(1)}, bf16[96,768]{1,0:T(8,128)(2,1)S(1)}, u32[]{:S(2)}, u32[]{:S(2)}) %collective-permute-start.21) | collective-permute-done | bytes 147488 | tf_op jit(solution)/shard_map/ppermute | solution.py:549
  (127 shorter events, 33.1 us)
Async XLA Ops:
  0.7 43.4 %all-to-all-start = ((bf16[4,256,768]{2,1,0:T(8,128)(2,1)}), bf16[4,256,768]{2,1,0:T(8,128)(2,1)S(1)}, u32[]{:S(2)}, u32[]{:S(2)}) async-start(bf16[4,256,768]{2,1,0:T(8,128)(2,1)} %param.13), calls=%async_computation | async-start | bytes 3145728 | tf_op jit(solution)/shard_map/all_to_all | solution.py:888
  7.9 40.6 %copy-start.6 = (f32[8,768]{1,0:T(8,128)}, f32[8,768]{1,0:T(8,128)S(1)}, u32[]{:S(2)}) copy-start(f32[8,768]{1,0:T(8,128)S(1)} %get-tuple-element.109.mod_ref) | copy-start | bytes 73732
  8.1 112.7 %copy-start.4 = (f32[128,1]{1,0:T(8,128)}, f32[128,1]{1,0:T(8,128)S(1)}, u32[]{:S(2)}) copy-start(f32[128,1]{1,0:T(8,128)S(1)} %copy.26.timing_ref) | copy-start | bytes 1540
  44.1 40.9 %all-to-all-start.1 = ((bf16[4,256,768]{2,1,0:T(8,128)(2,1)}), bf16[4,256,768]{2,1,0:T(8,128)(2,1)}, u32[]{:S(2)}, u32[]{:S(2)}) async-start(bf16[4,256,768]{2,1,0:T(8,128)(2,1)} %param.25), calls=%async_computation.1 | async-start | bytes 3145728 | tf_op jit(solution)/shard_map/all_to_all | solution.py:888
  57.1 27.9 %copy-start.9 = (bf16[768,768]{1,0:T(8,128)(2,1)S(1)}, bf16[768,768]{1,0:T(8,128)(2,1)}, u32[]{:S(2)}) copy-start(bf16[768,768]{1,0:T(8,128)(2,1)} %wo_ref.1) | copy-start | bytes 3538948
  132.6 14.2 %collective-permute-start.1 = (bf16[4,576,768]{2,1,0:T(8,128)(2,1)}, bf16[4,576,768]{2,1,0:T(8,128)(2,1)}, u32[]{:S(2)}, u32[]{:S(2)}) collective-permute-start(bf16[4,576,768]{2,1,0:T(8,128)(2,1)} %get-tuple-element.129), channel_id=1, source_target_pairs={{0,4},{4,0},{8,12},{12,8},{16,20},{20,16},{24,28},{28,24},{1,5},{5... | collective-permute-start | bytes 10616840 | tf_op jit(solution)/shard_map/ppermute | solution.py:549
  141.8 5.0 %collective-permute-start = (bf16[4,384,768]{2,1,0:T(8,128)(2,1)}, bf16[4,384,768]{2,1,0:T(8,128)(2,1)}, u32[]{:S(2)}, u32[]{:S(2)}) collective-permute-start(bf16[4,384,768]{2,1,0:T(8,128)(2,1)} %get-tuple-element.128), channel_id=1, source_target_pairs={{0,4},{4,0},{8,12},{12,8},{16,20},{20,16},{24,28},{28,24},{1,5},{5... | collective-permute-start | bytes 7077896 | tf_op jit(solution)/shard_map/ppermute | solution.py:549
  142.3 56.9 %all-to-all-start.2 = ((bf16[4,256,768]{2,1,0:T(8,128)(2,1)}), bf16[4,256,768]{2,1,0:T(8,128)(2,1)S(1)}, u32[]{:S(2)}, u32[]{:S(2)}) async-start(bf16[4,256,768]{2,1,0:T(8,128)(2,1)} %bitcast.52), calls=%async_computation.2 | async-start | bytes 3145728 | tf_op jit(solution)/shard_map/all_to_all | solution.py:888
  155.7 43.5 %collective-permute-start.2 = (bf16[4,480,384]{2,1,0:T(8,128)(2,1)}, bf16[4,480,384]{2,1,0:T(8,128)(2,1)}, u32[]{:S(2)}, u32[]{:S(2)}) collective-permute-start(bf16[4,480,384]{2,1,0:T(8,128)(2,1)} %get-tuple-element.130), channel_id=1, source_target_pairs={{0,8},{4,12},{8,0},{12,4},{16,24},{20,28},{24,16},{28,20},{1,9},{5... | collective-permute-start | bytes 4423688 | tf_op jit(solution)/shard_map/ppermute | solution.py:549
  157.2 42.0 %collective-permute-start.3 = (bf16[4,480,384]{2,1,0:T(8,128)(2,1)}, bf16[4,480,384]{2,1,0:T(8,128)(2,1)}, u32[]{:S(2)}, u32[]{:S(2)}) collective-permute-start(bf16[4,480,384]{2,1,0:T(8,128)(2,1)} %get-tuple-element.131), channel_id=1, source_target_pairs={{0,16},{4,20},{8,24},{12,28},{16,0},{20,4},{24,8},{28,12},{1,17},{... | collective-permute-start | bytes 4423688 | tf_op jit(solution)/shard_map/ppermute | solution.py:549
  203.8 50.3 %all-to-all-start.3 = ((bf16[4,256,768]{2,1,0:T(8,128)(2,1)}), bf16[4,256,768]{2,1,0:T(8,128)(2,1)}, u32[]{:S(2)}, u32[]{:S(2)}) async-start(bf16[4,256,768]{2,1,0:T(8,128)(2,1)} %bitcast.53), calls=%async_computation.3 | async-start | bytes 3145728 | tf_op jit(solution)/shard_map/all_to_all | solution.py:888
  208.5 18.5 %collective-permute-start.5 = (bf16[4,240,384]{2,1,0:T(8,128)(2,1)}, bf16[4,240,384]{2,1,0:T(8,128)(2,1)S(1)}, u32[]{:S(2)}, u32[]{:S(2)}) collective-permute-start(bf16[4,240,384]{2,1,0:T(8,128)(2,1)} %get-tuple-element.152), channel_id=1, source_target_pairs={{0,16},{4,20},{8,24},{12,28},{16,0},{20,4},{24,8},{28,12},{1,17},{... | collective-permute-start | bytes 2211848 | tf_op jit(solution)/shard_map/ppermute | solution.py:549
  209.2 18.7 %collective-permute-start.6 = (bf16[4,240,384]{2,1,0:T(8,128)(2,1)}, bf16[4,240,384]{2,1,0:T(8,128)(2,1)S(1)}, u32[]{:S(2)}, u32[]{:S(2)}) collective-permute-start(bf16[4,240,384]{2,1,0:T(8,128)(2,1)} %get-tuple-element.153), channel_id=1, source_target_pairs={{0,8},{4,12},{8,0},{12,4},{16,24},{20,28},{24,16},{28,20},{1,9},{5... | collective-permute-start | bytes 2211848 | tf_op jit(solution)/shard_map/ppermute | solution.py:549
  214.5 13.4 %copy-start.19 = (bf16[4,240,384]{2,1,0:T(8,128)(2,1)S(1)}, bf16[4,240,384]{2,1,0:T(8,128)(2,1)}, u32[]{:S(2)}) copy-start(bf16[4,240,384]{2,1,0:T(8,128)(2,1)} %get-tuple-element.148.refs_2_) | copy-start | bytes 2211844
  219.9 10.4 %collective-permute-start.4 = (bf16[4,384,768]{2,1,0:T(8,128)(2,1)S(1)}, bf16[4,384,768]{2,1,0:T(8,128)(2,1)S(1)}, u32[]{:S(2)}, u32[]{:S(2)}) collective-permute-start(bf16[4,384,768]{2,1,0:T(8,128)(2,1)S(1)} %get-tuple-element.151), channel_id=1, source_target_pairs={{0,4},{4,0},{8,12},{12,8},{16,20},{20,16},{24,28},{28,24},{1,5},{5... | collective-permute-start | bytes 7077896 | tf_op jit(solution)/shard_map/ppermute | solution.py:549
  228.8 25.3 %collective-permute-start.7 = (bf16[2,240,768]{2,1,0:T(8,128)(2,1)S(1)}, bf16[2,240,768]{2,1,0:T(8,128)(2,1)}, u32[]{:S(2)}, u32[]{:S(2)}) collective-permute-start(bf16[2,240,768]{2,1,0:T(8,128)(2,1)S(1)} %get-tuple-element.160), channel_id=1, source_target_pairs={{0,1},{1,0},{2,3},{3,2},{4,5},{5,4},{6,7},{7,6},{8,9},{9,8},{10,11... | collective-permute-start | bytes 2211848 | tf_op jit(solution)/shard_map/ppermute | solution.py:549
  232.4 24.4 %collective-permute-start.10 = (bf16[4,96,768]{2,1,0:T(8,128)(2,1)}, bf16[4,96,768]{2,1,0:T(8,128)(2,1)}, u32[]{:S(2)}, u32[]{:S(2)}) collective-permute-start(bf16[4,96,768]{2,1,0:T(8,128)(2,1)} %get-tuple-element.166), channel_id=1, source_target_pairs={{0,24},{4,28},{8,16},{12,20},{16,8},{20,12},{24,0},{28,4},{1,25},{... | collective-permute-start | bytes 1769480 | tf_op jit(solution)/shard_map/ppermute | solution.py:549
  233.8 26.4 %collective-permute-start.8 = (bf16[4,96,768]{2,1,0:T(8,128)(2,1)}, bf16[4,96,768]{2,1,0:T(8,128)(2,1)}, u32[]{:S(2)}, u32[]{:S(2)}) collective-permute-start(bf16[4,96,768]{2,1,0:T(8,128)(2,1)} %get-tuple-element.164), channel_id=1, source_target_pairs={{0,16},{4,20},{8,24},{12,28},{16,0},{20,4},{24,8},{28,12},{1,17},{... | collective-permute-start | bytes 1769480 | tf_op jit(solution)/shard_map/ppermute | solution.py:549
  235.3 24.9 %collective-permute-start.9 = (bf16[4,96,768]{2,1,0:T(8,128)(2,1)}, bf16[4,96,768]{2,1,0:T(8,128)(2,1)}, u32[]{:S(2)}, u32[]{:S(2)}) collective-permute-start(bf16[4,96,768]{2,1,0:T(8,128)(2,1)} %get-tuple-element.165), channel_id=1, source_target_pairs={{0,8},{4,12},{8,0},{12,4},{16,24},{20,28},{24,16},{28,20},{1,9},{5... | collective-permute-start | bytes 1769480 | tf_op jit(solution)/shard_map/ppermute | solution.py:549
  255.5 17.9 %collective-permute-start.12 = (bf16[240,768]{1,0:T(8,128)(2,1)S(1)}, bf16[240,768]{1,0:T(8,128)(2,1)S(1)}, u32[]{:S(2)}, u32[]{:S(2)}) collective-permute-start(bf16[240,768]{1,0:T(8,128)(2,1)S(1)} %get-tuple-element.201), channel_id=1, source_target_pairs={{0,2},{1,3},{2,0},{3,1},{4,6},{5,7},{6,4},{7,5},{8,10},{9,11},{10,... | collective-permute-start | bytes 1105928 | tf_op jit(solution)/shard_map/ppermute | solution.py:549
  262.0 16.4 %collective-permute-start.11 = (bf16[2,96,768]{2,1,0:T(8,128)(2,1)S(1)}, bf16[2,96,768]{2,1,0:T(8,128)(2,1)S(1)}, u32[]{:S(2)}, u32[]{:S(2)}) collective-permute-start(bf16[2,96,768]{2,1,0:T(8,128)(2,1)S(1)} %get-tuple-element.174), channel_id=1, source_target_pairs={{0,1},{1,0},{2,3},{3,2},{4,5},{5,4},{6,7},{7,6},{8,9},{9,8},{10,11... | collective-permute-start | bytes 884744 | tf_op jit(solution)/shard_map/ppermute | solution.py:549
  278.4 9.0 %collective-permute-start.13 = (bf16[96,768]{1,0:T(8,128)(2,1)S(1)}, bf16[96,768]{1,0:T(8,128)(2,1)S(1)}, u32[]{:S(2)}, u32[]{:S(2)}) collective-permute-start(bf16[96,768]{1,0:T(8,128)(2,1)S(1)} %fusion.4), channel_id=1, source_target_pairs={{0,2},{1,3},{2,0},{3,1},{4,6},{5,7},{6,4},{7,5},{8,10},{9,11},{10,... | collective-permute-start | bytes 442376 | tf_op jit(solution)/shard_map/ppermute | solution.py:549
  279.3 16.4 %collective-permute-start.16 = (bf16[240,768]{1,0:T(8,128)(2,1)S(1)}, bf16[240,768]{1,0:T(8,128)(2,1)S(1)}, u32[]{:S(2)}, u32[]{:S(2)}) collective-permute-start(bf16[240,768]{1,0:T(8,128)(2,1)S(1)} %add_convert_fusion.refs_0_), channel_id=1, source_target_pairs={{0,16},{4,20},{8,24},{12,28},{16,0},{20,4},{24,8},{28,12},{1,17},{... | collective-permute-start | bytes 1105928 | tf_op jit(solution)/shard_map/ppermute | solution.py:549
  279.9 15.8 %collective-permute-start.17 = (bf16[240,768]{1,0:T(8,128)(2,1)S(1)}, bf16[240,768]{1,0:T(8,128)(2,1)S(1)}, u32[]{:S(2)}, u32[]{:S(2)}) collective-permute-start(bf16[240,768]{1,0:T(8,128)(2,1)S(1)} %add_convert_fusion.refs_0_), channel_id=1, source_target_pairs={{0,8},{4,12},{8,0},{12,4},{16,24},{20,28},{24,16},{28,20},{1,9},{5... | collective-permute-start | bytes 1105928 | tf_op jit(solution)/shard_map/ppermute | solution.py:549
  281.4 16.9 %collective-permute-start.18 = (bf16[240,768]{1,0:T(8,128)(2,1)S(1)}, bf16[240,768]{1,0:T(8,128)(2,1)S(1)}, u32[]{:S(2)}, u32[]{:S(2)}) collective-permute-start(bf16[240,768]{1,0:T(8,128)(2,1)S(1)} %add_convert_fusion.refs_0_), channel_id=1, source_target_pairs={{0,24},{4,28},{8,16},{12,20},{16,8},{20,12},{24,0},{28,4},{1,25},{... | collective-permute-start | bytes 1105928 | tf_op jit(solution)/shard_map/ppermute | solution.py:549
  287.5 3.6 %collective-permute-start.14 = (bf16[1,128]{1,0:T(2,128)(2,1)S(1)}, bf16[1,128]{1,0:T(2,128)(2,1)S(1)}, u32[]{:S(2)}, u32[]{:S(2)}) collective-permute-start(bf16[1,128]{1,0:T(2,128)(2,1)S(1)} %get-tuple-element.179), channel_id=1, source_target_pairs={{0,1},{1,0},{2,3},{3,2},{4,5},{5,4},{6,7},{7,6},{8,9},{9,8},{10,11... | collective-permute-start | bytes 776 | tf_op jit(solution)/shard_map/ppermute | solution.py:549
  291.2 4.5 %collective-permute-start.15 = (bf16[2,128]{1,0:T(2,128)(2,1)S(1)}, bf16[2,128]{1,0:T(2,128)(2,1)S(1)}, u32[]{:S(2)}, u32[]{:S(2)}) collective-permute-start(bf16[2,128]{1,0:T(2,128)(2,1)S(1)} %pad_maximum_fusion.1), channel_id=1, source_target_pairs={{0,2},{1,3},{2,0},{3,1},{4,6},{5,7},{6,4},{7,5},{8,10},{9,11},{10,... | collective-permute-start | bytes 1544 | tf_op jit(solution)/shard_map/ppermute | solution.py:549
  299.0 3.6 %collective-permute-start.22 = (bf16[960,768]{1,0:T(8,128)(2,1)S(1)}, bf16[960,768]{1,0:T(8,128)(2,1)S(1)}, u32[]{:S(2)}, u32[]{:S(2)}) collective-permute-start(bf16[960,768]{1,0:T(8,128)(2,1)S(1)} %bitcast.47), channel_id=1, source_target_pairs={{0,4},{4,0},{8,12},{12,8},{16,20},{20,16},{24,28},{28,24},{1,5},{5... | collective-permute-start | bytes 4423688 | tf_op jit(solution)/shard_map/ppermute | solution.py:549
  299.1 6.3 %collective-permute-start.19 = (bf16[96,768]{1,0:T(8,128)(2,1)S(1)}, bf16[96,768]{1,0:T(8,128)(2,1)S(1)}, u32[]{:S(2)}, u32[]{:S(2)}) collective-permute-start(bf16[96,768]{1,0:T(8,128)(2,1)S(1)} %fusion.2.refs_0_), channel_id=1, source_target_pairs={{0,16},{4,20},{8,24},{12,28},{16,0},{20,4},{24,8},{28,12},{1,17},{... | collective-permute-start | bytes 442376 | tf_op jit(solution)/shard_map/ppermute | solution.py:549
  299.4 6.7 %collective-permute-start.20 = (bf16[96,768]{1,0:T(8,128)(2,1)S(1)}, bf16[96,768]{1,0:T(8,128)(2,1)S(1)}, u32[]{:S(2)}, u32[]{:S(2)}) collective-permute-start(bf16[96,768]{1,0:T(8,128)(2,1)S(1)} %fusion.2.refs_0_), channel_id=1, source_target_pairs={{0,8},{4,12},{8,0},{12,4},{16,24},{20,28},{24,16},{28,20},{1,9},{5... | collective-permute-start | bytes 442376 | tf_op jit(solution)/shard_map/ppermute | solution.py:549
  300.9 8.8 %collective-permute-start.21 = (bf16[96,768]{1,0:T(8,128)(2,1)S(1)}, bf16[96,768]{1,0:T(8,128)(2,1)S(1)}, u32[]{:S(2)}, u32[]{:S(2)}) collective-permute-start(bf16[96,768]{1,0:T(8,128)(2,1)S(1)} %fusion.2.refs_0_), channel_id=1, source_target_pairs={{0,24},{4,28},{8,16},{12,20},{16,8},{20,12},{24,0},{28,4},{1,25},{... | collective-permute-start | bytes 442376 | tf_op jit(solution)/shard_map/ppermute | solution.py:549
  310.3 2.1 collective-permute-start.23
  (25 other events, 214.5 us)

commit v6 on v5

--- a/solution.py
+++ b/solution.py
@@ -962,7 +962,7 @@
     time_row, late_send, late_keep = late_grads(
         core, grads, xm_attn, attn_sums, late_mods, ada_weight, column, early_parts, sp
     )
-    hidden_grad = exchange(after(hg, left, right))
+    hidden_grad = exchange(hg)
     late_got = pair_permute(late_send, CORE)
     left_got, right_got = after((left_got, right_got), late_keep)
     if lax.axis_size("dp") > 2 * SECOND:

time: 315 us -> 316 us (level)
  transfers between devices with their start and end apart: 28 -> 28, of which waited for: 17 -> 17; matrix products, arithmetic and copies ran while one was open for 3% -> 3% of each run, Pallas kernels for 32% -> 34%
where the time goes in v6:
time: 316 us; the launch traced here: 315 us
  Pallas kernels  156 us (49%)
  waiting for transfers between devices  104 us (33%)
  starting transfers between devices  43.4 us (14%)
  other arithmetic  8.68 us (3%)
    ppermute x24, waiting for transfers between devices, pair_permute(): return lax.ppermute(value, axis, [(i, i ^ bit) for i in range(n)])  60 us
    all_to_all x4, waiting for transfers between devices, exchange(): return lax.all_to_all(values, 'sp', split_axis=0, concat_axis=0, tiled=True)  43.8 us
    pallas_call x1, Pallas kernels, attention_backward(): pl.pallas_call(functools.partial(attention_backward_kernel, pairs=pairs),...  40.5 us
    pallas_call x1, Pallas kernels, feed_forward(): pl.pallas_call(mlp_kernel, grid=(length // rows,), in_specs=[block, block...  35.6 us
    ppermute x24, starting transfers between devices, pair_permute(): return lax.ppermute(value, axis, [(i, i ^ bit) for i in range(n)])  24.4 us
    pallas_call x1, Pallas kernels, attention_forward(): pl.pallas_call(functools.partial(attention_forward_kernel, chunk=length /...  19.6 us
    all_to_all x4, starting transfers between devices, exchange(): return lax.all_to_all(values, 'sp', split_axis=0, concat_axis=0, tiled=True)  19.1 us
    pallas_call x1, Pallas kernels, column_grad(): pl.pallas_call(functools.partial(column_grad_kernel, blocks=n), grid_spec...  11.9 us
  transfers between devices with their start and end apart: 28, of which 17 were waited for; matrix products, arithmetic and copies ran while one was open for 3% of the time, Pallas kernels for 34%

profile of v6, /device:TPU:0, one launch (start us, length us, event | category | flops | bytes accessed | tf_op | source)
XLA Modules:
  0.0 314.9 jit_solution(8979139639750188276)
XLA Ops:
  0.7 6.5 %all-to-all-start = ((bf16[4,256,768]{2,1,0:T(8,128)(2,1)}), bf16[4,256,768]{2,1,0:T(8,128)(2,1)S(1)}, u32[]{:S(2)}, u32[]{:S(2)}) async-start(bf16[4,256,768]{2,1,0:T(8,128)(2,1)} %param.13), calls=%async_computation | async-start | bytes 3145728 | tf_op jit(solution)/shard_map/all_to_all | solution.py:888
  8.1 3.1 multiply_sine_fusion
  11.1 33.0 %all-to-all-done = bf16[4,256,768]{2,1,0:T(8,128)(2,1)S(1)} async-done(((bf16[4,256,768]{2,1,0:T(8,128)(2,1)}), bf16[4,256,768]{2,1,0:T(8,128)(2,1)S(1)}, u32[]{:S(2)}, u32[]{:S(2)}) %all-to-all-start) | async-done | bytes 1572896 | tf_op jit(solution)/shard_map/all_to_all | solution.py:888
  44.1 4.3 %all-to-all-start.1 = ((bf16[4,256,768]{2,1,0:T(8,128)(2,1)}), bf16[4,256,768]{2,1,0:T(8,128)(2,1)}, u32[]{:S(2)}, u32[]{:S(2)}) async-start(bf16[4,256,768]{2,1,0:T(8,128)(2,1)} %param.25), calls=%async_computation.1 | async-start | bytes 3145728 | tf_op jit(solution)/shard_map/all_to_all | solution.py:888
  48.5 8.6 %project_qkv.1 = (bf16[1024,768]{1,0:T(8,128)(2,1)}, bf16[1024,768]{1,0:T(8,128)(2,1)}, bf16[1024,768]{1,0:T(8,128)(2,1)}, bf16[1024,768]{1,0:T(8,128)(2,1)}) custom-call(bf16[1024,768]{1,0:T(8,128)(2,1)S(1)} %bitcast.42, f32[8,768]{1,0:T(8,128)S(1)} %get-tuple-element.108.mod_ref, bf16[768,2304]{1,0:T(8,128)(2,1)} %w_ref.3, ...), custom_call_target="tpu_custom_call" | custom-call | flops 40000000000 | bytes 100000000 | tf_op jit(solution)/shard_map/project_qkv/pallas_call | solution.py:99
  57.1 19.6 %attention_forward.1 = (bf16[1024,768]{1,0:T(8,128)(2,1)}, f32[6,2,1024]{2,1,0:T(2,128)}) custom-call(bf16[1024,768]{1,0:T(8,128)(2,1)} %get-tuple-element.109.q_ref, bf16[1024,768]{1,0:T(8,128)(2,1)} %get-tuple-element.110.k_ref, bf16[1024,768]{1,0:T(8,128)(2,1)} %get-tuple-element.111.v_ref), custom_call_target="tpu_custom_call" | custom-call | flops 40000000000 | bytes 100000000 | tf_op jit(solution)/shard_map/attention_forward/pallas_call | solution.py:151
  76.7 8.3 %all-to-all-done.1 = bf16[4,256,768]{2,1,0:T(8,128)(2,1)} async-done(((bf16[4,256,768]{2,1,0:T(8,128)(2,1)}), bf16[4,256,768]{2,1,0:T(8,128)(2,1)}, u32[]{:S(2)}, u32[]{:S(2)}) %all-to-all-start.1) | async-done | bytes 1572896 | tf_op jit(solution)/shard_map/all_to_all | solution.py:888
  85.0 35.6 %feed_forward.1 = (bf16[2,1024,768]{2,1,0:T(8,128)(2,1)}, bf16[1024,3072]{1,0:T(8,128)(2,1)}, bf16[1024,768]{1,0:T(8,128)(2,1)}, bf16[5,1024,768]{2,1,0:T(8,128)...) custom-call(bf16[1024,768]{1,0:T(8,128)(2,1)S(1)} %bitcast.43, ...), custom_call_target="tpu_custom_call" | custom-call | flops 40000000000 | bytes 100000000 | tf_op jit(solution)/shard_map/feed_forward/pallas_call | solution.py:335
  120.6 11.9 %column_grad.1 = (bf16[4,576,768]{2,1,0:T(8,128)(2,1)}, bf16[4,576,768]{2,1,0:T(8,128)(2,1)}, f32[4,768]{1,0:T(4,128)S(1)}) custom-call(s32[1]{0:T(128)} %bitcast.6.core_ref, f32[8,768]{1,0:T(8,128)S(1)} %get-tuple-element.117.sum_ref, f32[1,3072]{1,0:T(1,128)S(1)} %get-tuple-element.118.up_sum_ref, f32[8,768]{1,0:T(8,128)S(1)} %get-tuple-element.119.mod_ref, ...), custom_call_target="tpu_custom_call" | custom-call | flops 40000000000 | bytes 100000000 | tf_op jit(solution)/shard_map/column_grad/pallas_call | solution.py:523
  132.5 9.2 %row_grad.1 = (bf16[4,384,768]{2,1,0:T(8,128)(2,1)}, bf16[4,384,768]{2,1,0:T(8,128)(2,1)}) custom-call(s32[1]{0:T(128)} %bitcast.6.core_ref, bf16[1024,3072]{1,0:T(8,128)(2,1)} %get-tuple-element.124.a_ref, bf16[1024,768]{1,0:T(8,128)(2,1)} %get-tuple-element.125.b_ref), custom_call_target="tpu_custom_call" | custom-call | flops 40000000000 | bytes 100000000 | tf_op jit(solution)/shard_map/row_grad/pallas_call | solution.py:454
  142.2 3.6 %all-to-all-start.2 = ((bf16[4,256,768]{2,1,0:T(8,128)(2,1)}), bf16[4,256,768]{2,1,0:T(8,128)(2,1)S(1)}, u32[]{:S(2)}, u32[]{:S(2)}) async-start(bf16[4,256,768]{2,1,0:T(8,128)(2,1)} %bitcast.54), calls=%async_computation.2 | async-start | bytes 3145728 | tf_op jit(solution)/shard_map/all_to_all | solution.py:888
  146.8 8.8 %first_halves.1 = (bf16[4,480,384]{2,1,0:T(8,128)(2,1)}, bf16[4,480,384]{2,1,0:T(8,128)(2,1)}, bf16[4,480,384]{2,1,0:T(8,128)(2,1)}, bf16[4,480,384]{2,1,0:T(8,128)(2,1)}) custom-call(s32[3]{0:T(128)S(1)} %pad_add_fusion.at_ref, bf16[4,384,768]{2,1,0:T(8,128)(2,1)} %get-tuple-element.126.row_keep, bf16[4,384,768]{2,1,0:T(8,128)(2,1)} %collective-permute-done.row_got, ...), custom_call_target="tpu_custom_call" | custom-call | flops 40000000000 | bytes 100000000 | tf_op jit(solution)/shard_map/first_halves/pallas_call | solution.py:594
  158.7 40.5 %attention_backward.1 = (bf16[3,1024,768]{2,1,0:T(8,128)(2,1)}, bf16[1024,768]{1,0:T(8,128)(2,1)}, f32[8,768]{1,0:T(8,128)S(1)}) custom-call(bf16[1024,768]{1,0:T(8,128)(2,1)S(1)} %copy-done.11, bf16[1024,768]{1,0:T(8,128)(2,1)S(1)} %copy-done.12, bf16[1024,768]{1,0:T(8,128)(2,1)S(1)} %copy-done.13, bf16[1024,768]{1,0:T(8,128)(2,1)S(1)} %copy-done.15, ...), custom_call_target="tpu_custom_call" | custom-call | flops 40000000000 | bytes 100000000 | tf_op jit(solution)/shard_map/attention_backward/pallas_call | solution.py:237
  199.2 4.7 %all-to-all-start.3 = ((bf16[4,256,768]{2,1,0:T(8,128)(2,1)}), bf16[4,256,768]{2,1,0:T(8,128)(2,1)}, u32[]{:S(2)}, u32[]{:S(2)}) async-start(bf16[4,256,768]{2,1,0:T(8,128)(2,1)} %bitcast.55), calls=%async_computation.3 | async-start | bytes 3145728 | tf_op jit(solution)/shard_map/all_to_all | solution.py:888
  204.0 4.6 %second_halves.1 = (bf16[4,240,384]{2,1,0:T(8,128)(2,1)}, bf16[4,240,384]{2,1,0:T(8,128)(2,1)}, bf16[4,240,384]{2,1,0:T(8,128)(2,1)}, bf16[4,240,384]{2,1,0:T(8,128)(2,1)}) custom-call(s32[3]{0:T(128)S(1)} %pad_add_fusion.at_ref, bf16[4,2,240,384]{3,2,1,0:T(8,128)(2,1)} %bitcast.56, bf16[4,2,240,384]{3,2,1,0:T(8,128)(2,1)} %bitcast.12.refs_1_, ...), custom_call_target="tpu_custom_call" | custom-call | flops 40000000000 | bytes 100000000 | tf_op jit(solution)/shard_map/second_halves/pallas_call | solution.py:621
  210.8 5.4 %late_grads.1 = (bf16[1,128]{1,0:T(2,128)(2,1)S(1)}, bf16[4,384,768]{2,1,0:T(8,128)(2,1)S(1)}, bf16[4,384,768]{2,1,0:T(8,128)(2,1)S(1)}) custom-call(s32[1]{0:T(128)} %bitcast.6.core_ref, f32[8,768]{1,0:T(8,128)S(1)} %get-tuple-element.140.sum_ref, f32[8,768]{1,0:T(8,128)S(1)} %get-tuple-element.141.mod_ref, bf16[128,4608]{1,0:T(8,128)(2,1)S(1)} %copy-done.1, ...), custom_call_target="tpu_custom_call" | custom-call | flops 40000000000 | bytes 100000000 | tf_op jit(solution)/shard_map/late_grads/pallas_call | solution.py:415
  216.3 10.7 %collective-permute-done.5.refs_1_ = bf16[4,240,384]{2,1,0:T(8,128)(2,1)S(1)} collective-permute-done((bf16[4,240,384]{2,1,0:T(8,128)(2,1)}, bf16[4,240,384]{2,1,0:T(8,128)(2,1)S(1)}, u32[]{:S(2)}, u32[]{:S(2)}) %collective-permute-start.5) | collective-permute-done | bytes 737312 | tf_op jit(solution)/shard_map/ppermute | solution.py:549
  230.4 2.1 quarters.1
  238.5 2.5 all-to-all-done.3
  241.0 13.1 %collective-permute-done.7 = bf16[2,240,768]{2,1,0:T(8,128)(2,1)} collective-permute-done((bf16[2,240,768]{2,1,0:T(8,128)(2,1)S(1)}, bf16[2,240,768]{2,1,0:T(8,128)(2,1)}, u32[]{:S(2)}, u32[]{:S(2)}) %collective-permute-start.7) | collective-permute-done | bytes 737312 | tf_op jit(solution)/shard_map/ppermute | solution.py:549
  256.8 4.4 %collective-permute-done.8.refs_1_ = bf16[4,96,768]{2,1,0:T(8,128)(2,1)} collective-permute-done((bf16[4,96,768]{2,1,0:T(8,128)(2,1)}, bf16[4,96,768]{2,1,0:T(8,128)(2,1)}, u32[]{:S(2)}, u32[]{:S(2)}) %collective-permute-start.8) | collective-permute-done | bytes 589856 | tf_op jit(solution)/shard_map/ppermute | solution.py:549
  261.2 1.7 near_halves.3
  263.9 9.5 %collective-permute-done.12 = bf16[240,768]{1,0:T(8,128)(2,1)S(1)} collective-permute-done((bf16[240,768]{1,0:T(8,128)(2,1)S(1)}, bf16[240,768]{1,0:T(8,128)(2,1)S(1)}, u32[]{:S(2)}, u32[]{:S(2)}) %collective-permute-start.12) | collective-permute-done | bytes 368672 | tf_op jit(solution)/shard_map/ppermute | solution.py:549
  273.5 4.9 %collective-permute-done.11 = bf16[2,96,768]{2,1,0:T(8,128)(2,1)S(1)} collective-permute-done((bf16[2,96,768]{2,1,0:T(8,128)(2,1)S(1)}, bf16[2,96,768]{2,1,0:T(8,128)(2,1)S(1)}, u32[]{:S(2)}, u32[]{:S(2)}) %collective-permute-start.11) | collective-permute-done | bytes 294944 | tf_op jit(solution)/shard_map/ppermute | solution.py:549
  278.4 1.9 collective-permute-start.13
  283.8 3.7 %collective-permute-done.13 = bf16[96,768]{1,0:T(8,128)(2,1)S(1)} collective-permute-done((bf16[96,768]{1,0:T(8,128)(2,1)S(1)}, bf16[96,768]{1,0:T(8,128)(2,1)S(1)}, u32[]{:S(2)}, u32[]{:S(2)}) %collective-permute-start.13) | collective-permute-done | bytes 147488 | tf_op jit(solution)/shard_map/ppermute | solution.py:549
  287.9 3.2 %collective-permute-done.14 = bf16[1,128]{1,0:T(2,128)(2,1)S(1)} collective-permute-done((bf16[1,128]{1,0:T(2,128)(2,1)S(1)}, bf16[1,128]{1,0:T(2,128)(2,1)S(1)}, u32[]{:S(2)}, u32[]{:S(2)}) %collective-permute-start.14) | collective-permute-done | bytes 288 | tf_op jit(solution)/shard_map/ppermute | solution.py:549
  291.1 1.8 collective-permute-start.15
  292.9 3.3 %convert_element_type.142 = f32[4,256,768]{2,1,0:T(8,128)} convert(bf16[4,256,768]{2,1,0:T(8,128)(2,1)} %all-to-all-done.3) | non-fusion elementwise | flops 786432 | bytes 4718592 | tf_op jit(solution)/shard_map/convert_element_type | solution.py:1001
  296.3 2.9 collective-permute-done.18.refs_3_
  303.5 2.6 finish.1
  307.3 3.3 %collective-permute-done.21.refs_3_ = bf16[96,768]{1,0:T(8,128)(2,1)S(1)} collective-permute-done((bf16[96,768]{1,0:T(8,128)(2,1)S(1)}, bf16[96,768]{1,0:T(8,128)(2,1)S(1)}, u32[]{:S(2)}, u32[]{:S(2)}) %collective-permute-start.21) | collective-permute-done | bytes 147488 | tf_op jit(solution)/shard_map/ppermute | solution.py:549
  (130 shorter events, 34.4 us)
Async XLA Ops:
  0.7 43.4 %all-to-all-start = ((bf16[4,256,768]{2,1,0:T(8,128)(2,1)}), bf16[4,256,768]{2,1,0:T(8,128)(2,1)S(1)}, u32[]{:S(2)}, u32[]{:S(2)}) async-start(bf16[4,256,768]{2,1,0:T(8,128)(2,1)} %param.13), calls=%async_computation | async-start | bytes 3145728 | tf_op jit(solution)/shard_map/all_to_all | solution.py:888
  7.9 40.6 %copy-start.6 = (f32[8,768]{1,0:T(8,128)}, f32[8,768]{1,0:T(8,128)S(1)}, u32[]{:S(2)}) copy-start(f32[8,768]{1,0:T(8,128)S(1)} %get-tuple-element.108.mod_ref) | copy-start | bytes 73732
  8.1 112.6 %copy-start.4 = (f32[128,1]{1,0:T(8,128)}, f32[128,1]{1,0:T(8,128)S(1)}, u32[]{:S(2)}) copy-start(f32[128,1]{1,0:T(8,128)S(1)} %copy.26.timing_ref) | copy-start | bytes 1540
  44.1 40.9 %all-to-all-start.1 = ((bf16[4,256,768]{2,1,0:T(8,128)(2,1)}), bf16[4,256,768]{2,1,0:T(8,128)(2,1)}, u32[]{:S(2)}, u32[]{:S(2)}) async-start(bf16[4,256,768]{2,1,0:T(8,128)(2,1)} %param.25), calls=%async_computation.1 | async-start | bytes 3145728 | tf_op jit(solution)/shard_map/all_to_all | solution.py:888
  57.1 27.9 %copy-start.9 = (bf16[768,768]{1,0:T(8,128)(2,1)S(1)}, bf16[768,768]{1,0:T(8,128)(2,1)}, u32[]{:S(2)}) copy-start(bf16[768,768]{1,0:T(8,128)(2,1)} %wo_ref.1) | copy-start | bytes 3538948
  132.5 14.2 %collective-permute-start.1 = (bf16[4,576,768]{2,1,0:T(8,128)(2,1)}, bf16[4,576,768]{2,1,0:T(8,128)(2,1)}, u32[]{:S(2)}, u32[]{:S(2)}) collective-permute-start(bf16[4,576,768]{2,1,0:T(8,128)(2,1)} %get-tuple-element.128), channel_id=1, source_target_pairs={{0,4},{4,0},{8,12},{12,8},{16,20},{20,16},{24,28},{28,24},{1,5},{5... | collective-permute-start | bytes 10616840 | tf_op jit(solution)/shard_map/ppermute | solution.py:549
  141.7 5.0 %collective-permute-start = (bf16[4,384,768]{2,1,0:T(8,128)(2,1)}, bf16[4,384,768]{2,1,0:T(8,128)(2,1)}, u32[]{:S(2)}, u32[]{:S(2)}) collective-permute-start(bf16[4,384,768]{2,1,0:T(8,128)(2,1)} %get-tuple-element.127), channel_id=1, source_target_pairs={{0,4},{4,0},{8,12},{12,8},{16,20},{20,16},{24,28},{28,24},{1,5},{5... | collective-permute-start | bytes 7077896 | tf_op jit(solution)/shard_map/ppermute | solution.py:549
  142.2 57.0 %all-to-all-start.2 = ((bf16[4,256,768]{2,1,0:T(8,128)(2,1)}), bf16[4,256,768]{2,1,0:T(8,128)(2,1)S(1)}, u32[]{:S(2)}, u32[]{:S(2)}) async-start(bf16[4,256,768]{2,1,0:T(8,128)(2,1)} %bitcast.54), calls=%async_computation.2 | async-start | bytes 3145728 | tf_op jit(solution)/shard_map/all_to_all | solution.py:888
  155.6 48.3 %collective-permute-start.2 = (bf16[4,480,384]{2,1,0:T(8,128)(2,1)}, bf16[4,480,384]{2,1,0:T(8,128)(2,1)}, u32[]{:S(2)}, u32[]{:S(2)}) collective-permute-start(bf16[4,480,384]{2,1,0:T(8,128)(2,1)} %get-tuple-element.129), channel_id=1, source_target_pairs={{0,8},{4,12},{8,0},{12,4},{16,24},{20,28},{24,16},{28,20},{1,9},{5... | collective-permute-start | bytes 4423688 | tf_op jit(solution)/shard_map/ppermute | solution.py:549
  157.1 46.8 %collective-permute-start.3 = (bf16[4,480,384]{2,1,0:T(8,128)(2,1)}, bf16[4,480,384]{2,1,0:T(8,128)(2,1)}, u32[]{:S(2)}, u32[]{:S(2)}) collective-permute-start(bf16[4,480,384]{2,1,0:T(8,128)(2,1)} %get-tuple-element.130), channel_id=1, source_target_pairs={{0,16},{4,20},{8,24},{12,28},{16,0},{20,4},{24,8},{28,12},{1,17},{... | collective-permute-start | bytes 4423688 | tf_op jit(solution)/shard_map/ppermute | solution.py:549
  199.2 41.9 %all-to-all-start.3 = ((bf16[4,256,768]{2,1,0:T(8,128)(2,1)}), bf16[4,256,768]{2,1,0:T(8,128)(2,1)}, u32[]{:S(2)}, u32[]{:S(2)}) async-start(bf16[4,256,768]{2,1,0:T(8,128)(2,1)} %bitcast.55), calls=%async_computation.3 | async-start | bytes 3145728 | tf_op jit(solution)/shard_map/all_to_all | solution.py:888
  208.6 18.4 %collective-permute-start.5 = (bf16[4,240,384]{2,1,0:T(8,128)(2,1)}, bf16[4,240,384]{2,1,0:T(8,128)(2,1)S(1)}, u32[]{:S(2)}, u32[]{:S(2)}) collective-permute-start(bf16[4,240,384]{2,1,0:T(8,128)(2,1)} %get-tuple-element.151), channel_id=1, source_target_pairs={{0,16},{4,20},{8,24},{12,28},{16,0},{20,4},{24,8},{28,12},{1,17},{... | collective-permute-start | bytes 2211848 | tf_op jit(solution)/shard_map/ppermute | solution.py:549
  209.3 18.7 %collective-permute-start.6 = (bf16[4,240,384]{2,1,0:T(8,128)(2,1)}, bf16[4,240,384]{2,1,0:T(8,128)(2,1)S(1)}, u32[]{:S(2)}, u32[]{:S(2)}) collective-permute-start(bf16[4,240,384]{2,1,0:T(8,128)(2,1)} %get-tuple-element.152), channel_id=1, source_target_pairs={{0,8},{4,12},{8,0},{12,4},{16,24},{20,28},{24,16},{28,20},{1,9},{5... | collective-permute-start | bytes 2211848 | tf_op jit(solution)/shard_map/ppermute | solution.py:549
  216.3 14.2 %collective-permute-start.4 = (bf16[4,384,768]{2,1,0:T(8,128)(2,1)S(1)}, bf16[4,384,768]{2,1,0:T(8,128)(2,1)S(1)}, u32[]{:S(2)}, u32[]{:S(2)}) collective-permute-start(bf16[4,384,768]{2,1,0:T(8,128)(2,1)S(1)} %get-tuple-element.150), channel_id=1, source_target_pairs={{0,4},{4,0},{8,12},{12,8},{16,20},{20,16},{24,28},{28,24},{1,5},{5... | collective-permute-start | bytes 7077896 | tf_op jit(solution)/shard_map/ppermute | solution.py:549
  228.9 25.3 %collective-permute-start.7 = (bf16[2,240,768]{2,1,0:T(8,128)(2,1)S(1)}, bf16[2,240,768]{2,1,0:T(8,128)(2,1)}, u32[]{:S(2)}, u32[]{:S(2)}) collective-permute-start(bf16[2,240,768]{2,1,0:T(8,128)(2,1)S(1)} %get-tuple-element.159), channel_id=1, source_target_pairs={{0,1},{1,0},{2,3},{3,2},{4,5},{5,4},{6,7},{7,6},{8,9},{9,8},{10,11... | collective-permute-start | bytes 2211848 | tf_op jit(solution)/shard_map/ppermute | solution.py:549
  233.4 23.4 %collective-permute-start.10 = (bf16[4,96,768]{2,1,0:T(8,128)(2,1)}, bf16[4,96,768]{2,1,0:T(8,128)(2,1)}, u32[]{:S(2)}, u32[]{:S(2)}) collective-permute-start(bf16[4,96,768]{2,1,0:T(8,128)(2,1)} %get-tuple-element.164), channel_id=1, source_target_pairs={{0,24},{4,28},{8,16},{12,20},{16,8},{20,12},{24,0},{28,4},{1,25},{... | collective-permute-start | bytes 1769480 | tf_op jit(solution)/shard_map/ppermute | solution.py:549
  234.8 26.4 %collective-permute-start.8 = (bf16[4,96,768]{2,1,0:T(8,128)(2,1)}, bf16[4,96,768]{2,1,0:T(8,128)(2,1)}, u32[]{:S(2)}, u32[]{:S(2)}) collective-permute-start(bf16[4,96,768]{2,1,0:T(8,128)(2,1)} %get-tuple-element.162), channel_id=1, source_target_pairs={{0,16},{4,20},{8,24},{12,28},{16,0},{20,4},{24,8},{28,12},{1,17},{... | collective-permute-start | bytes 1769480 | tf_op jit(solution)/shard_map/ppermute | solution.py:549
  236.3 24.9 %collective-permute-start.9 = (bf16[4,96,768]{2,1,0:T(8,128)(2,1)}, bf16[4,96,768]{2,1,0:T(8,128)(2,1)}, u32[]{:S(2)}, u32[]{:S(2)}) collective-permute-start(bf16[4,96,768]{2,1,0:T(8,128)(2,1)} %get-tuple-element.163), channel_id=1, source_target_pairs={{0,8},{4,12},{8,0},{12,4},{16,24},{20,28},{24,16},{28,20},{1,9},{5... | collective-permute-start | bytes 1769480 | tf_op jit(solution)/shard_map/ppermute | solution.py:549
  238.5 22.7 %copy-start.20 = (bf16[4,96,768]{2,1,0:T(8,128)(2,1)S(1)}, bf16[4,96,768]{2,1,0:T(8,128)(2,1)}, u32[]{:S(2)}) copy-start(bf16[4,96,768]{2,1,0:T(8,128)(2,1)} %copy-done.19) | copy-start | bytes 1769476
  255.5 17.9 %collective-permute-start.12 = (bf16[240,768]{1,0:T(8,128)(2,1)S(1)}, bf16[240,768]{1,0:T(8,128)(2,1)S(1)}, u32[]{:S(2)}, u32[]{:S(2)}) collective-permute-start(bf16[240,768]{1,0:T(8,128)(2,1)S(1)} %get-tuple-element.199), channel_id=1, source_target_pairs={{0,2},{1,3},{2,0},{3,1},{4,6},{5,7},{6,4},{7,5},{8,10},{9,11},{10,... | collective-permute-start | bytes 1105928 | tf_op jit(solution)/shard_map/ppermute | solution.py:549
  262.9 15.4 %collective-permute-start.11 = (bf16[2,96,768]{2,1,0:T(8,128)(2,1)S(1)}, bf16[2,96,768]{2,1,0:T(8,128)(2,1)S(1)}, u32[]{:S(2)}, u32[]{:S(2)}) collective-permute-start(bf16[2,96,768]{2,1,0:T(8,128)(2,1)S(1)} %get-tuple-element.172), channel_id=1, source_target_pairs={{0,1},{1,0},{2,3},{3,2},{4,5},{5,4},{6,7},{7,6},{8,9},{9,8},{10,11... | collective-permute-start | bytes 884744 | tf_op jit(solution)/shard_map/ppermute | solution.py:549
  278.4 9.0 %collective-permute-start.13 = (bf16[96,768]{1,0:T(8,128)(2,1)S(1)}, bf16[96,768]{1,0:T(8,128)(2,1)S(1)}, u32[]{:S(2)}, u32[]{:S(2)}) collective-permute-start(bf16[96,768]{1,0:T(8,128)(2,1)S(1)} %fusion.4), channel_id=1, source_target_pairs={{0,2},{1,3},{2,0},{3,1},{4,6},{5,7},{6,4},{7,5},{8,10},{9,11},{10,... | collective-permute-start | bytes 442376 | tf_op jit(solution)/shard_map/ppermute | solution.py:549
  280.3 16.0 %collective-permute-start.16 = (bf16[240,768]{1,0:T(8,128)(2,1)S(1)}, bf16[240,768]{1,0:T(8,128)(2,1)S(1)}, u32[]{:S(2)}, u32[]{:S(2)}) collective-permute-start(bf16[240,768]{1,0:T(8,128)(2,1)S(1)} %add_convert_fusion.refs_0_), channel_id=1, source_target_pairs={{0,16},{4,20},{8,24},{12,28},{16,0},{20,4},{24,8},{28,12},{1,17},{... | collective-permute-start | bytes 1105928 | tf_op jit(solution)/shard_map/ppermute | solution.py:549
  280.9 15.4 %collective-permute-start.17 = (bf16[240,768]{1,0:T(8,128)(2,1)S(1)}, bf16[240,768]{1,0:T(8,128)(2,1)S(1)}, u32[]{:S(2)}, u32[]{:S(2)}) collective-permute-start(bf16[240,768]{1,0:T(8,128)(2,1)S(1)} %add_convert_fusion.refs_0_), channel_id=1, source_target_pairs={{0,8},{4,12},{8,0},{12,4},{16,24},{20,28},{24,16},{28,20},{1,9},{5... | collective-permute-start | bytes 1105928 | tf_op jit(solution)/shard_map/ppermute | solution.py:549
  282.4 16.8 %collective-permute-start.18 = (bf16[240,768]{1,0:T(8,128)(2,1)S(1)}, bf16[240,768]{1,0:T(8,128)(2,1)S(1)}, u32[]{:S(2)}, u32[]{:S(2)}) collective-permute-start(bf16[240,768]{1,0:T(8,128)(2,1)S(1)} %add_convert_fusion.refs_0_), channel_id=1, source_target_pairs={{0,24},{4,28},{8,16},{12,20},{16,8},{20,12},{24,0},{28,4},{1,25},{... | collective-permute-start | bytes 1105928 | tf_op jit(solution)/shard_map/ppermute | solution.py:549
  287.5 3.6 %collective-permute-start.14 = (bf16[1,128]{1,0:T(2,128)(2,1)S(1)}, bf16[1,128]{1,0:T(2,128)(2,1)S(1)}, u32[]{:S(2)}, u32[]{:S(2)}) collective-permute-start(bf16[1,128]{1,0:T(2,128)(2,1)S(1)} %get-tuple-element.177), channel_id=1, source_target_pairs={{0,1},{1,0},{2,3},{3,2},{4,5},{5,4},{6,7},{7,6},{8,9},{9,8},{10,11... | collective-permute-start | bytes 776 | tf_op jit(solution)/shard_map/ppermute | solution.py:549
  291.1 5.1 %collective-permute-start.15 = (bf16[2,128]{1,0:T(2,128)(2,1)S(1)}, bf16[2,128]{1,0:T(2,128)(2,1)S(1)}, u32[]{:S(2)}, u32[]{:S(2)}) collective-permute-start(bf16[2,128]{1,0:T(2,128)(2,1)S(1)} %pad_maximum_fusion.1), channel_id=1, source_target_pairs={{0,2},{1,3},{2,0},{3,1},{4,6},{5,7},{6,4},{7,5},{8,10},{9,11},{10,... | collective-permute-start | bytes 1544 | tf_op jit(solution)/shard_map/ppermute | solution.py:549
  299.9 3.6 %collective-permute-start.22 = (bf16[960,768]{1,0:T(8,128)(2,1)S(1)}, bf16[960,768]{1,0:T(8,128)(2,1)S(1)}, u32[]{:S(2)}, u32[]{:S(2)}) collective-permute-start(bf16[960,768]{1,0:T(8,128)(2,1)S(1)} %bitcast.47), channel_id=1, source_target_pairs={{0,4},{4,0},{8,12},{12,8},{16,20},{20,16},{24,28},{28,24},{1,5},{5... | collective-permute-start | bytes 4423688 | tf_op jit(solution)/shard_map/ppermute | solution.py:549
  300.0 6.3 %collective-permute-start.19 = (bf16[96,768]{1,0:T(8,128)(2,1)S(1)}, bf16[96,768]{1,0:T(8,128)(2,1)S(1)}, u32[]{:S(2)}, u32[]{:S(2)}) collective-permute-start(bf16[96,768]{1,0:T(8,128)(2,1)S(1)} %fusion.2.refs_0_), channel_id=1, source_target_pairs={{0,16},{4,20},{8,24},{12,28},{16,0},{20,4},{24,8},{28,12},{1,17},{... | collective-permute-start | bytes 442376 | tf_op jit(solution)/shard_map/ppermute | solution.py:549
  300.6 6.7 %collective-permute-start.20 = (bf16[96,768]{1,0:T(8,128)(2,1)S(1)}, bf16[96,768]{1,0:T(8,128)(2,1)S(1)}, u32[]{:S(2)}, u32[]{:S(2)}) collective-permute-start(bf16[96,768]{1,0:T(8,128)(2,1)S(1)} %fusion.2.refs_0_), channel_id=1, source_target_pairs={{0,8},{4,12},{8,0},{12,4},{16,24},{20,28},{24,16},{28,20},{1,9},{5... | collective-permute-start | bytes 442376 | tf_op jit(solution)/shard_map/ppermute | solution.py:549
  302.1 8.5 %collective-permute-start.21 = (bf16[96,768]{1,0:T(8,128)(2,1)S(1)}, bf16[96,768]{1,0:T(8,128)(2,1)S(1)}, u32[]{:S(2)}, u32[]{:S(2)}) collective-permute-start(bf16[96,768]{1,0:T(8,128)(2,1)S(1)} %fusion.2.refs_0_), channel_id=1, source_target_pairs={{0,24},{4,28},{8,16},{12,20},{16,8},{20,12},{24,0},{28,4},{1,25},{... | collective-permute-start | bytes 442376 | tf_op jit(solution)/shard_map/ppermute | solution.py:549
  311.2 2.1 collective-permute-start.23
  (26 other events, 246.5 us)
